TPU v7x, 512 devices: a whole 4x8x8 slice. The times are simulated.
512 devices in a mesh: seq: 128 (over y, z, core), dp: 4 (over x).
Axes of the slice: x: 4, y: 8, z: 8, core: 2. Of those that a mesh axis runs over, the one named last changes fastest.
Arguments:
- layer_inputs: bfloat16 [4, 32768, 4096], P('dp', 'seq')
- doc_start: int32 [4, 32768], P('dp', 'seq'), may hold values from 0 to 32767, as said below
- w_qkv: bfloat16 [4096, 512], P(('seq', 'dp'))
- d_context: bfloat16 [4, 32768, 256], P('dp', 'seq'), may hold values from -6 to 6
Outputs:
- d_x: bfloat16 [4, 32768, 4096], P('dp', 'seq')
- g_qkv: float32 [4096, 512], P(('seq', 'dp'))
Inputs may be any that keep to these rules, and one draw needn't show every extreme that they name: doc_start[g, i] is at most i, never falls along positions, doc_start[g, 0] = 0, and doc_start[g, doc_start[g, i]] = doc_start[g, i].
All inputs are finite; a program needn't handle non-finite values.
Results may differ from a plain program's by a relative error of at most 0.017.
Values may be sent and summed in bfloat16 or wider, within the bound.
No kernel may reach another device: no remote copies, remote signals or barrier semaphores. Data moves between devices by JAX's collectives and lax.ppermute only.
A program may use at most 64 MiB of HBM per device.

v0:
```python
import jax
import jax.numpy as jnp
from jax import lax
from jax.sharding import PartitionSpec as P

WIN = 256


def from_partner(block, axis, stride):
    count = lax.axis_size(axis)
    route = []
    for low in range(count):
        high = low | 1 << stride
        if high != low and high < count:
            route += [(low, high), (high, low)]
    return lax.ppermute(block, axis, route)


def from_behind(block, axis, distance):
    devices = range(lax.axis_size(axis))
    route = [(i - distance, i) for i in devices if i - distance in devices]
    return lax.ppermute(block, axis, route)


def masked_scores(queries, key_rows, doc_first, query_pos, key_pos):
    inv_root = queries.shape[2] ** (-0.5)
    scores = (
        jnp.einsum("rhd,kd->hrk", queries, key_rows, preferred_element_type=jnp.float32) * inv_root
    )
    visible = (
        (key_pos[None, :] <= query_pos[:, None])
        & (key_pos[None, :] > query_pos[:, None] - WIN)
        & (key_pos[None, :] >= doc_first[:, None])
    )
    return jnp.where(visible[None, :, :], scores, -jnp.inf)


def backward_terms(queries, key_rows, value_rows, out_grad, attn_probs, prob_low, row_dot):
    inv_root = queries.shape[2] ** (-0.5)
    prob_grad = jnp.einsum("rhd,kd->hrk", out_grad, value_rows, preferred_element_type=jnp.float32)
    score_grad = (attn_probs * (prob_grad - row_dot[:, :, None])).astype(jnp.bfloat16)
    grad_query = (
        jnp.einsum("hrk,kd->rhd", score_grad, key_rows, preferred_element_type=jnp.float32)
        * inv_root
    )
    grad_keys = (
        jnp.einsum("hrk,rhd->kd", score_grad, queries, preferred_element_type=jnp.float32)
        * inv_root
    )
    grad_values = jnp.einsum("hrk,rhd->kd", prob_low, out_grad, preferred_element_type=jnp.float32)
    return (grad_query, grad_keys, grad_values)


def local_pass(queries, key_rows, value_rows, out_grad, doc_first, query_pos, key_pos):
    scores = masked_scores(queries, key_rows, doc_first, query_pos, key_pos)
    row_max = jnp.max(scores, axis=2)
    log_total = row_max + jnp.log(jnp.sum(jnp.exp(scores - row_max[:, :, None]), axis=2))
    attn_probs = jnp.exp(scores - log_total[:, :, None])
    prob_low = attn_probs.astype(jnp.bfloat16)
    context = jnp.einsum("hrk,kd->rhd", prob_low, value_rows, preferred_element_type=jnp.float32)
    row_dot = jnp.sum(out_grad.astype(jnp.float32) * context, axis=2).T
    grad_query, grad_keys, grad_values = backward_terms(
        queries, key_rows, value_rows, out_grad, attn_probs, prob_low, row_dot
    )
    return (grad_query, grad_keys, grad_values, log_total, row_dot)


def halve_over_seq(buffer, bit_index):
    half_rows = buffer.shape[0] // 2
    my_bit = lax.axis_index("seq") >> bit_index & 1
    kept_half = lax.dynamic_slice_in_dim(buffer, my_bit * half_rows, half_rows, 0)
    sent_half = lax.dynamic_slice_in_dim(buffer, (1 - my_bit) * half_rows, half_rows, 0)
    return kept_half + from_partner(sent_half.astype(jnp.bfloat16), "seq", bit_index).astype(
        sent_half.dtype
    )


def halve_over_dp(buffer, bit_index):
    half_rows = buffer.shape[0] // 2
    my_bit = lax.axis_index("dp") >> bit_index & 1
    kept_half = lax.dynamic_slice_in_dim(buffer, my_bit * half_rows, half_rows, 0)
    sent_half = lax.dynamic_slice_in_dim(buffer, (1 - my_bit) * half_rows, half_rows, 0)
    return kept_half + from_partner(sent_half.astype(jnp.bfloat16), "dp", bit_index).astype(
        sent_half.dtype
    )


def body(layer_inputs, doc_start, w_qkv, d_context):
    x_local = layer_inputs[0]
    tok_rows = x_local.shape[0]
    q_width = d_context.shape[2]
    head_dim = (w_qkv.shape[1] - q_width) // 2
    heads = q_width // head_dim
    out_grad = d_context[0].reshape(tok_rows, heads, head_dim)
    doc_first = doc_start[0]
    positions = lax.axis_index("seq") * tok_rows + jnp.arange(tok_rows, dtype=jnp.int32)
    full_weights = lax.all_gather(w_qkv, ("seq", "dp"), axis=0, tiled=True)
    projected = jnp.dot(x_local, full_weights, preferred_element_type=jnp.float32)
    projected = projected.astype(jnp.bfloat16)
    queries = projected[:, :q_width].reshape(tok_rows, heads, head_dim)
    key_value = projected[:, q_width:]
    prior = from_behind(key_value, "seq", 1)
    key_rows = jnp.concatenate([prior[:, :head_dim], key_value[:, :head_dim]], axis=0)
    value_rows = jnp.concatenate([prior[:, head_dim:], key_value[:, head_dim:]], axis=0)
    key_pos = jnp.concatenate([positions - tok_rows, positions])
    grad_query, grad_keys, grad_values, log_total, row_dot = local_pass(
        queries, key_rows, value_rows, out_grad, doc_first, positions, key_pos
    )
    returned = from_behind(
        jnp.concatenate([grad_keys[:tok_rows], grad_values[:tok_rows]], axis=1).astype(
            jnp.bfloat16
        ),
        "seq",
        -1,
    ).astype(jnp.float32)
    far_keys = returned[:, :head_dim]
    far_values = returned[:, head_dim:]
    key_grad = (grad_keys[tok_rows:] + far_keys).astype(jnp.bfloat16)
    value_grad = (grad_values[tok_rows:] + far_values).astype(jnp.bfloat16)
    grad_proj = jnp.concatenate(
        [grad_query.astype(jnp.bfloat16).reshape(tok_rows, q_width), key_grad, value_grad], axis=1
    )
    input_grad = lax.dot_general(
        grad_proj, full_weights, (((1,), (1,)), ((), ())), preferred_element_type=jnp.float32
    )
    input_grad = input_grad.astype(jnp.bfloat16).reshape(1, tok_rows, x_local.shape[1])
    partial_grad = lax.dot_general(
        x_local, grad_proj, (((0,), (0,)), ((), ())), preferred_element_type=jnp.float32
    )
    seq_count = lax.axis_size("seq")
    dp_count = lax.axis_size("dp")
    seq_levels = seq_count.bit_length() - 1
    dp_levels = dp_count.bit_length() - 1
    buffer = partial_grad
    for bit_index in range(seq_levels - 1, -1, -1):
        buffer = halve_over_seq(buffer, bit_index)
    for bit_index in range(dp_levels - 1, -1, -1):
        buffer = halve_over_dp(buffer, bit_index)
    return (input_grad, buffer)


def solution(mesh):
    return jax.shard_map(
        body,
        mesh=mesh,
        in_specs=(
            P("dp", "seq", None),
            P("dp", "seq"),
            P(("seq", "dp"), None),
            P("dp", "seq", None),
        ),
        out_specs=(P("dp", "seq", None), P(("seq", "dp"), None)),
        check_vma=False,
    )
```

profile of v0, /device:TPU:1, one launch (start us, length us, event | category | flops | bytes accessed | tf_op | source)
XLA Modules:
  0.0 401.5 jit_solution(3054772189091527799)
XLA Ops:
  9.9 126.9 %all-gather.2.cloned.1.call-done = bf16[4096,512]{1,0:T(8,128)(2,1)} async-done(((bf16[8,512]{1,0:T(8,128)(2,1)}), bf16[4096,512]{1,0:T(8,128)(2,1)}) %all-gather.2.cloned.1.call-update) | async-done | bytes 4194320 | tf_op jit(solution)/shard_map/all_gather | solution.py:97
  136.8 3.4 fusion.11
  140.4 2.6 collective-permute-start
  143.0 1.9 collective-permute-done
  146.7 1.9 collective-permute-start.1
  148.9 4.8 %collective-permute-done.1 = bf16[256,256]{0,1:T(8,128)(2,1)S(1)} collective-permute-done((bf16[256,256]{0,1:T(8,128)(2,1)S(1)}, bf16[256,256]{0,1:T(8,128)(2,1)S(1)}, u32[]{:S(2)}, u32[]{:S(2)}) %collective-permute-start.1) | collective-permute-done | bytes 131104 | tf_op jit(solution)/shard_map/ppermute | solution.py:22
  153.8 1.3 fusion.2
  155.1 3.2 copy-done.1
  158.3 1.6 fusion.1
  159.9 5.6 %collective-permute-start.2 = (bf16[2048,512]{0,1:T(8,128)(2,1)}, bf16[2048,512]{0,1:T(8,128)(2,1)}, u32[]{:S(2)}, u32[]{:S(2)}) collective-permute-start(bf16[2048,512]{0,1:T(8,128)(2,1)} %fusion.1), channel_id=1, source_target_pairs={{0,256},{256,0},{4,260},{260,4},{8,264},{264,8},{12,268},{268,12},... | collective-permute-start | bytes 6291464 | tf_op jit(solution)/shard_map/ppermute | solution.py:16
  165.5 93.5 %collective-permute-done.2 = bf16[2048,512]{0,1:T(8,128)(2,1)} collective-permute-done((bf16[2048,512]{0,1:T(8,128)(2,1)}, bf16[2048,512]{0,1:T(8,128)(2,1)}, u32[]{:S(2)}, u32[]{:S(2)}) %collective-permute-start.2) | collective-permute-done | bytes 2097184 | tf_op jit(solution)/shard_map/ppermute | solution.py:16
  259.0 3.4 bitcast_add_fusion
  262.4 2.0 copy-done.2
  264.6 1.9 collective-permute-start.3
  266.5 47.4 %collective-permute-done.3 = bf16[1024,512]{0,1:T(8,128)(2,1)} collective-permute-done((bf16[1024,512]{0,1:T(8,128)(2,1)S(1)}, bf16[1024,512]{0,1:T(8,128)(2,1)}, u32[]{:S(2)}, u32[]{:S(2)}) %collective-permute-start.3) | collective-permute-done | bytes 1048608 | tf_op jit(solution)/shard_map/ppermute | solution.py:16
  313.9 2.2 convert_add_fusion
  316.2 1.3 copy-done.3
  317.6 1.9 collective-permute-start.4
  319.5 13.1 %collective-permute-done.4 = bf16[512,512]{0,1:T(8,128)(2,1)} collective-permute-done((bf16[512,512]{0,1:T(8,128)(2,1)S(1)}, bf16[512,512]{0,1:T(8,128)(2,1)}, u32[]{:S(2)}, u32[]{:S(2)}) %collective-permute-start.4) | collective-permute-done | bytes 524320 | tf_op jit(solution)/shard_map/ppermute | solution.py:16
  332.6 1.5 convert_add_fusion.1
  334.9 3.3 collective-permute-start.5
  338.1 10.9 %collective-permute-done.5 = bf16[256,512]{0,1:T(8,128)(2,1)} collective-permute-done((bf16[256,512]{0,1:T(8,128)(2,1)}, bf16[256,512]{0,1:T(8,128)(2,1)}, u32[]{:S(2)}, u32[]{:S(2)}) %collective-permute-start.5) | collective-permute-done | bytes 262176 | tf_op jit(solution)/shard_map/ppermute | solution.py:16
  349.0 1.0 convert_add_fusion.2
  350.8 8.4 %collective-permute-start.6 = (bf16[128,512]{0,1:T(8,128)(2,1)S(1)}, bf16[128,512]{0,1:T(8,128)(2,1)S(1)}, u32[]{:S(2)}, u32[]{:S(2)}) collective-permute-start(bf16[128,512]{0,1:T(8,128)(2,1)S(1)} %dynamic-slice_convert_fusion.8), channel_id=1, source_target_pairs={{0,16},{16,0},{4,20},{20,4},{8,24},{24,8},{12,28},{28,12},{32,48},... | collective-permute-start | bytes 393224 | tf_op jit(solution)/shard_map/ppermute | solution.py:16
  359.3 2.3 collective-permute-done.6
  362.7 4.0 collective-permute-start.7
  366.7 2.3 collective-permute-done.7
  369.3 7.5 %collective-permute-start.8 = (bf16[32,512]{0,1:T(8,128)(2,1)S(1)}, bf16[32,512]{0,1:T(8,128)(2,1)S(1)}, u32[]{:S(2)}, u32[]{:S(2)}) collective-permute-start(bf16[32,512]{0,1:T(8,128)(2,1)S(1)} %dynamic-slice_convert_fusion.6), channel_id=1, source_target_pairs={{0,4},{4,0},{8,12},{12,8},{16,20},{20,16},{24,28},{28,24},{32,36},... | collective-permute-start | bytes 98312 | tf_op jit(solution)/shard_map/ppermute | solution.py:16
  378.1 4.8 %collective-permute-start.9 = (bf16[16,512]{0,1:T(8,128)(2,1)S(1)}, bf16[16,512]{0,1:T(8,128)(2,1)S(1)}, u32[]{:S(2)}, u32[]{:S(2)}) collective-permute-start(bf16[16,512]{0,1:T(8,128)(2,1)S(1)} %dynamic-slice_convert_fusion.5), channel_id=1, source_target_pairs={{0,2},{2,0},{1,3},{3,1},{4,6},{6,4},{5,7},{7,5},{8,10},{10,8},{9,1... | collective-permute-start | bytes 49160 | tf_op jit(solution)/shard_map/ppermute | solution.py:16
  382.9 3.3 collective-permute-done.9
  386.4 2.5 collective-permute-start.10
  389.0 4.8 %fusion = bf16[1,256,4096]{2,1,0:T(8,128)(2,1)} fusion(bf16[4096,512]{1,0:T(8,128)(2,1)} %all-gather.2.cloned.1.call-done, bf16[256,128]{0,1:T(8,128)(2,1)S(1)} %get-tuple-element.5, bf16[256,128]{0,1:T(8,128)(2,1)S(1)} %get-tuple-element.4, bf16[256,256]{0,1:T(8,128)(2,1)S(1)} %bitcast.68), kind=kOutput, calls=%fused_computation.1 | convolution fusion | flops 1075576832 | bytes 6553600 | tf_op jit(solution)/shard_map/dot_general | solution.py:123
  (46 shorter events, 10.2 us)
Async XLA Ops:
  7.2 129.6 %copy-start = (bf16[1,256,4096]{2,1,0:T(8,128)(2,1)S(1)}, bf16[1,256,4096]{2,1,0:T(8,128)(2,1)}, u32[]{:S(2)}) copy-start(bf16[1,256,4096]{2,1,0:T(8,128)(2,1)} %param.4) | copy-start | bytes 6291460
  7.2 129.6 %all-gather.2.cloned.1.call-start = ((), (), s32[]{:S(2)}) async-start(), calls=%async_computation | async-start | bytes 4202496 | tf_op jit(solution)/shard_map/all_gather | solution.py:97
  140.4 4.6 %collective-permute-start = (bf16[256,256]{1,0:T(8,128)(2,1)S(1)}, bf16[256,256]{1,0:T(8,128)(2,1)S(1)}, u32[]{:S(2)}, u32[]{:S(2)}) collective-permute-start(bf16[256,256]{1,0:T(8,128)(2,1)S(1)} %get-tuple-element.8), channel_id=1, source_target_pairs={{0,4},{4,8},{8,12},{12,16},{16,20},{20,24},{24,28},{28,32},{32,36}... | collective-permute-start | bytes 393224 | tf_op jit(solution)/shard_map/ppermute | solution.py:22
  146.7 7.0 %collective-permute-start.1 = (bf16[256,256]{0,1:T(8,128)(2,1)S(1)}, bf16[256,256]{0,1:T(8,128)(2,1)S(1)}, u32[]{:S(2)}, u32[]{:S(2)}) collective-permute-start(bf16[256,256]{0,1:T(8,128)(2,1)S(1)} %pad_maximum_fusion.1), channel_id=1, source_target_pairs={{4,0},{8,4},{12,8},{16,12},{20,16},{24,20},{28,24},{32,28},{36,32}... | collective-permute-start | bytes 393224 | tf_op jit(solution)/shard_map/ppermute | solution.py:22
  155.1 3.2 copy-start.1
  159.9 99.1 %collective-permute-start.2 = (bf16[2048,512]{0,1:T(8,128)(2,1)}, bf16[2048,512]{0,1:T(8,128)(2,1)}, u32[]{:S(2)}, u32[]{:S(2)}) collective-permute-start(bf16[2048,512]{0,1:T(8,128)(2,1)} %fusion.1), channel_id=1, source_target_pairs={{0,256},{256,0},{4,260},{260,4},{8,264},{264,8},{12,268},{268,12},... | collective-permute-start | bytes 6291464 | tf_op jit(solution)/shard_map/ppermute | solution.py:16
  262.4 2.0 copy-start.2
  264.6 49.4 %collective-permute-start.3 = (bf16[1024,512]{0,1:T(8,128)(2,1)S(1)}, bf16[1024,512]{0,1:T(8,128)(2,1)}, u32[]{:S(2)}, u32[]{:S(2)}) collective-permute-start(bf16[1024,512]{0,1:T(8,128)(2,1)S(1)} %dynamic-slice_convert_fusion.1), channel_id=1, source_target_pairs={{0,128},{128,0},{4,132},{132,4},{8,136},{136,8},{12,140},{140,12},... | collective-permute-start | bytes 3145736 | tf_op jit(solution)/shard_map/ppermute | solution.py:16
  316.2 1.3 copy-start.3
  317.6 15.0 %collective-permute-start.4 = (bf16[512,512]{0,1:T(8,128)(2,1)S(1)}, bf16[512,512]{0,1:T(8,128)(2,1)}, u32[]{:S(2)}, u32[]{:S(2)}) collective-permute-start(bf16[512,512]{0,1:T(8,128)(2,1)S(1)} %dynamic-slice_convert_fusion.2), channel_id=1, source_target_pairs={{0,64},{64,0},{4,68},{68,4},{8,72},{72,8},{12,76},{76,12},{16,80},... | collective-permute-start | bytes 1572872 | tf_op jit(solution)/shard_map/ppermute | solution.py:16
  334.9 14.1 %collective-permute-start.5 = (bf16[256,512]{0,1:T(8,128)(2,1)}, bf16[256,512]{0,1:T(8,128)(2,1)}, u32[]{:S(2)}, u32[]{:S(2)}) collective-permute-start(bf16[256,512]{0,1:T(8,128)(2,1)} %dynamic-slice_convert_fusion.3), channel_id=1, source_target_pairs={{0,32},{32,0},{4,36},{36,4},{8,40},{40,8},{12,44},{44,12},{16,48},... | collective-permute-start | bytes 786440 | tf_op jit(solution)/shard_map/ppermute | solution.py:16
  350.0 0.8 copy-start.4
  350.8 10.8 %collective-permute-start.6 = (bf16[128,512]{0,1:T(8,128)(2,1)S(1)}, bf16[128,512]{0,1:T(8,128)(2,1)S(1)}, u32[]{:S(2)}, u32[]{:S(2)}) collective-permute-start(bf16[128,512]{0,1:T(8,128)(2,1)S(1)} %dynamic-slice_convert_fusion.8), channel_id=1, source_target_pairs={{0,16},{16,0},{4,20},{20,4},{8,24},{24,8},{12,28},{28,12},{32,48},... | collective-permute-start | bytes 393224 | tf_op jit(solution)/shard_map/ppermute | solution.py:16
  362.7 6.3 %collective-permute-start.7 = (bf16[64,512]{0,1:T(8,128)(2,1)S(1)}, bf16[64,512]{0,1:T(8,128)(2,1)S(1)}, u32[]{:S(2)}, u32[]{:S(2)}) collective-permute-start(bf16[64,512]{0,1:T(8,128)(2,1)S(1)} %dynamic-slice_convert_fusion.7), channel_id=1, source_target_pairs={{0,8},{8,0},{4,12},{12,4},{16,24},{24,16},{20,28},{28,20},{32,40},... | collective-permute-start | bytes 196616 | tf_op jit(solution)/shard_map/ppermute | solution.py:16
  369.3 8.5 %collective-permute-start.8 = (bf16[32,512]{0,1:T(8,128)(2,1)S(1)}, bf16[32,512]{0,1:T(8,128)(2,1)S(1)}, u32[]{:S(2)}, u32[]{:S(2)}) collective-permute-start(bf16[32,512]{0,1:T(8,128)(2,1)S(1)} %dynamic-slice_convert_fusion.6), channel_id=1, source_target_pairs={{0,4},{4,0},{8,12},{12,8},{16,20},{20,16},{24,28},{28,24},{32,36},... | collective-permute-start | bytes 98312 | tf_op jit(solution)/shard_map/ppermute | solution.py:16
  378.1 8.1 %collective-permute-start.9 = (bf16[16,512]{0,1:T(8,128)(2,1)S(1)}, bf16[16,512]{0,1:T(8,128)(2,1)S(1)}, u32[]{:S(2)}, u32[]{:S(2)}) collective-permute-start(bf16[16,512]{0,1:T(8,128)(2,1)S(1)} %dynamic-slice_convert_fusion.5), channel_id=1, source_target_pairs={{0,2},{2,0},{1,3},{3,1},{4,6},{6,4},{5,7},{7,5},{8,10},{10,8},{9,1... | collective-permute-start | bytes 49160 | tf_op jit(solution)/shard_map/ppermute | solution.py:16
  386.4 7.4 %collective-permute-start.10 = (bf16[8,512]{0,1:T(8,128)(2,1)S(1)}, bf16[8,512]{0,1:T(8,128)(2,1)S(1)}, u32[]{:S(2)}, u32[]{:S(2)}) collective-permute-start(bf16[8,512]{0,1:T(8,128)(2,1)S(1)} %dynamic-slice_convert_fusion.4), channel_id=1, source_target_pairs={{0,1},{1,0},{2,3},{3,2},{4,5},{5,4},{6,7},{7,6},{8,9},{9,8},{10,11... | collective-permute-start | bytes 24584 | tf_op jit(solution)/shard_map/ppermute | solution.py:16
Sparse Core Ops, SparseCore 0:
  12.2 124.5 all-gather.1
where the time goes:
time: 402 us; the launch traced here: 401 us
  waiting for transfers between devices  308 us (77%)
  starting transfers between devices  44.6 us (11%)
  between operations  14.5 us (4%)
  local copies, waits for them, and re-layouts  12.2 us (3%)
  matrix products  11.3 us (3%)
  other arithmetic  10.9 us (3%)
    ppermute x9, waiting for transfers between devices, from_partner(): return lax.ppermute(block, axis, route)  174 us
    all_gather x1, waiting for transfers between devices, body(): full_weights = lax.all_gather(w_qkv, ('seq', 'dp'), axis=0, tiled=True)  127 us
    ppermute x9, starting transfers between devices, from_partner(): return lax.ppermute(block, axis, route)  40 us
    add x7, other arithmetic, halve_over_seq(): kept_half + from_partner(sent_half.astype(jnp.bfloat16), 'seq', bit_index...  9.44 us
    unnamed x12, local copies, waits for them, and re-layouts  9.01 us
  transfers between devices with their start and end apart: 12, of which 11 were waited for; matrix products, arithmetic and copies ran while one was open for 2% of the time, Pallas kernels for 0%

commit v1 on v0

--- a/solution.py
+++ b/solution.py
@@ -4,16 +4,6 @@
 from jax.sharding import PartitionSpec as P
 
 WIN = 256
-
-
-def from_partner(block, axis, stride):
-    count = lax.axis_size(axis)
-    route = []
-    for low in range(count):
-        high = low | 1 << stride
-        if high != low and high < count:
-            route += [(low, high), (high, low)]
-    return lax.ppermute(block, axis, route)
 
 
 def from_behind(block, axis, distance):
@@ -65,24 +55,76 @@
     return (grad_query, grad_keys, grad_values, log_total, row_dot)
 
 
-def halve_over_seq(buffer, bit_index):
-    half_rows = buffer.shape[0] // 2
-    my_bit = lax.axis_index("seq") >> bit_index & 1
-    kept_half = lax.dynamic_slice_in_dim(buffer, my_bit * half_rows, half_rows, 0)
-    sent_half = lax.dynamic_slice_in_dim(buffer, (1 - my_bit) * half_rows, half_rows, 0)
-    return kept_half + from_partner(sent_half.astype(jnp.bfloat16), "seq", bit_index).astype(
-        sent_half.dtype
-    )
+AXES = ("seq", "dp")
 
 
-def halve_over_dp(buffer, bit_index):
-    half_rows = buffer.shape[0] // 2
-    my_bit = lax.axis_index("dp") >> bit_index & 1
-    kept_half = lax.dynamic_slice_in_dim(buffer, my_bit * half_rows, half_rows, 0)
-    sent_half = lax.dynamic_slice_in_dim(buffer, (1 - my_bit) * half_rows, half_rows, 0)
-    return kept_half + from_partner(sent_half.astype(jnp.bfloat16), "dp", bit_index).astype(
-        sent_half.dtype
-    )
+def spot(y, z, core, x):
+    return ((y % 8 * 8 + z % 8) * 2 + core) * 4 + x % 4
+
+
+def far_groups():
+    return [
+        [spot(2 * y + a, 2 * z + b, core, 2 * x + d) for y in range(4) for z in range(4) for x in range(2)]
+        for a in range(2)
+        for b in range(2)
+        for core in range(2)
+        for d in range(2)
+    ]
+
+
+def near_groups():
+    groups = []
+    for core in range(2):
+        for y in range(4):
+            for z in range(4):
+                for x in range(2):
+                    low = [(k, k) if core == 0 else (k, 2 - k) for k in range(2)]
+                    groups.append(
+                        [
+                            spot(2 * y + a[1], 2 * z + b[1], core, 2 * x + d[1])
+                            for a in low
+                            for b in low
+                            for d in low
+                        ]
+                    )
+    return groups
+
+
+def exchange(blocks, groups):
+    return lax.all_to_all(blocks, AXES, 0, 0, axis_index_groups=groups)
+
+
+def swap_cores(block):
+    count = lax.axis_size("seq")
+    return lax.ppermute(block, "seq", [(i, i ^ 1) for i in range(count)])
+
+
+def gather_weights(w_block):
+    rows, width = w_block.shape
+    far = exchange(jnp.broadcast_to(w_block, (32, rows, width)), far_groups())
+    far = far.reshape(32 * rows, width)
+    own = exchange(jnp.broadcast_to(far, (8,) + far.shape), near_groups())
+    other = swap_cores(own)
+    core = lax.axis_index("seq") & 1
+    both = jnp.stack([jnp.where(core == 0, own, other), jnp.where(core == 0, other, own)])
+    both = both.reshape(2, 2, 2, 2, 4, 4, 2, rows, width)
+    return both.transpose(4, 1, 5, 2, 0, 6, 3, 7, 8).reshape(512 * rows, width)
+
+
+def scatter_sum(partial):
+    rows, width = partial.shape[0] // 512, partial.shape[1]
+    core = lax.axis_index("seq") & 1
+    split = partial.reshape(4, 2, 4, 2, 2, 2, 2, rows, width)
+
+    def half(which):
+        part = lax.dynamic_index_in_dim(split, which, 4, keepdims=False)
+        return part.transpose(1, 3, 5, 0, 2, 4, 6, 7).reshape(8, 32 * rows, width)
+
+    received = swap_cores(half(1 - core).astype(jnp.bfloat16))
+    total = (half(core) + received.astype(jnp.float32)).astype(jnp.bfloat16)
+    total = jnp.sum(exchange(total, near_groups()).astype(jnp.float32), axis=0)
+    total = total.astype(jnp.bfloat16).reshape(32, rows, width)
+    return jnp.sum(exchange(total, far_groups()).astype(jnp.float32), axis=0)
 
 
 def body(layer_inputs, doc_start, w_qkv, d_context):
@@ -94,7 +136,7 @@
     out_grad = d_context[0].reshape(tok_rows, heads, head_dim)
     doc_first = doc_start[0]
     positions = lax.axis_index("seq") * tok_rows + jnp.arange(tok_rows, dtype=jnp.int32)
-    full_weights = lax.all_gather(w_qkv, ("seq", "dp"), axis=0, tiled=True)
+    full_weights = gather_weights(w_qkv)
     projected = jnp.dot(x_local, full_weights, preferred_element_type=jnp.float32)
     projected = projected.astype(jnp.bfloat16)
     queries = projected[:, :q_width].reshape(tok_rows, heads, head_dim)
@@ -127,16 +169,7 @@
     partial_grad = lax.dot_general(
         x_local, grad_proj, (((0,), (0,)), ((), ())), preferred_element_type=jnp.float32
     )
-    seq_count = lax.axis_size("seq")
-    dp_count = lax.axis_size("dp")
-    seq_levels = seq_count.bit_length() - 1
-    dp_levels = dp_count.bit_length() - 1
-    buffer = partial_grad
-    for bit_index in range(seq_levels - 1, -1, -1):
-        buffer = halve_over_seq(buffer, bit_index)
-    for bit_index in range(dp_levels - 1, -1, -1):
-        buffer = halve_over_dp(buffer, bit_index)
-    return (input_grad, buffer)
+    return (input_grad, scatter_sum(partial_grad))
 
 
 def solution(mesh):

time: 402 us -> 160 us (0.40)
  waiting for transfers between devices: 308 us -> 21.9 us
  blocking collectives: 0 us -> 80.8 us
  starting transfers between devices: 44.6 us -> 15.7 us
  between operations: 14.5 us -> 0.93 us
  local copies, waits for them, and re-layouts: 12.2 us -> 18.7 us
    ppermute x9 -> x2, waiting for transfers between devices: 174 us -> 5.3 us  [swap_cores(): return lax.ppermute(block, 'seq', [(i, i ^ 1) for i in range(count)])]
    all_gather x1 -> x0, waiting for transfers between devices: 127 us -> none  [body(): full_weights = lax.all_gather(w_qkv, ('seq', 'dp'), axis=0, tiled=True)]
    all_to_all x0 -> x3, blocking collectives: none -> 80.8 us  [exchange(): return lax.all_to_all(blocks, AXES, 0, 0, axis_index_groups=groups)]
    ppermute x9 -> x2, starting transfers between devices: 40 us -> 3.92 us  [swap_cores(): return lax.ppermute(block, 'seq', [(i, i ^ 1) for i in range(count)])]
    all_to_all x0 -> x1, waiting for transfers between devices: none -> 9.89 us  [exchange(): return lax.all_to_all(blocks, AXES, 0, 0, axis_index_groups=groups)]
    add x9 -> x0, other arithmetic: 9.71 us -> none  [the longest x7 9.44 us: halve_over_seq(): kept_half + from_partner(sent_half.astype(jnp.bfloat16), 'seq', bit_index...]
    dot_general x0 -> x1, local copies, waits for them, and re-layouts: none -> 9.03 us  [body(): lax.dot_general(x_local, grad_proj, (((0,), (0,)), ((), ())), preferred_e...]
    unnamed x12 -> x9, local copies, waits for them, and re-layouts: 9.01 us -> 0.74 us
  transfers between devices with their start and end apart: 12 -> 5, of which waited for: 11 -> 5; matrix products, arithmetic and copies ran while one was open for 2% -> 5% of each run, Pallas kernels for 0% -> 0%
where the time goes in v1:
time: 160 us
  blocking collectives  80.8 us (50%)
  waiting for transfers between devices  21.9 us (14%)
  local copies, waits for them, and re-layouts  18.7 us (12%)
  starting transfers between devices  15.7 us (10%)
  matrix products  12.5 us (8%)
  other arithmetic  9.16 us (6%)
    all_to_all x3, blocking collectives, exchange(): return lax.all_to_all(blocks, AXES, 0, 0, axis_index_groups=groups)  80.8 us
    all_to_all x1, waiting for transfers between devices, exchange(): return lax.all_to_all(blocks, AXES, 0, 0, axis_index_groups=groups)  9.89 us
    dot_general x1, local copies, waits for them, and re-layouts, body(): lax.dot_general(x_local, grad_proj, (((0,), (0,)), ((), ())), preferred_e...  9.03 us
    all_to_all x1, starting transfers between devices, exchange(): return lax.all_to_all(blocks, AXES, 0, 0, axis_index_groups=groups)  7.64 us
    ppermute x2, waiting for transfers between devices, from_behind(): return lax.ppermute(block, axis, route)  6.74 us
    ppermute x2, waiting for transfers between devices, swap_cores(): return lax.ppermute(block, 'seq', [(i, i ^ 1) for i in range(count)])  5.3 us
    dot_general x1, matrix products, body(): lax.dot_general(grad_proj, full_weights, (((1,), (1,)), ((), ())), prefer...  4.82 us
    dot_general x1, matrix products, body(): lax.dot_general(x_local, grad_proj, (((0,), (0,)), ((), ())), preferred_e...  4.49 us
  transfers between devices with their start and end apart: 5, of which 5 were waited for; matrix products, arithmetic and copies ran while one was open for 5% of the time, Pallas kernels for 0%

profile of v1, /device:TPU:1, one launch (start us, length us, event | category | flops | bytes accessed | tf_op | source)
XLA Modules:
  0.0 159.7 jit_solution(1600068396499982458)
XLA Ops:
  0.6 0.9 broadcast_in_dim.16
  1.5 33.6 %all_to_all.20 = bf16[32,8,512]{2,1,0:T(8,128)(2,1)S(1)} all-to-all(bf16[32,8,512]{2,1,0:T(8,128)(2,1)S(1)} %broadcast_in_dim.16), channel_id=1, replica_groups={{0,2,16,18,32,34,48,50,128,130,144,146,160,162,176,178,256,258,272,274,..., dimensions={0} | all-to-all | bytes 524288 | tf_op jit(solution)/shard_map/all_to_all | solution.py:94
  35.3 22.2 %all_to_all.21 = bf16[8,256,512]{2,1,0:T(8,128)(2,1)} all-to-all(bf16[8,256,512]{2,1,0:T(8,128)(2,1)S(1)} %broadcast_in_dim.17), channel_id=1, replica_groups={{0,1,8,9,64,65,72,73},{2,3,10,11,66,67,74,75},{16,17,24,25,80,81,88,89}..., dimensions={0} | all-to-all | bytes 4194304 | tf_op jit(solution)/shard_map/all_to_all | solution.py:94
  57.5 2.0 %collective-permute-start = (bf16[8,256,512]{2,1,0:T(8,128)(2,1)}, bf16[8,256,512]{2,1,0:T(8,128)(2,1)}, u32[]{:S(2)}, u32[]{:S(2)}) collective-permute-start(bf16[8,256,512]{2,1,0:T(8,128)(2,1)} %all_to_all.21), channel_id=1, source_target_pairs={{0,4},{4,0},{8,12},{12,8},{16,20},{20,16},{24,28},{28,24},{32,36},... | collective-permute-start | bytes 6291464 | tf_op jit(solution)/shard_map/ppermute | solution.py:99
  59.9 4.0 %collective-permute-done = bf16[8,256,512]{2,1,0:T(8,128)(2,1)} collective-permute-done((bf16[8,256,512]{2,1,0:T(8,128)(2,1)}, bf16[8,256,512]{2,1,0:T(8,128)(2,1)}, u32[]{:S(2)}, u32[]{:S(2)}) %collective-permute-start) | collective-permute-done | bytes 2097184 | tf_op jit(solution)/shard_map/ppermute | solution.py:99
  63.9 2.5 %broadcast_select_fusion.1 = (bf16[8,256,512]{2,1,0:T(8,128)(2,1)S(1)}, bf16[8,256,512]{2,1,0:T(8,128)(2,1)S(1)}) fusion(bf16[8,256,512]{2,1,0:T(8,128)(2,1)} %all_to_all.21, bf16[8,256,512]{2,1,0:T(8,128)(2,1)} %collective-permute-done, pred[]{:T(512)S(6)} %eq.4), kind=kLoop, calls=%fused_computation.12 | loop fusion | flops 2097152 | bytes 8388609 | tf_op jit(solution)/shard_map/jit(_where)/select_n | solution.py:109
  66.4 0.4 maximum_bitcast_fusion
  66.8 0.5 copy.39
  67.4 1.3 fusion.15
  68.7 0.6 copy-done.1
  69.3 2.2 %collective-permute-start.1 = (bf16[256,256]{0,1:T(8,128)(2,1)S(1)}, bf16[256,256]{0,1:T(8,128)(2,1)S(1)}, u32[]{:S(2)}, u32[]{:S(2)}) collective-permute-start(bf16[256,256]{0,1:T(8,128)(2,1)S(1)} %get-tuple-element.8), channel_id=1, source_target_pairs={{0,4},{4,8},{8,12},{12,16},{16,20},{20,24},{24,28},{28,32},{32,36}... | collective-permute-start | bytes 393224 | tf_op jit(solution)/shard_map/ppermute | solution.py:12
  71.5 1.9 %collective-permute-done.1 = bf16[256,256]{0,1:T(8,128)(2,1)S(1)} collective-permute-done((bf16[256,256]{0,1:T(8,128)(2,1)S(1)}, bf16[256,256]{0,1:T(8,128)(2,1)S(1)}, u32[]{:S(2)}, u32[]{:S(2)}) %collective-permute-start.1) | collective-permute-done | bytes 131104 | tf_op jit(solution)/shard_map/ppermute | solution.py:12
  73.4 0.3 fusion.34
  74.3 0.3 fusion.19
  74.7 0.3 fusion.9
  75.3 1.9 %collective-permute-start.2 = (bf16[256,256]{0,1:T(8,128)(2,1)S(1)}, bf16[256,256]{0,1:T(8,128)(2,1)S(1)}, u32[]{:S(2)}, u32[]{:S(2)}) collective-permute-start(bf16[256,256]{0,1:T(8,128)(2,1)S(1)} %pad_maximum_fusion.1), channel_id=1, source_target_pairs={{4,0},{8,4},{12,8},{16,12},{20,16},{24,20},{28,24},{32,28},{36,32}... | collective-permute-start | bytes 393224 | tf_op jit(solution)/shard_map/ppermute | solution.py:12
  77.5 4.8 %collective-permute-done.2 = bf16[256,256]{0,1:T(8,128)(2,1)S(1)} collective-permute-done((bf16[256,256]{0,1:T(8,128)(2,1)S(1)}, bf16[256,256]{0,1:T(8,128)(2,1)S(1)}, u32[]{:S(2)}, u32[]{:S(2)}) %collective-permute-start.2) | collective-permute-done | bytes 131104 | tf_op jit(solution)/shard_map/ppermute | solution.py:12
  82.4 4.5 %convolution_bitcast_fusion = f32[4096,512]{0,1:T(8,128)} fusion(bf16[1,256,4096]{2,1,0:T(8,128)(2,1)S(1)} %copy-done, bf16[256,128]{0,1:T(8,128)(2,1)S(1)} %get-tuple-element.5, bf16[256,128]{0,1:T(8,128)(2,1)S(1)} %get-tuple-element.4, bf16[256,256]{0,1:T(8,128)(2,1)S(1)} %bitcast.94), kind=kOutput, calls=%fused_computation | convolution fusion | flops 1074528256 | bytes 10747904 | tf_op jit(solution)/shard_map/dot_general | solution.py:169
  86.9 9.0 %copy.49 = f32[4096,512]{1,0:T(8,128)} copy(f32[4096,512]{0,1:T(8,128)} %convolution_bitcast_fusion) | data formatting | bytes 16777216 | tf_op jit(solution)/shard_map/dot_general | solution.py:169
  95.9 2.5 %fusion.1 = bf16[2,2,2,4,4,2,8,512]{7,6,2,5,1,4,0,3:T(8,128)(2,1)S(1)} fusion(f32[4,2,4,2,2,2,2,8,512]{8,7,6,5,4,3,2,1,0:T(8,128)} %bitcast.84, s32[]{:T(128)S(6)} %select_n.28), kind=kLoop, calls=%fused_computation.7 | loop fusion | bytes 4194308 | tf_op jit(solution)/shard_map/convert_element_type | solution.py:123
  98.5 1.6 %copy.51 = bf16[2,2,2,4,4,2,8,512]{7,6,5,4,3,2,1,0:T(8,128)(2,1)} copy(bf16[2,2,2,4,4,2,8,512]{7,6,2,5,1,4,0,3:T(8,128)(2,1)S(1)} %fusion.1) | data formatting | bytes 4194304 | tf_op jit(solution)/shard_map/convert_element_type | solution.py:123
  100.1 1.9 %collective-permute-start.3 = (bf16[8,256,512]{2,1,0:T(8,128)(2,1)}, bf16[8,256,512]{2,1,0:T(8,128)(2,1)}, u32[]{:S(2)}, u32[]{:S(2)}) collective-permute-start(bf16[8,256,512]{2,1,0:T(8,128)(2,1)} %bitcast.30), channel_id=1, source_target_pairs={{0,4},{4,0},{8,12},{12,8},{16,20},{20,16},{24,28},{28,24},{32,36},... | collective-permute-start | bytes 6291464 | tf_op jit(solution)/shard_map/ppermute | solution.py:99
  102.0 2.7 %dynamic-slice_bitcast_fusion = f32[2,2,2,4,4,2,8,512]{7,6,2,5,1,4,0,3:T(8,128)S(1)} fusion(f32[4,2,4,2,2,2,2,8,512]{8,7,6,5,4,3,2,1,0:T(8,128)} %bitcast.85, s32[]{:T(128)S(6)} %select_n.27), kind=kLoop, calls=%fused_computation.6 | loop fusion | bytes 8388612 | tf_op jit(solution)/shard_map/transpose | solution.py:121
  104.7 0.5 copy.50
  105.2 1.3 collective-permute-done.3
  106.5 2.5 %add_convert_fusion = bf16[8,256,512]{2,1,0:T(8,128)(2,1)S(1)} fusion(f32[8,256,512]{2,1,0:T(8,128)S(1)} %bitcast.88, bf16[8,256,512]{2,1,0:T(8,128)(2,1)} %collective-permute-done.3), kind=kLoop, calls=%fused_computation.4 | loop fusion | flops 3145728 | bytes 8388608 | tf_op jit(solution)/shard_map/convert_element_type | solution.py:124
  109.0 25.0 %all_to_all.22 = bf16[8,256,512]{2,1,0:T(8,128)(2,1)} all-to-all(bf16[8,256,512]{2,1,0:T(8,128)(2,1)S(1)} %add_convert_fusion), channel_id=1, replica_groups={{0,1,8,9,64,65,72,73},{2,3,10,11,66,67,74,75},{16,17,24,25,80,81,88,89}..., dimensions={0} | all-to-all | bytes 4194304 | tf_op jit(solution)/shard_map/all_to_all | solution.py:94
  134.0 2.7 %reduce_sum.41 = bf16[256,512]{1,0:T(8,128)(2,1)} reduce(bf16[8,256,512]{2,1,0:T(8,128)(2,1)} %all_to_all.22, bf16[]{:T(256)} %constant.35.clone.1), dimensions={0}, to_apply=%region_3.4 | reduce | flops 917504 | bytes 2359298 | tf_op jit(solution)/shard_map/reduce_sum | solution.py:125
  136.7 7.6 %all-to-all-start.3 = ((bf16[32,8,512]{2,1,0:T(8,128)(2,1)}), bf16[32,8,512]{2,1,0:T(8,128)(2,1)S(1)}, u32[]{:S(2)}, u32[]{:S(2)}) async-start(bf16[32,8,512]{2,1,0:T(8,128)(2,1)} %bitcast.31), calls=%async_computation.3 | async-start | bytes 524288 | tf_op jit(solution)/shard_map/all_to_all | solution.py:94
  144.3 4.8 %fusion = bf16[1,256,4096]{2,1,0:T(8,128)(2,1)} fusion(bf16[4096,512]{1,0:T(8,128)(2,1)} %bitcast.87, bf16[256,128]{0,1:T(8,128)(2,1)S(1)} %get-tuple-element.5, bf16[256,128]{0,1:T(8,128)(2,1)S(1)} %get-tuple-element.4, bf16[256,256]{0,1:T(8,128)(2,1)S(1)} %bitcast.95), kind=kOutput, calls=%fused_computation.2 | convolution fusion | flops 1075576832 | bytes 6553600 | tf_op jit(solution)/shard_map/dot_general | solution.py:165
  149.2 9.9 %all-to-all-done.3 = bf16[32,8,512]{2,1,0:T(8,128)(2,1)S(1)} async-done(((bf16[32,8,512]{2,1,0:T(8,128)(2,1)}), bf16[32,8,512]{2,1,0:T(8,128)(2,1)S(1)}, u32[]{:S(2)}, u32[]{:S(2)}) %all-to-all-start.3) | async-done | bytes 262176 | tf_op jit(solution)/shard_map/all_to_all | solution.py:94
  159.1 0.7 convert_reduce_fusion
  (25 shorter events, 1.7 us)
Async XLA Ops:
  0.6 66.7 %copy-start = (bf16[1,256,4096]{2,1,0:T(8,128)(2,1)S(1)}, bf16[1,256,4096]{2,1,0:T(8,128)(2,1)}, u32[]{:S(2)}) copy-start(bf16[1,256,4096]{2,1,0:T(8,128)(2,1)} %param.4) | copy-start | bytes 6291460
  35.3 24.3 %copy-start.2 = (bf16[1,256,256]{2,1,0:T(8,128)(2,1)S(1)}, bf16[1,256,256]{2,1,0:T(8,128)(2,1)}, u32[]{:S(2)}) copy-start(bf16[1,256,256]{2,1,0:T(8,128)(2,1)} %param.7) | copy-start | bytes 393220
  35.3 24.4 %copy-start.3 = (s32[1,256]{1,0:T(1,128)S(1)}, s32[1,256]{1,0:T(1,128)}, u32[]{:S(2)}) copy-start(s32[1,256]{1,0:T(1,128)} %param.5) | copy-start | bytes 3076
  57.5 6.4 %collective-permute-start = (bf16[8,256,512]{2,1,0:T(8,128)(2,1)}, bf16[8,256,512]{2,1,0:T(8,128)(2,1)}, u32[]{:S(2)}, u32[]{:S(2)}) collective-permute-start(bf16[8,256,512]{2,1,0:T(8,128)(2,1)} %all_to_all.21), channel_id=1, source_target_pairs={{0,4},{4,0},{8,12},{12,8},{16,20},{20,16},{24,28},{28,24},{32,36},... | collective-permute-start | bytes 6291464 | tf_op jit(solution)/shard_map/ppermute | solution.py:99
  67.4 1.9 %copy-start.1 = (bf16[4,2,4,2,2,2,2,8,512]{8,7,6,5,4,3,2,1,0:T(8,128)(2,1)}, bf16[4,2,4,2,2,2,2,8,512]{8,7,6,5,4,3,2,1,0:T(8,128)(2,1)S(1)}, u32[]{:S(2)}) copy-start(bf16[4,2,4,2,2,2,2,8,512]{8,7,6,5,4,3,2,1,0:T(8,128)(2,1)S(1)} %copy.39) | copy-start | bytes 12582916
  69.3 4.1 %collective-permute-start.1 = (bf16[256,256]{0,1:T(8,128)(2,1)S(1)}, bf16[256,256]{0,1:T(8,128)(2,1)S(1)}, u32[]{:S(2)}, u32[]{:S(2)}) collective-permute-start(bf16[256,256]{0,1:T(8,128)(2,1)S(1)} %get-tuple-element.8), channel_id=1, source_target_pairs={{0,4},{4,8},{8,12},{12,16},{16,20},{20,24},{24,28},{28,32},{32,36}... | collective-permute-start | bytes 393224 | tf_op jit(solution)/shard_map/ppermute | solution.py:12
  75.3 7.0 %collective-permute-start.2 = (bf16[256,256]{0,1:T(8,128)(2,1)S(1)}, bf16[256,256]{0,1:T(8,128)(2,1)S(1)}, u32[]{:S(2)}, u32[]{:S(2)}) collective-permute-start(bf16[256,256]{0,1:T(8,128)(2,1)S(1)} %pad_maximum_fusion.1), channel_id=1, source_target_pairs={{4,0},{8,4},{12,8},{16,12},{20,16},{24,20},{28,24},{32,28},{36,32}... | collective-permute-start | bytes 393224 | tf_op jit(solution)/shard_map/ppermute | solution.py:12
  100.1 6.4 %collective-permute-start.3 = (bf16[8,256,512]{2,1,0:T(8,128)(2,1)}, bf16[8,256,512]{2,1,0:T(8,128)(2,1)}, u32[]{:S(2)}, u32[]{:S(2)}) collective-permute-start(bf16[8,256,512]{2,1,0:T(8,128)(2,1)} %bitcast.30), channel_id=1, source_target_pairs={{0,4},{4,0},{8,12},{12,8},{16,20},{20,16},{24,28},{28,24},{32,36},... | collective-permute-start | bytes 6291464 | tf_op jit(solution)/shard_map/ppermute | solution.py:99
  136.7 22.4 %all-to-all-start.3 = ((bf16[32,8,512]{2,1,0:T(8,128)(2,1)}), bf16[32,8,512]{2,1,0:T(8,128)(2,1)S(1)}, u32[]{:S(2)}, u32[]{:S(2)}) async-start(bf16[32,8,512]{2,1,0:T(8,128)(2,1)} %bitcast.31), calls=%async_computation.3 | async-start | bytes 524288 | tf_op jit(solution)/shard_map/all_to_all | solution.py:94

commit v2 on v1

--- a/solution.py
+++ b/solution.py
@@ -99,32 +99,39 @@
     return lax.ppermute(block, "seq", [(i, i ^ 1) for i in range(count)])
 
 
-def gather_weights(w_block):
-    rows, width = w_block.shape
-    far = exchange(jnp.broadcast_to(w_block, (32, rows, width)), far_groups())
-    far = far.reshape(32 * rows, width)
+def gather_far(w_block):
+    far = exchange(jnp.broadcast_to(w_block, (32,) + w_block.shape), far_groups())
+    return far.reshape(32 * w_block.shape[0], w_block.shape[1])
+
+
+def gather_near(far):
     own = exchange(jnp.broadcast_to(far, (8,) + far.shape), near_groups())
-    other = swap_cores(own)
-    core = lax.axis_index("seq") & 1
-    both = jnp.stack([jnp.where(core == 0, own, other), jnp.where(core == 0, other, own)])
-    both = both.reshape(2, 2, 2, 2, 4, 4, 2, rows, width)
+    return own.reshape(8 * far.shape[0], far.shape[1])
+
+
+def by_holder(x_local):
+    tokens, width = x_local.shape
+    rows = width // 512
+    split = x_local.T.reshape(4, 2, 4, 2, 2, 2, 2, rows, tokens)
+    return split.transpose(4, 1, 3, 6, 0, 2, 5, 7, 8).reshape(2, 256 * rows, tokens)
+
+
+def in_order(first, second):
+    rows, width = first.shape[0] // 256, first.shape[1]
+    both = jnp.stack([first, second]).reshape(2, 2, 2, 2, 4, 4, 2, rows, width)
     return both.transpose(4, 1, 5, 2, 0, 6, 3, 7, 8).reshape(512 * rows, width)
 
 
-def scatter_sum(partial):
-    rows, width = partial.shape[0] // 512, partial.shape[1]
-    core = lax.axis_index("seq") & 1
-    split = partial.reshape(4, 2, 4, 2, 2, 2, 2, rows, width)
-
-    def half(which):
-        part = lax.dynamic_index_in_dim(split, which, 4, keepdims=False)
-        return part.transpose(1, 3, 5, 0, 2, 4, 6, 7).reshape(8, 32 * rows, width)
-
-    received = swap_cores(half(1 - core).astype(jnp.bfloat16))
-    total = (half(core) + received.astype(jnp.float32)).astype(jnp.bfloat16)
-    total = jnp.sum(exchange(total, near_groups()).astype(jnp.float32), axis=0)
+def scatter_total(total):
+    rows, width = total.shape[0] // 256, total.shape[1]
+    total = exchange(total.reshape(8, 32 * rows, width), near_groups())
+    total = jnp.sum(total.astype(jnp.float32), axis=0)
     total = total.astype(jnp.bfloat16).reshape(32, rows, width)
     return jnp.sum(exchange(total, far_groups()).astype(jnp.float32), axis=0)
+
+
+def dot32(a, b):
+    return jnp.dot(a, b, preferred_element_type=jnp.float32)
 
 
 def body(layer_inputs, doc_start, w_qkv, d_context):
@@ -136,8 +143,16 @@
     out_grad = d_context[0].reshape(tok_rows, heads, head_dim)
     doc_first = doc_start[0]
     positions = lax.axis_index("seq") * tok_rows + jnp.arange(tok_rows, dtype=jnp.int32)
-    full_weights = gather_weights(w_qkv)
-    projected = jnp.dot(x_local, full_weights, preferred_element_type=jnp.float32)
+    core = lax.axis_index("seq") & 1
+    x_rows = by_holder(x_local)
+    rows_own = lax.dynamic_index_in_dim(x_rows, core, 0, keepdims=False)
+    rows_other = lax.dynamic_index_in_dim(x_rows, 1 - core, 0, keepdims=False)
+    far = gather_far(w_qkv)
+    rows_own, rows_other, far = lax.optimization_barrier((rows_own, rows_other, far))
+    x_own, x_other = rows_own.T, rows_other.T
+    w_own = gather_near(far)
+    w_other = swap_cores(w_own)
+    projected = dot32(x_own, w_own) + dot32(x_other, w_other)
     projected = projected.astype(jnp.bfloat16)
     queries = projected[:, :q_width].reshape(tok_rows, heads, head_dim)
     key_value = projected[:, q_width:]
@@ -162,14 +177,17 @@
     grad_proj = jnp.concatenate(
         [grad_query.astype(jnp.bfloat16).reshape(tok_rows, q_width), key_grad, value_grad], axis=1
     )
+    received = swap_cores(dot32(rows_other, grad_proj).astype(jnp.bfloat16))
+    total = dot32(rows_own, grad_proj) + received.astype(jnp.float32)
+    weight_grad = scatter_total(total.astype(jnp.bfloat16))
+    full_weights = in_order(
+        jnp.where(core == 0, w_own, w_other), jnp.where(core == 0, w_other, w_own)
+    )
     input_grad = lax.dot_general(
         grad_proj, full_weights, (((1,), (1,)), ((), ())), preferred_element_type=jnp.float32
     )
     input_grad = input_grad.astype(jnp.bfloat16).reshape(1, tok_rows, x_local.shape[1])
-    partial_grad = lax.dot_general(
-        x_local, grad_proj, (((0,), (0,)), ((), ())), preferred_element_type=jnp.float32
-    )
-    return (input_grad, scatter_sum(partial_grad))
+    return (input_grad, weight_grad)
 
 
 def solution(mesh):

time: 160 us -> 137 us (0.86)
  blocking collectives: 80.8 us -> 21.5 us
  starting transfers between devices: 15.7 us -> 41 us
  waiting for transfers between devices: 21.9 us -> 41.8 us
  local copies, waits for them, and re-layouts: 18.7 us -> 9.47 us
    all_to_all x3 -> x1, blocking collectives: 80.8 us -> 21.5 us  [exchange(): return lax.all_to_all(blocks, AXES, 0, 0, axis_index_groups=groups)]
    all_to_all x1 -> x3, starting transfers between devices: 7.64 us -> 32.8 us  [exchange(): return lax.all_to_all(blocks, AXES, 0, 0, axis_index_groups=groups)]
    all_to_all x1 -> x3, waiting for transfers between devices: 9.89 us -> 29.3 us  [exchange(): return lax.all_to_all(blocks, AXES, 0, 0, axis_index_groups=groups)]
    dot_general x1 -> x0, local copies, waits for them, and re-layouts: 9.03 us -> none  [body(): lax.dot_general(x_local, grad_proj, (((0,), (0,)), ((), ())), preferred_e...]
    convert_element_type x2 -> x0, local copies, waits for them, and re-layouts: 4.17 us -> none  [scatter_sum(): received = swap_cores(half(1 - core).astype(jnp.bfloat16))]
    unnamed x9 -> x10, local copies, waits for them, and re-layouts: 0.74 us -> 4.19 us
    convert_element_type x1 -> x0, other arithmetic: 2.49 us -> none  [scatter_sum(): total = (half(core) + received.astype(jnp.float32)).astype(jnp.bfloat16)]
    transpose x1, other arithmetic: 0.39 us -> 2.61 us  [in_order(): return both.transpose(4, 1, 5, 2, 0, 6, 3, 7, 8).reshape(512 * rows, width)]
  transfers between devices with their start and end apart: 5 -> 7, of which waited for: 5 -> 7; matrix products, arithmetic and copies ran while one was open for 5% -> 15% of each run, Pallas kernels for 0% -> 0%
where the time goes in v2:
time: 137 us; the launch traced here: 136 us
  waiting for transfers between devices  41.8 us (31%)
  starting transfers between devices  41 us (30%)
  blocking collectives  21.5 us (16%)
  matrix products  11.5 us (8%)
  local copies, waits for them, and re-layouts  9.47 us (7%)
  other arithmetic  9.29 us (7%)
    all_to_all x3, starting transfers between devices, exchange(): return lax.all_to_all(blocks, AXES, 0, 0, axis_index_groups=groups)  32.8 us
    all_to_all x3, waiting for transfers between devices, exchange(): return lax.all_to_all(blocks, AXES, 0, 0, axis_index_groups=groups)  29.3 us
    all_to_all x1, blocking collectives, exchange(): return lax.all_to_all(blocks, AXES, 0, 0, axis_index_groups=groups)  21.5 us
    dot_general x4, matrix products, dot32(): return jnp.dot(a, b, preferred_element_type=jnp.float32)  7.1 us
    ppermute x2, waiting for transfers between devices, from_behind(): return lax.ppermute(block, axis, route)  6.61 us
    ppermute x2, waiting for transfers between devices, swap_cores(): return lax.ppermute(block, 'seq', [(i, i ^ 1) for i in range(count)])  5.85 us
    select_n x1, other arithmetic, body(): jnp.where(core == 0, w_own, w_other)  4.53 us
    ppermute x2, starting transfers between devices, from_behind(): return lax.ppermute(block, axis, route)  4.21 us
  transfers between devices with their start and end apart: 7, of which 7 were waited for; matrix products, arithmetic and copies ran while one was open for 15% of the time, Pallas kernels for 0%

profile of v2, /device:TPU:1, one launch (start us, length us, event | category | flops | bytes accessed | tf_op | source)
XLA Modules:
  0.0 135.6 jit_solution(10508808569824432661)
XLA Ops:
  0.6 1.4 %broadcast_in_dim.16 = bf16[32,8,512]{2,1,0:T(8,128)(2,1)} broadcast(bf16[8,512]{1,0:T(8,128)(2,1)} %param.6), dimensions={1,2} | broadcast | bytes 270336 | tf_op jit(solution)/shard_map/broadcast_in_dim | solution.py:103
  2.0 19.0 %all-to-all-start = ((bf16[32,8,512]{2,1,0:T(8,128)(2,1)}), bf16[32,8,512]{2,1,0:T(8,128)(2,1)S(1)}, u32[]{:S(2)}, u32[]{:S(2)}) async-start(bf16[32,8,512]{2,1,0:T(8,128)(2,1)} %broadcast_in_dim.16), calls=%async_computation | async-start | bytes 524288 | tf_op jit(solution)/shard_map/all_to_all | solution.py:94
  21.0 4.1 %copy.41 = bf16[1,256,4096]{1,2,0:T(8,128)(2,1)} copy(bf16[1,256,4096]{2,1,0:T(8,128)(2,1)} %param.4) | data formatting | bytes 4194304 | tf_op args[0]
  25.1 1.9 %copy.42 = bf16[2,2,2,2,4,4,2,8,256]{8,7,6,5,4,3,2,1,0:T(8,128)(2,1)S(1)} copy(bf16[2,2,2,2,4,4,2,8,256]{8,7,3,6,0,2,5,1,4:T(8,128)(2,1)} %bitcast.84) | data formatting | bytes 4194304 | tf_op jit(solution)/shard_map/transpose | solution.py:116
  27.0 1.1 dynamic-slice_bitcast_fusion
  28.1 7.7 %all-to-all-done = bf16[32,8,512]{2,1,0:T(8,128)(2,1)S(1)} async-done(((bf16[32,8,512]{2,1,0:T(8,128)(2,1)}), bf16[32,8,512]{2,1,0:T(8,128)(2,1)S(1)}, u32[]{:S(2)}, u32[]{:S(2)}) %all-to-all-start) | async-done | bytes 262176 | tf_op jit(solution)/shard_map/all_to_all | solution.py:94
  36.0 21.5 %all_to_all.20 = bf16[8,256,512]{2,1,0:T(8,128)(2,1)S(1)} all-to-all(bf16[8,256,512]{2,1,0:T(8,128)(2,1)S(1)} %broadcast_in_dim.17), channel_id=1, replica_groups={{0,1,8,9,64,65,72,73},{2,3,10,11,66,67,74,75},{16,17,24,25,80,81,88,89}..., dimensions={0} | all-to-all | bytes 4194304 | tf_op jit(solution)/shard_map/all_to_all | solution.py:94
  57.6 2.1 %collective-permute-start = (bf16[2048,512]{1,0:T(8,128)(2,1)S(1)}, bf16[2048,512]{1,0:T(8,128)(2,1)}, u32[]{:S(2)}, u32[]{:S(2)}) collective-permute-start(bf16[2048,512]{1,0:T(8,128)(2,1)S(1)} %bitcast.85), channel_id=1, source_target_pairs={{0,4},{4,0},{8,12},{12,8},{16,20},{20,16},{24,28},{28,24},{32,36},... | collective-permute-start | bytes 6291464 | tf_op jit(solution)/shard_map/ppermute | solution.py:99
  60.0 1.9 %fusion.25 = f32[256,512]{1,0:T(8,128)S(1)} fusion(bf16[2048,256]{1,0:T(8,128)(2,1)} %get-tuple-element.5, bf16[2048,512]{1,0:T(8,128)(2,1)S(1)} %bitcast.86), kind=kOutput, calls=%fused_computation.54 | convolution fusion | flops 536870912 | bytes 3670016 | tf_op jit(solution)/shard_map/dot_general | solution.py:134
  62.0 1.7 %collective-permute-done = bf16[2048,512]{1,0:T(8,128)(2,1)} collective-permute-done((bf16[2048,512]{1,0:T(8,128)(2,1)S(1)}, bf16[2048,512]{1,0:T(8,128)(2,1)}, u32[]{:S(2)}, u32[]{:S(2)}) %collective-permute-start) | collective-permute-done | bytes 2097184 | tf_op jit(solution)/shard_map/ppermute | solution.py:99
  63.7 2.3 %fusion.6 = bf16[256,512]{1,0:T(8,128)(2,1)S(1)} fusion(f32[256,512]{1,0:T(8,128)S(1)} %fusion.25, bf16[2048,256]{1,0:T(8,128)(2,1)S(1)} %get-tuple-element.7, bf16[2048,512]{1,0:T(8,128)(2,1)} %collective-permute-done), kind=kOutput, calls=%fused_computation.15 | convolution fusion | flops 537133056 | bytes 3932160 | tf_op jit(solution)/shard_map/dot_general | solution.py:134
  66.1 2.3 %collective-permute-start.1 = (bf16[256,256]{1,0:T(8,128)(2,1)S(1)}, bf16[256,256]{1,0:T(8,128)(2,1)S(1)}, u32[]{:S(2)}, u32[]{:S(2)}) collective-permute-start(bf16[256,256]{1,0:T(8,128)(2,1)S(1)} %get-tuple-element.16), channel_id=1, source_target_pairs={{0,4},{4,8},{8,12},{12,16},{16,20},{20,24},{24,28},{28,32},{32,36}... | collective-permute-start | bytes 393224 | tf_op jit(solution)/shard_map/ppermute | solution.py:12
  68.5 1.8 %collective-permute-done.1 = bf16[256,256]{1,0:T(8,128)(2,1)S(1)} collective-permute-done((bf16[256,256]{1,0:T(8,128)(2,1)S(1)}, bf16[256,256]{1,0:T(8,128)(2,1)S(1)}, u32[]{:S(2)}, u32[]{:S(2)}) %collective-permute-start.1) | collective-permute-done | bytes 131104 | tf_op jit(solution)/shard_map/ppermute | solution.py:12
  70.8 0.3 convolution_bitcast_fusion.1
  71.1 0.3 fusion.10
  71.8 0.3 fusion.7
  72.1 1.9 %collective-permute-start.2 = (bf16[256,256]{0,1:T(8,128)(2,1)S(1)}, bf16[256,256]{0,1:T(8,128)(2,1)S(1)}, u32[]{:S(2)}, u32[]{:S(2)}) collective-permute-start(bf16[256,256]{0,1:T(8,128)(2,1)S(1)} %pad_maximum_fusion.1), channel_id=1, source_target_pairs={{4,0},{8,4},{12,8},{16,12},{20,16},{24,20},{28,24},{32,28},{36,32}... | collective-permute-start | bytes 393224 | tf_op jit(solution)/shard_map/ppermute | solution.py:12
  74.3 4.8 %collective-permute-done.2 = bf16[256,256]{0,1:T(8,128)(2,1)S(1)} collective-permute-done((bf16[256,256]{0,1:T(8,128)(2,1)S(1)}, bf16[256,256]{0,1:T(8,128)(2,1)S(1)}, u32[]{:S(2)}, u32[]{:S(2)}) %collective-permute-start.2) | collective-permute-done | bytes 131104 | tf_op jit(solution)/shard_map/ppermute | solution.py:12
  79.2 0.7 convolution_convert_fusion.1
  80.0 1.9 %collective-permute-start.3 = (bf16[2048,512]{1,0:T(8,128)(2,1)S(1)}, bf16[2048,512]{1,0:T(8,128)(2,1)S(1)}, u32[]{:S(2)}, u32[]{:S(2)}) collective-permute-start(bf16[2048,512]{1,0:T(8,128)(2,1)S(1)} %convolution_convert_fusion.1), channel_id=1, source_target_pairs={{0,4},{4,0},{8,12},{12,8},{16,20},{20,16},{24,28},{28,24},{32,36},... | collective-permute-start | bytes 6291464 | tf_op jit(solution)/shard_map/ppermute | solution.py:99
  81.9 4.1 %collective-permute-done.3 = bf16[2048,512]{1,0:T(8,128)(2,1)S(1)} collective-permute-done((bf16[2048,512]{1,0:T(8,128)(2,1)S(1)}, bf16[2048,512]{1,0:T(8,128)(2,1)S(1)}, u32[]{:S(2)}, u32[]{:S(2)}) %collective-permute-start.3) | collective-permute-done | bytes 2097184 | tf_op jit(solution)/shard_map/ppermute | solution.py:99
  86.0 2.1 %add_convert_fusion = bf16[2048,512]{1,0:T(8,128)(2,1)} fusion(bf16[2048,512]{1,0:T(8,128)(2,1)S(1)} %collective-permute-done.3, bf16[2048,256]{1,0:T(8,128)(2,1)S(1)} %copy-done.1, bf16[256,128]{0,1:T(8,128)(2,1)S(1)} %get-tuple-element.13, bf16[256,128]{0,1:T(8,128)(2,1)S(1)} %get-tuple-element.12, bf16[256,256]{0,1:T(8,128)(2,1)S(1)} %bitcast.93), kind=kOutput, calls=%fused_computation.3 | convolution fusion | flops 540803072 | bytes 5505024 | tf_op jit(solution)/shard_map/dot_general | solution.py:134
  88.1 6.7 %all-to-all-start.2 = ((bf16[8,256,512]{2,1,0:T(8,128)(2,1)}), bf16[8,256,512]{2,1,0:T(8,128)(2,1)S(1)}, u32[]{:S(2)}, u32[]{:S(2)}) async-start(bf16[8,256,512]{2,1,0:T(8,128)(2,1)} %bitcast.83), calls=%async_computation.2 | async-start | bytes 4194304 | tf_op jit(solution)/shard_map/all_to_all | solution.py:94
  94.8 4.5 %broadcast_select_fusion.1 = (bf16[2048,512]{1,0:T(8,128)(2,1)}, bf16[2048,512]{1,0:T(8,128)(2,1)}) fusion(bf16[2048,512]{1,0:T(8,128)(2,1)} %collective-permute-done, pred[]{:T(512)S(6)} %eq.4, bf16[8,256,512]{2,1,0:T(8,128)(2,1)} %copy-done), kind=kLoop, calls=%fused_computation.6 | loop fusion | flops 2097152 | bytes 8388609 | tf_op jit(solution)/shard_map/jit(_where)/select_n | solution.py:184
  99.3 12.6 %all-to-all-done.2 = bf16[8,256,512]{2,1,0:T(8,128)(2,1)S(1)} async-done(((bf16[8,256,512]{2,1,0:T(8,128)(2,1)}), bf16[8,256,512]{2,1,0:T(8,128)(2,1)S(1)}, u32[]{:S(2)}, u32[]{:S(2)}) %all-to-all-start.2) | async-done | bytes 2097184 | tf_op jit(solution)/shard_map/all_to_all | solution.py:94
  112.0 1.0 reduce_sum.41
  113.0 7.2 %all-to-all-start.3 = ((bf16[32,8,512]{2,1,0:T(8,128)(2,1)}), bf16[32,8,512]{2,1,0:T(8,128)(2,1)S(1)}, u32[]{:S(2)}, u32[]{:S(2)}) async-start(bf16[32,8,512]{2,1,0:T(8,128)(2,1)} %bitcast.29), calls=%async_computation.3 | async-start | bytes 524288 | tf_op jit(solution)/shard_map/all_to_all | solution.py:94
  120.2 2.6 %maximum_bitcast_fusion = bf16[4,2,4,2,2,2,2,8,512]{8,7,5,2,0,6,3,1,4:T(8,128)(2,1)S(1)} fusion(bf16[1,2,2,2,4,4,2,8,512]{8,7,6,5,4,3,2,1,0:T(8,128)(2,1)} %bitcast.88, bf16[1,2,2,2,4,4,2,8,512]{8,7,6,5,4,3,2,1,0:T(8,128)(2,1)} %bitcast.87), kind=kLoop, calls=%fused_computation.2 | loop fusion | flops 2097152 | bytes 8388608 | tf_op jit(solution)/shard_map/transpose | solution.py:122
  122.8 0.5 copy.53
  123.4 2.6 %fusion = bf16[1,256,4096]{2,1,0:T(8,128)(2,1)} fusion(bf16[4096,512]{1,0:T(8,128)(2,1)S(1)} %bitcast.81, bf16[256,128]{0,1:T(8,128)(2,1)S(1)} %get-tuple-element.13, bf16[256,128]{0,1:T(8,128)(2,1)S(1)} %get-tuple-element.12, bf16[256,256]{0,1:T(8,128)(2,1)S(1)} %bitcast.94), kind=kOutput, calls=%fused_computation.1 | convolution fusion | flops 1075576832 | bytes 6553600 | tf_op jit(solution)/shard_map/dot_general | solution.py:186
  126.0 8.9 %all-to-all-done.3 = bf16[32,8,512]{2,1,0:T(8,128)(2,1)S(1)} async-done(((bf16[32,8,512]{2,1,0:T(8,128)(2,1)}), bf16[32,8,512]{2,1,0:T(8,128)(2,1)S(1)}, u32[]{:S(2)}, u32[]{:S(2)}) %all-to-all-start.3) | async-done | bytes 262176 | tf_op jit(solution)/shard_map/all_to_all | solution.py:94
  134.9 0.7 convert_reduce_fusion
  (27 shorter events, 1.8 us)
Async XLA Ops:
  2.0 33.8 %all-to-all-start = ((bf16[32,8,512]{2,1,0:T(8,128)(2,1)}), bf16[32,8,512]{2,1,0:T(8,128)(2,1)S(1)}, u32[]{:S(2)}, u32[]{:S(2)}) async-start(bf16[32,8,512]{2,1,0:T(8,128)(2,1)} %broadcast_in_dim.16), calls=%async_computation | async-start | bytes 524288 | tf_op jit(solution)/shard_map/all_to_all | solution.py:94
  36.0 23.7 %copy-start.2 = (bf16[1,256,256]{2,1,0:T(8,128)(2,1)S(1)}, bf16[1,256,256]{2,1,0:T(8,128)(2,1)}, u32[]{:S(2)}) copy-start(bf16[1,256,256]{2,1,0:T(8,128)(2,1)} %param.7) | copy-start | bytes 393220
  36.0 23.8 %copy-start.3 = (s32[1,256]{1,0:T(1,128)S(1)}, s32[1,256]{1,0:T(1,128)}, u32[]{:S(2)}) copy-start(s32[1,256]{1,0:T(1,128)} %param.5) | copy-start | bytes 3076
  57.6 4.4 %copy-start = (bf16[8,256,512]{2,1,0:T(8,128)(2,1)}, bf16[8,256,512]{2,1,0:T(8,128)(2,1)S(1)}, u32[]{:S(2)}) copy-start(bf16[8,256,512]{2,1,0:T(8,128)(2,1)S(1)} %all_to_all.20) | copy-start | bytes 6291460
  57.6 6.2 %collective-permute-start = (bf16[2048,512]{1,0:T(8,128)(2,1)S(1)}, bf16[2048,512]{1,0:T(8,128)(2,1)}, u32[]{:S(2)}, u32[]{:S(2)}) collective-permute-start(bf16[2048,512]{1,0:T(8,128)(2,1)S(1)} %bitcast.85), channel_id=1, source_target_pairs={{0,4},{4,0},{8,12},{12,8},{16,20},{20,16},{24,28},{28,24},{32,36},... | collective-permute-start | bytes 6291464 | tf_op jit(solution)/shard_map/ppermute | solution.py:99
  66.1 4.2 %collective-permute-start.1 = (bf16[256,256]{1,0:T(8,128)(2,1)S(1)}, bf16[256,256]{1,0:T(8,128)(2,1)S(1)}, u32[]{:S(2)}, u32[]{:S(2)}) collective-permute-start(bf16[256,256]{1,0:T(8,128)(2,1)S(1)} %get-tuple-element.16), channel_id=1, source_target_pairs={{0,4},{4,8},{8,12},{12,16},{16,20},{20,24},{24,28},{28,32},{32,36}... | collective-permute-start | bytes 393224 | tf_op jit(solution)/shard_map/ppermute | solution.py:12
  72.1 7.0 %collective-permute-start.2 = (bf16[256,256]{0,1:T(8,128)(2,1)S(1)}, bf16[256,256]{0,1:T(8,128)(2,1)S(1)}, u32[]{:S(2)}, u32[]{:S(2)}) collective-permute-start(bf16[256,256]{0,1:T(8,128)(2,1)S(1)} %pad_maximum_fusion.1), channel_id=1, source_target_pairs={{4,0},{8,4},{12,8},{16,12},{20,16},{24,20},{28,24},{32,28},{36,32}... | collective-permute-start | bytes 393224 | tf_op jit(solution)/shard_map/ppermute | solution.py:12
  79.2 6.9 %copy-start.1 = (bf16[2048,256]{1,0:T(8,128)(2,1)S(1)}, bf16[2048,256]{1,0:T(8,128)(2,1)}, u32[]{:S(2)}) copy-start(bf16[2048,256]{1,0:T(8,128)(2,1)} %get-tuple-element.5) | copy-start | bytes 3145732
  80.0 6.1 %collective-permute-start.3 = (bf16[2048,512]{1,0:T(8,128)(2,1)S(1)}, bf16[2048,512]{1,0:T(8,128)(2,1)S(1)}, u32[]{:S(2)}, u32[]{:S(2)}) collective-permute-start(bf16[2048,512]{1,0:T(8,128)(2,1)S(1)} %convolution_convert_fusion.1), channel_id=1, source_target_pairs={{0,4},{4,0},{8,12},{12,8},{16,20},{20,16},{24,28},{28,24},{32,36},... | collective-permute-start | bytes 6291464 | tf_op jit(solution)/shard_map/ppermute | solution.py:99
  88.1 23.9 %all-to-all-start.2 = ((bf16[8,256,512]{2,1,0:T(8,128)(2,1)}), bf16[8,256,512]{2,1,0:T(8,128)(2,1)S(1)}, u32[]{:S(2)}, u32[]{:S(2)}) async-start(bf16[8,256,512]{2,1,0:T(8,128)(2,1)} %bitcast.83), calls=%async_computation.2 | async-start | bytes 4194304 | tf_op jit(solution)/shard_map/all_to_all | solution.py:94
  113.0 21.9 %all-to-all-start.3 = ((bf16[32,8,512]{2,1,0:T(8,128)(2,1)}), bf16[32,8,512]{2,1,0:T(8,128)(2,1)S(1)}, u32[]{:S(2)}, u32[]{:S(2)}) async-start(bf16[32,8,512]{2,1,0:T(8,128)(2,1)} %bitcast.29), calls=%async_computation.3 | async-start | bytes 524288 | tf_op jit(solution)/shard_map/all_to_all | solution.py:94

commit v3 on v2

--- a/solution.py
+++ b/solution.py
@@ -1,6 +1,7 @@
 import jax
 import jax.numpy as jnp
 from jax import lax
+from jax.experimental.layout import Layout, with_layout_constraint
 from jax.sharding import PartitionSpec as P
 
 WIN = 256
@@ -130,6 +131,17 @@
     return jnp.sum(exchange(total, far_groups()).astype(jnp.float32), axis=0)
 
 
+def core_pair(rows, core):
+    own = lax.dynamic_index_in_dim(rows, core, 0, keepdims=False)
+    return own, lax.dynamic_index_in_dim(rows, 1 - core, 0, keepdims=False)
+
+
+def contract_rows(a, b):
+    return lax.dot_general(
+        a, b, (((0,), (0,)), ((), ())), preferred_element_type=jnp.float32
+    )
+
+
 def dot32(a, b):
     return jnp.dot(a, b, preferred_element_type=jnp.float32)
 
@@ -144,42 +156,42 @@
     doc_first = doc_start[0]
     positions = lax.axis_index("seq") * tok_rows + jnp.arange(tok_rows, dtype=jnp.int32)
     core = lax.axis_index("seq") & 1
-    x_rows = by_holder(x_local)
-    rows_own = lax.dynamic_index_in_dim(x_rows, core, 0, keepdims=False)
-    rows_other = lax.dynamic_index_in_dim(x_rows, 1 - core, 0, keepdims=False)
+    x_prior = with_layout_constraint(from_behind(x_local, "seq", 1), Layout((0, 1)))
     far = gather_far(w_qkv)
-    rows_own, rows_other, far = lax.optimization_barrier((rows_own, rows_other, far))
-    x_own, x_other = rows_own.T, rows_other.T
+    own_pair, x_prior, far = lax.optimization_barrier(
+        (core_pair(by_holder(x_local), core), x_prior, far)
+    )
     w_own = gather_near(far)
+    prior_pair = core_pair(by_holder(x_prior), core)
+    rows_own, rows_other = (
+        jnp.concatenate([a, b], axis=1) for a, b in zip(prior_pair, own_pair)
+    )
+    rows_own, rows_other, w_own = lax.optimization_barrier((rows_own, rows_other, w_own))
     w_other = swap_cores(w_own)
-    projected = dot32(x_own, w_own) + dot32(x_other, w_other)
+    projected = contract_rows(rows_own, w_own) + contract_rows(rows_other, w_other)
     projected = projected.astype(jnp.bfloat16)
-    queries = projected[:, :q_width].reshape(tok_rows, heads, head_dim)
-    key_value = projected[:, q_width:]
-    prior = from_behind(key_value, "seq", 1)
-    key_rows = jnp.concatenate([prior[:, :head_dim], key_value[:, :head_dim]], axis=0)
-    value_rows = jnp.concatenate([prior[:, head_dim:], key_value[:, head_dim:]], axis=0)
+    queries = projected[tok_rows:, :q_width].reshape(tok_rows, heads, head_dim)
+    key_rows = projected[:, q_width : q_width + head_dim]
+    value_rows = projected[:, q_width + head_dim :]
     key_pos = jnp.concatenate([positions - tok_rows, positions])
     grad_query, grad_keys, grad_values, log_total, row_dot = local_pass(
         queries, key_rows, value_rows, out_grad, doc_first, positions, key_pos
     )
-    returned = from_behind(
-        jnp.concatenate([grad_keys[:tok_rows], grad_values[:tok_rows]], axis=1).astype(
-            jnp.bfloat16
-        ),
-        "seq",
-        -1,
-    ).astype(jnp.float32)
-    far_keys = returned[:, :head_dim]
-    far_values = returned[:, head_dim:]
-    key_grad = (grad_keys[tok_rows:] + far_keys).astype(jnp.bfloat16)
-    value_grad = (grad_values[tok_rows:] + far_values).astype(jnp.bfloat16)
+    low_query = grad_query.astype(jnp.bfloat16).reshape(tok_rows, q_width)
+    grad_kv = jnp.concatenate([grad_keys, grad_values], axis=1)
+    low_kv = grad_kv.astype(jnp.bfloat16)
+    low_all = jnp.concatenate(
+        [jnp.concatenate([jnp.zeros_like(low_query), low_query], axis=0), low_kv], axis=1
+    )
+    sent = dot32(rows_other, low_all).astype(jnp.bfloat16)
+    sent, far_kv = lax.optimization_barrier((sent, low_kv[:tok_rows]))
+    received = swap_cores(sent)
+    returned = from_behind(far_kv, "seq", -1).astype(jnp.float32)
+    total = dot32(rows_own, low_all) + received.astype(jnp.float32)
+    weight_grad = scatter_total(total.astype(jnp.bfloat16))
     grad_proj = jnp.concatenate(
-        [grad_query.astype(jnp.bfloat16).reshape(tok_rows, q_width), key_grad, value_grad], axis=1
-    )
-    received = swap_cores(dot32(rows_other, grad_proj).astype(jnp.bfloat16))
-    total = dot32(rows_own, grad_proj) + received.astype(jnp.float32)
-    weight_grad = scatter_total(total.astype(jnp.bfloat16))
+        [low_query, (grad_kv[tok_rows:] + returned).astype(jnp.bfloat16)], axis=1
+    )
     full_weights = in_order(
         jnp.where(core == 0, w_own, w_other), jnp.where(core == 0, w_other, w_own)
     )

time: 137 us -> 138 us (level)
  blocking collectives: 21.5 us -> 0 us
  local copies, waits for them, and re-layouts: 9.47 us -> 17.3 us
  starting transfers between devices: 41 us -> 47.1 us
  waiting for transfers between devices: 41.8 us -> 47.5 us
  matrix products: 11.5 us -> 15.5 us
  other arithmetic: 9.29 us -> 7.4 us
    all_to_all x1 -> x0, blocking collectives: 21.5 us -> none  [exchange(): return lax.all_to_all(blocks, AXES, 0, 0, axis_index_groups=groups)]
    all_to_all x3 -> x4, waiting for transfers between devices: 29.3 us -> 43.3 us  [exchange(): return lax.all_to_all(blocks, AXES, 0, 0, axis_index_groups=groups)]
    transpose x0 -> x2, local copies, waits for them, and re-layouts: none -> 7.35 us  [by_holder(): split = x_local.T.reshape(4, 2, 4, 2, 2, 2, 2, rows, tokens)]
    ppermute x2, waiting for transfers between devices: 6.61 us -> 0.01 us  [from_behind(): return lax.ppermute(block, axis, route)]
    dot_general x0 -> x2, matrix products: none -> 4.97 us  [contract_rows(): lax.dot_general(a, b, (((0,), (0,)), ((), ())), preferred_element_type=jn...]
    dot_general x4 -> x2, matrix products: 7.1 us -> 3.85 us  [dot32(): return jnp.dot(a, b, preferred_element_type=jnp.float32)]
    ppermute x2, starting transfers between devices: 4.21 us -> 7.4 us  [from_behind(): return lax.ppermute(block, axis, route)]
    unnamed x10 -> x13, local copies, waits for them, and re-layouts: 4.19 us -> 1.19 us
  transfers between devices with their start and end apart: 7 -> 8, of which waited for: 7 -> 6; matrix products, arithmetic and copies ran while one was open for 15% -> 22% of each run, Pallas kernels for 0% -> 0%
where the time goes in v3:
time: 138 us; the launch traced here: 136 us
  waiting for transfers between devices  47.5 us (34%)
  starting transfers between devices  47.1 us (34%)
  local copies, waits for them, and re-layouts  17.3 us (13%)
  matrix products  15.5 us (11%)
  other arithmetic  7.4 us (5%)
    all_to_all x4, waiting for transfers between devices, exchange(): return lax.all_to_all(blocks, AXES, 0, 0, axis_index_groups=groups)  43.3 us
    all_to_all x4, starting transfers between devices, exchange(): return lax.all_to_all(blocks, AXES, 0, 0, axis_index_groups=groups)  35.7 us
    ppermute x2, starting transfers between devices, from_behind(): return lax.ppermute(block, axis, route)  7.4 us
    transpose x2, local copies, waits for them, and re-layouts, by_holder(): split = x_local.T.reshape(4, 2, 4, 2, 2, 2, 2, rows, tokens)  7.35 us
    dot_general x2, matrix products, contract_rows(): lax.dot_general(a, b, (((0,), (0,)), ((), ())), preferred_element_type=jn...  4.97 us
    dot_general x1, matrix products, body(): lax.dot_general(grad_proj, full_weights, (((1,), (1,)), ((), ())), prefer...  4.82 us
    ppermute x2, waiting for transfers between devices, swap_cores(): return lax.ppermute(block, 'seq', [(i, i ^ 1) for i in range(count)])  4.18 us
    ppermute x2, starting transfers between devices, swap_cores(): return lax.ppermute(block, 'seq', [(i, i ^ 1) for i in range(count)])  4.06 us
  transfers between devices with their start and end apart: 8, of which 6 were waited for; matrix products, arithmetic and copies ran while one was open for 22% of the time, Pallas kernels for 0%

profile of v3, /device:TPU:1, one launch (start us, length us, event | category | flops | bytes accessed | tf_op | source)
XLA Modules:
  0.0 135.7 jit_solution(9708740000164461956)
XLA Ops:
  0.6 5.4 %collective-permute-start = (bf16[256,4096]{1,0:T(8,128)(2,1)}, bf16[256,4096]{1,0:T(8,128)(2,1)}, u32[]{:S(2)}, u32[]{:S(2)}) collective-permute-start(bf16[256,4096]{1,0:T(8,128)(2,1)} %bitcast.97), channel_id=1, source_target_pairs={{0,4},{4,8},{8,12},{12,16},{16,20},{20,24},{24,28},{28,32},{32,36}... | collective-permute-start | bytes 6291464 | tf_op jit(solution)/shard_map/ppermute | solution.py:13
  6.0 1.4 %broadcast_in_dim.12 = bf16[32,8,512]{2,1,0:T(8,128)(2,1)} broadcast(bf16[8,512]{1,0:T(8,128)(2,1)} %param.6), dimensions={1,2} | broadcast | bytes 270336 | tf_op jit(solution)/shard_map/broadcast_in_dim | solution.py:104
  7.4 17.2 %all-to-all-start = ((bf16[32,8,512]{2,1,0:T(8,128)(2,1)}), bf16[32,8,512]{2,1,0:T(8,128)(2,1)S(1)}, u32[]{:S(2)}, u32[]{:S(2)}) async-start(bf16[32,8,512]{2,1,0:T(8,128)(2,1)} %broadcast_in_dim.12), calls=%async_computation | async-start | bytes 524288 | tf_op jit(solution)/shard_map/all_to_all | solution.py:95
  24.7 4.1 %copy.42 = bf16[4096,256]{1,0:T(8,128)(2,1)} copy(bf16[4096,256]{0,1:T(8,128)(2,1)} %bitcast.98) | data formatting | bytes 4194304 | tf_op jit(solution)/shard_map/transpose | solution.py:116
  28.8 1.9 %copy.43 = bf16[2,2,2,2,4,4,2,8,256]{8,7,6,5,4,3,2,1,0:T(8,128)(2,1)S(1)} copy(bf16[2,2,2,2,4,4,2,8,256]{8,7,3,6,0,2,5,1,4:T(8,128)(2,1)} %bitcast.91) | data formatting | bytes 4194304 | tf_op jit(solution)/shard_map/transpose | solution.py:117
  30.6 1.1 dynamic-slice_bitcast_fusion.2
  31.7 13.6 %all-to-all-done = bf16[32,8,512]{2,1,0:T(8,128)(2,1)S(1)} async-done(((bf16[32,8,512]{2,1,0:T(8,128)(2,1)}), bf16[32,8,512]{2,1,0:T(8,128)(2,1)S(1)}, u32[]{:S(2)}, u32[]{:S(2)}) %all-to-all-start) | async-done | bytes 262176 | tf_op jit(solution)/shard_map/all_to_all | solution.py:95
  45.3 1.5 %broadcast_in_dim.17 = bf16[8,256,512]{2,1,0:T(8,128)(2,1)} broadcast(bf16[256,512]{1,0:T(8,128)(2,1)S(1)} %bitcast.100), dimensions={1,2} | broadcast | bytes 2359296 | tf_op jit(solution)/shard_map/broadcast_in_dim | solution.py:109
  46.8 6.4 %all-to-all-start.1 = ((bf16[8,256,512]{2,1,0:T(8,128)(2,1)}), bf16[8,256,512]{2,1,0:T(8,128)(2,1)}, u32[]{:S(2)}, u32[]{:S(2)}) async-start(bf16[8,256,512]{2,1,0:T(8,128)(2,1)} %broadcast_in_dim.17), calls=%async_computation.1 | async-start | bytes 4194304 | tf_op jit(solution)/shard_map/all_to_all | solution.py:95
  53.3 3.3 %copy.44 = bf16[4096,256]{1,0:T(8,128)(2,1)S(1)} copy(bf16[4096,256]{0,1:T(8,128)(2,1)} %bitcast.8) | data formatting | bytes 4194304 | tf_op jit(solution)/shard_map/transpose | solution.py:116
  57.0 1.1 copy-done
  58.0 2.4 %pad_maximum_fusion = (bf16[2048,512]{1,0:T(8,128)(2,1)}, bf16[2048,512]{1,0:T(8,128)(2,1)}) fusion(bf16[2048,256]{1,0:T(8,128)(2,1)S(1)} %copy-done, bf16[2048,256]{1,0:T(8,128)(2,1)S(1)} %get-tuple-element.23, bf16[2048,256]{1,0:T(8,128)(2,1)S(1)} %get-tuple-element.13, bf16[2048,256]{1,0:T(8,128)(2,1)S(1)} %get-tuple-element.22), kind=kLoop, calls=%fused_computation.5 | loop fusion | flops 8388608 | bytes 8388608 | tf_op jit(solution)/shard_map/concatenate | solution.py:167
  60.4 10.1 %all-to-all-done.1 = bf16[8,256,512]{2,1,0:T(8,128)(2,1)} async-done(((bf16[8,256,512]{2,1,0:T(8,128)(2,1)}), bf16[8,256,512]{2,1,0:T(8,128)(2,1)}, u32[]{:S(2)}, u32[]{:S(2)}) %all-to-all-start.1) | async-done | bytes 2097184 | tf_op jit(solution)/shard_map/all_to_all | solution.py:95
  70.5 1.9 %collective-permute-start.1 = (bf16[2048,512]{1,0:T(8,128)(2,1)}, bf16[2048,512]{1,0:T(8,128)(2,1)S(1)}, u32[]{:S(2)}, u32[]{:S(2)}) collective-permute-start(bf16[2048,512]{1,0:T(8,128)(2,1)} %bitcast.14), channel_id=1, source_target_pairs={{0,4},{4,0},{8,12},{12,8},{16,20},{20,16},{24,28},{28,24},{32,36},... | collective-permute-start | bytes 6291464 | tf_op jit(solution)/shard_map/ppermute | solution.py:100
  72.8 3.7 %fusion.38 = f32[512,512]{0,1:T(8,128)S(1)} fusion(bf16[2048,512]{1,0:T(8,128)(2,1)} %get-tuple-element.15, bf16[2048,512]{1,0:T(8,128)(2,1)} %bitcast.14), kind=kOutput, calls=%fused_computation.65 | convolution fusion | flops 1073741824 | bytes 5242880 | tf_op jit(solution)/shard_map/dot_general | solution.py:140
  76.8 1.3 fusion.6
  79.0 0.3 fusion.10
  80.3 1.3 convolution_convert_fusion.1
  81.6 2.2 %collective-permute-start.3 = (bf16[2048,512]{1,0:T(8,128)(2,1)S(1)}, bf16[2048,512]{1,0:T(8,128)(2,1)S(1)}, u32[]{:S(2)}, u32[]{:S(2)}) collective-permute-start(bf16[2048,512]{1,0:T(8,128)(2,1)S(1)} %convolution_convert_fusion.1), channel_id=1, source_target_pairs={{0,4},{4,0},{8,12},{12,8},{16,20},{20,16},{24,28},{28,24},{32,36},... | collective-permute-start | bytes 6291464 | tf_op jit(solution)/shard_map/ppermute | solution.py:100
  83.7 3.9 %collective-permute-done.3 = bf16[2048,512]{1,0:T(8,128)(2,1)S(1)} collective-permute-done((bf16[2048,512]{1,0:T(8,128)(2,1)S(1)}, bf16[2048,512]{1,0:T(8,128)(2,1)S(1)}, u32[]{:S(2)}, u32[]{:S(2)}) %collective-permute-start.3) | collective-permute-done | bytes 2097184 | tf_op jit(solution)/shard_map/ppermute | solution.py:100
  87.6 2.6 %add_convert_fusion = bf16[2048,512]{1,0:T(8,128)(2,1)} fusion(bf16[2048,512]{1,0:T(8,128)(2,1)S(1)} %collective-permute-done.3, bf16[2048,512]{1,0:T(8,128)(2,1)S(1)} %copy-done.2, bf16[256,256]{0,1:T(8,128)(2,1)S(1)} %bitcast.104, bf16[512,256]{0,1:T(8,128)(2,1)S(1)} %fusion.13), kind=kOutput, calls=%fused_computation.3 | convolution fusion | flops 1078460416 | bytes 6684672 | tf_op jit(solution)/shard_map/dot_general | solution.py:146
  90.2 3.8 %all-to-all-start.2 = ((bf16[8,256,512]{2,1,0:T(8,128)(2,1)}), bf16[8,256,512]{2,1,0:T(8,128)(2,1)S(1)}, u32[]{:S(2)}, u32[]{:S(2)}) async-start(bf16[8,256,512]{2,1,0:T(8,128)(2,1)} %bitcast.99), calls=%async_computation.2 | async-start | bytes 4194304 | tf_op jit(solution)/shard_map/all_to_all | solution.py:95
  94.0 2.0 %collective-permute-start.2 = (bf16[256,256]{0,1:T(8,128)(2,1)S(1)}, bf16[256,256]{0,1:T(8,128)(2,1)S(1)}, u32[]{:S(2)}, u32[]{:S(2)}) collective-permute-start(bf16[256,256]{0,1:T(8,128)(2,1)S(1)} %slice.25), channel_id=1, source_target_pairs={{4,0},{8,4},{12,8},{16,12},{20,16},{24,20},{28,24},{32,28},{36,32}... | collective-permute-start | bytes 393224 | tf_op jit(solution)/shard_map/ppermute | solution.py:13
  96.0 2.5 %broadcast_select_fusion.1 = (bf16[2048,512]{1,0:T(8,128)(2,1)S(1)}, bf16[2048,512]{1,0:T(8,128)(2,1)S(1)}) fusion(bf16[2048,512]{1,0:T(8,128)(2,1)} %bitcast.14, bf16[2048,512]{1,0:T(8,128)(2,1)} %copy-done.1, pred[]{:T(512)S(6)} %eq.4), kind=kLoop, calls=%fused_computation.8 | loop fusion | flops 2097152 | bytes 8388609 | tf_op jit(solution)/shard_map/jit(_where)/select_n | solution.py:196
  98.5 0.4 maximum_bitcast_fusion
  98.9 2.4 %copy.55 = bf16[4,2,4,2,2,2,2,8,512]{8,7,6,5,4,3,2,1,0:T(8,128)(2,1)} copy(bf16[4,2,4,2,2,2,2,8,512]{8,7,5,2,0,6,3,1,4:T(8,128)(2,1)S(1)} %maximum_bitcast_fusion) | data formatting | bytes 8388608 | tf_op jit(solution)/shard_map/transpose | solution.py:123
  101.3 9.8 %all-to-all-done.2 = bf16[8,256,512]{2,1,0:T(8,128)(2,1)S(1)} async-done(((bf16[8,256,512]{2,1,0:T(8,128)(2,1)}), bf16[8,256,512]{2,1,0:T(8,128)(2,1)S(1)}, u32[]{:S(2)}, u32[]{:S(2)}) %all-to-all-start.2) | async-done | bytes 2097184 | tf_op jit(solution)/shard_map/all_to_all | solution.py:95
  111.1 1.0 reduce_sum.41
  112.2 8.2 %all-to-all-start.3 = ((bf16[32,8,512]{2,1,0:T(8,128)(2,1)}), bf16[32,8,512]{2,1,0:T(8,128)(2,1)S(1)}, u32[]{:S(2)}, u32[]{:S(2)}) async-start(bf16[32,8,512]{2,1,0:T(8,128)(2,1)} %bitcast.37), calls=%async_computation.3 | async-start | bytes 524288 | tf_op jit(solution)/shard_map/all_to_all | solution.py:95
  120.5 4.8 %fusion = bf16[1,256,4096]{2,1,0:T(8,128)(2,1)} fusion(bf16[4096,512]{1,0:T(8,128)(2,1)} %bitcast.87, bf16[256,256]{0,1:T(8,128)(2,1)S(1)} %fusion.22, bf16[256,256]{0,1:T(8,128)(2,1)S(1)} %bitcast.105), kind=kOutput, calls=%fused_computation.1 | convolution fusion | flops 1075314688 | bytes 6553600 | tf_op jit(solution)/shard_map/dot_general | solution.py:198
  125.3 9.8 %all-to-all-done.3 = bf16[32,8,512]{2,1,0:T(8,128)(2,1)S(1)} async-done(((bf16[32,8,512]{2,1,0:T(8,128)(2,1)}), bf16[32,8,512]{2,1,0:T(8,128)(2,1)S(1)}, u32[]{:S(2)}, u32[]{:S(2)}) %all-to-all-start.3) | async-done | bytes 262176 | tf_op jit(solution)/shard_map/all_to_all | solution.py:95
  135.1 0.7 convert_reduce_fusion
  (31 shorter events, 2.8 us)
Async XLA Ops:
  0.6 44.7 %collective-permute-start = (bf16[256,4096]{1,0:T(8,128)(2,1)}, bf16[256,4096]{1,0:T(8,128)(2,1)}, u32[]{:S(2)}, u32[]{:S(2)}) collective-permute-start(bf16[256,4096]{1,0:T(8,128)(2,1)} %bitcast.97), channel_id=1, source_target_pairs={{0,4},{4,8},{8,12},{12,16},{16,20},{20,24},{24,28},{28,32},{32,36}... | collective-permute-start | bytes 6291464 | tf_op jit(solution)/shard_map/ppermute | solution.py:13
  7.4 37.9 %all-to-all-start = ((bf16[32,8,512]{2,1,0:T(8,128)(2,1)}), bf16[32,8,512]{2,1,0:T(8,128)(2,1)S(1)}, u32[]{:S(2)}, u32[]{:S(2)}) async-start(bf16[32,8,512]{2,1,0:T(8,128)(2,1)} %broadcast_in_dim.12), calls=%async_computation | async-start | bytes 524288 | tf_op jit(solution)/shard_map/all_to_all | solution.py:95
  46.8 23.7 %all-to-all-start.1 = ((bf16[8,256,512]{2,1,0:T(8,128)(2,1)}), bf16[8,256,512]{2,1,0:T(8,128)(2,1)}, u32[]{:S(2)}, u32[]{:S(2)}) async-start(bf16[8,256,512]{2,1,0:T(8,128)(2,1)} %broadcast_in_dim.17), calls=%async_computation.1 | async-start | bytes 4194304 | tf_op jit(solution)/shard_map/all_to_all | solution.py:95
  56.8 1.2 copy-start
  58.0 14.4 %copy-start.4 = (bf16[1,256,256]{2,1,0:T(8,128)(2,1)S(1)}, bf16[1,256,256]{2,1,0:T(8,128)(2,1)}, u32[]{:S(2)}) copy-start(bf16[1,256,256]{2,1,0:T(8,128)(2,1)} %param.7) | copy-start | bytes 393220
  58.0 14.6 %copy-start.5 = (s32[1,256]{1,0:T(1,128)S(1)}, s32[1,256]{1,0:T(1,128)}, u32[]{:S(2)}) copy-start(s32[1,256]{1,0:T(1,128)} %param.5) | copy-start | bytes 3076
  70.5 6.3 %collective-permute-start.1 = (bf16[2048,512]{1,0:T(8,128)(2,1)}, bf16[2048,512]{1,0:T(8,128)(2,1)S(1)}, u32[]{:S(2)}, u32[]{:S(2)}) collective-permute-start(bf16[2048,512]{1,0:T(8,128)(2,1)} %bitcast.14), channel_id=1, source_target_pairs={{0,4},{4,0},{8,12},{12,8},{16,20},{20,16},{24,28},{28,24},{32,36},... | collective-permute-start | bytes 6291464 | tf_op jit(solution)/shard_map/ppermute | solution.py:100
  72.8 4.0 %copy-start.3 = (bf16[2048,512]{1,0:T(8,128)(2,1)S(1)}, bf16[2048,512]{1,0:T(8,128)(2,1)}, u32[]{:S(2)}) copy-start(bf16[2048,512]{1,0:T(8,128)(2,1)} %get-tuple-element.17) | copy-start | bytes 6291460
  76.8 1.3 copy-start.1
  80.3 7.3 %copy-start.2 = (bf16[2048,512]{1,0:T(8,128)(2,1)S(1)}, bf16[2048,512]{1,0:T(8,128)(2,1)}, u32[]{:S(2)}) copy-start(bf16[2048,512]{1,0:T(8,128)(2,1)} %get-tuple-element.15) | copy-start | bytes 6291460
  81.6 6.1 %collective-permute-start.3 = (bf16[2048,512]{1,0:T(8,128)(2,1)S(1)}, bf16[2048,512]{1,0:T(8,128)(2,1)S(1)}, u32[]{:S(2)}, u32[]{:S(2)}) collective-permute-start(bf16[2048,512]{1,0:T(8,128)(2,1)S(1)} %convolution_convert_fusion.1), channel_id=1, source_target_pairs={{0,4},{4,0},{8,12},{12,8},{16,20},{20,16},{24,28},{28,24},{32,36},... | collective-permute-start | bytes 6291464 | tf_op jit(solution)/shard_map/ppermute | solution.py:100
  90.2 20.9 %all-to-all-start.2 = ((bf16[8,256,512]{2,1,0:T(8,128)(2,1)}), bf16[8,256,512]{2,1,0:T(8,128)(2,1)S(1)}, u32[]{:S(2)}, u32[]{:S(2)}) async-start(bf16[8,256,512]{2,1,0:T(8,128)(2,1)} %bitcast.99), calls=%async_computation.2 | async-start | bytes 4194304 | tf_op jit(solution)/shard_map/all_to_all | solution.py:95
  94.0 26.5 %collective-permute-start.2 = (bf16[256,256]{0,1:T(8,128)(2,1)S(1)}, bf16[256,256]{0,1:T(8,128)(2,1)S(1)}, u32[]{:S(2)}, u32[]{:S(2)}) collective-permute-start(bf16[256,256]{0,1:T(8,128)(2,1)S(1)} %slice.25), channel_id=1, source_target_pairs={{4,0},{8,4},{12,8},{16,12},{20,16},{24,20},{28,24},{32,28},{36,32}... | collective-permute-start | bytes 393224 | tf_op jit(solution)/shard_map/ppermute | solution.py:13
  112.2 22.9 %all-to-all-start.3 = ((bf16[32,8,512]{2,1,0:T(8,128)(2,1)}), bf16[32,8,512]{2,1,0:T(8,128)(2,1)S(1)}, u32[]{:S(2)}, u32[]{:S(2)}) async-start(bf16[32,8,512]{2,1,0:T(8,128)(2,1)} %bitcast.37), calls=%async_computation.3 | async-start | bytes 524288 | tf_op jit(solution)/shard_map/all_to_all | solution.py:95

commit v4 on v3

--- a/solution.py
+++ b/solution.py
@@ -11,6 +11,10 @@
     devices = range(lax.axis_size(axis))
     route = [(i - distance, i) for i in devices if i - distance in devices]
     return lax.ppermute(block, axis, route)
+
+
+def from_behind_rows(rows):
+    return with_layout_constraint(from_behind(rows, "seq", 1), Layout((0, 1)))
 
 
 def masked_scores(queries, key_rows, doc_first, query_pos, key_pos):
@@ -156,15 +160,18 @@
     doc_first = doc_start[0]
     positions = lax.axis_index("seq") * tok_rows + jnp.arange(tok_rows, dtype=jnp.int32)
     core = lax.axis_index("seq") & 1
-    x_prior = with_layout_constraint(from_behind(x_local, "seq", 1), Layout((0, 1)))
+    half = tok_rows // 2
+    prior_first = from_behind_rows(x_local[:half])
     far = gather_far(w_qkv)
-    own_pair, x_prior, far = lax.optimization_barrier(
-        (core_pair(by_holder(x_local), core), x_prior, far)
-    )
+    own_pair, prior_first, far = lax.optimization_barrier(
+        (core_pair(by_holder(x_local), core), prior_first, far)
+    )
+    prior_second = from_behind_rows(x_local[half:])
     w_own = gather_near(far)
-    prior_pair = core_pair(by_holder(x_prior), core)
+    first_pair = core_pair(by_holder(prior_first), core)
+    second_pair = core_pair(by_holder(prior_second), core)
     rows_own, rows_other = (
-        jnp.concatenate([a, b], axis=1) for a, b in zip(prior_pair, own_pair)
+        jnp.concatenate(parts, axis=1) for parts in zip(first_pair, second_pair, own_pair)
     )
     rows_own, rows_other, w_own = lax.optimization_barrier((rows_own, rows_other, w_own))
     w_other = swap_cores(w_own)

time: 138 us -> 151 us (1.094)
  waiting for transfers between devices: 47.5 us -> 52.1 us
  local copies, waits for them, and re-layouts: 17.3 us -> 21.4 us
  starting transfers between devices: 47.1 us -> 50.7 us
    ppermute x2 -> x3, waiting for transfers between devices: 0.01 us -> 17.1 us  [from_behind(): return lax.ppermute(block, axis, route)]
    all_to_all x4, waiting for transfers between devices: 43.3 us -> 30.1 us  [exchange(): return lax.all_to_all(blocks, AXES, 0, 0, axis_index_groups=groups)]
    transpose x2, local copies, waits for them, and re-layouts: 7.35 us -> 3.23 us  [by_holder(): split = x_local.T.reshape(4, 2, 4, 2, 2, 2, 2, rows, tokens)]
    unnamed x13 -> x24, local copies, waits for them, and re-layouts: 1.19 us -> 4.99 us
    ppermute x2 -> x3, starting transfers between devices: 7.4 us -> 11 us  [from_behind(): return lax.ppermute(block, axis, route)]
    slice x0 -> x1, local copies, waits for them, and re-layouts: none -> 3.24 us  [body(): prior_second = from_behind_rows(x_local[half:])]
    transpose x2 -> x3, local copies, waits for them, and re-layouts: 2.13 us -> 3.43 us  [by_holder(): split.transpose(4, 1, 3, 6, 0, 2, 5, 7, 8).reshape(2, 256 * rows, tokens)]
  transfers between devices with their start and end apart: 8 -> 9, of which waited for: 6 -> 6; matrix products, arithmetic and copies ran while one was open for 22% -> 19% of each run, Pallas kernels for 0% -> 0%
where the time goes in v4:
time: 151 us; the launch traced here: 149 us
  waiting for transfers between devices  52.1 us (35%)
  starting transfers between devices  50.7 us (34%)
  local copies, waits for them, and re-layouts  21.4 us (14%)
  matrix products  16.5 us (11%)
  other arithmetic  7.29 us (5%)
    all_to_all x4, starting transfers between devices, exchange(): return lax.all_to_all(blocks, AXES, 0, 0, axis_index_groups=groups)  35.7 us
    all_to_all x4, waiting for transfers between devices, exchange(): return lax.all_to_all(blocks, AXES, 0, 0, axis_index_groups=groups)  30.1 us
    ppermute x3, waiting for transfers between devices, from_behind(): return lax.ppermute(block, axis, route)  17.1 us
    ppermute x3, starting transfers between devices, from_behind(): return lax.ppermute(block, axis, route)  11 us
    dot_general x2, matrix products, contract_rows(): lax.dot_general(a, b, (((0,), (0,)), ((), ())), preferred_element_type=jn...  5.94 us
    unnamed x24, local copies, waits for them, and re-layouts  4.99 us
    ppermute x2, waiting for transfers between devices, swap_cores(): return lax.ppermute(block, 'seq', [(i, i ^ 1) for i in range(count)])  4.84 us
    dot_general x1, matrix products, body(): lax.dot_general(grad_proj, full_weights, (((1,), (1,)), ((), ())), prefer...  4.82 us
  transfers between devices with their start and end apart: 9, of which 6 were waited for; matrix products, arithmetic and copies ran while one was open for 19% of the time, Pallas kernels for 0%

profile of v4, /device:TPU:1, one launch (start us, length us, event | category | flops | bytes accessed | tf_op | source)
XLA Modules:
  0.0 149.0 jit_solution(6284848443850352016)
XLA Ops:
  0.6 3.2 %slice_bitcast_fusion = (bf16[128,4096]{1,0:T(8,128)(2,1)}, bf16[128,4096]{1,0:T(8,128)(2,1)}) fusion(bf16[1,256,4096]{2,1,0:T(8,128)(2,1)} %param.4), kind=kLoop, calls=%fused_computation.29 | loop fusion | bytes 4194304 | tf_op jit(solution)/shard_map/slice | solution.py:169
  3.9 5.4 %collective-permute-start = (bf16[128,4096]{1,0:T(8,128)(2,1)}, bf16[128,4096]{1,0:T(8,128)(2,1)S(1)}, u32[]{:S(2)}, u32[]{:S(2)}) collective-permute-start(bf16[128,4096]{1,0:T(8,128)(2,1)} %get-tuple-element.23), channel_id=1, source_target_pairs={{0,4},{4,8},{8,12},{12,16},{16,20},{20,24},{24,28},{28,32},{32,36}... | collective-permute-start | bytes 3145736 | tf_op jit(solution)/shard_map/ppermute | solution.py:13
  10.0 17.2 %all-to-all-start = ((bf16[32,8,512]{2,1,0:T(8,128)(2,1)}), bf16[32,8,512]{2,1,0:T(8,128)(2,1)S(1)}, u32[]{:S(2)}, u32[]{:S(2)}) async-start(bf16[32,8,512]{2,1,0:T(8,128)(2,1)} %broadcast_in_dim.12), calls=%async_computation | async-start | bytes 524288 | tf_op jit(solution)/shard_map/all_to_all | solution.py:99
  27.3 2.5 %copy.46 = bf16[1,256,4096]{1,2,0:T(8,128)(2,1)} copy(bf16[1,256,4096]{2,1,0:T(8,128)(2,1)S(1)} %copy-done) | data formatting | bytes 4194304 | tf_op args[0]
  29.7 1.9 %copy.47 = bf16[2,2,2,2,4,4,2,8,256]{8,7,6,5,4,3,2,1,0:T(8,128)(2,1)S(1)} copy(bf16[2,2,2,2,4,4,2,8,256]{8,7,3,6,0,2,5,1,4:T(8,128)(2,1)} %bitcast.103) | data formatting | bytes 4194304 | tf_op jit(solution)/shard_map/transpose | solution.py:121
  31.6 1.5 dynamic-slice_bitcast_fusion
  33.1 10.6 %all-to-all-done = bf16[32,8,512]{2,1,0:T(8,128)(2,1)S(1)} async-done(((bf16[32,8,512]{2,1,0:T(8,128)(2,1)}), bf16[32,8,512]{2,1,0:T(8,128)(2,1)S(1)}, u32[]{:S(2)}, u32[]{:S(2)}) %all-to-all-start) | async-done | bytes 262176 | tf_op jit(solution)/shard_map/all_to_all | solution.py:99
  43.7 1.7 %broadcast_in_dim.17 = bf16[8,256,512]{2,1,0:T(8,128)(2,1)} broadcast(bf16[256,512]{1,0:T(8,128)(2,1)S(1)} %bitcast.117), dimensions={1,2} | broadcast | bytes 2359296 | tf_op jit(solution)/shard_map/broadcast_in_dim | solution.py:113
  45.4 3.6 %all-to-all-start.1 = ((bf16[8,256,512]{2,1,0:T(8,128)(2,1)}), bf16[8,256,512]{2,1,0:T(8,128)(2,1)S(1)}, u32[]{:S(2)}, u32[]{:S(2)}) async-start(bf16[8,256,512]{2,1,0:T(8,128)(2,1)} %broadcast_in_dim.17), calls=%async_computation.1 | async-start | bytes 4194304 | tf_op jit(solution)/shard_map/all_to_all | solution.py:99
  49.1 3.8 %collective-permute-start.1 = (bf16[128,4096]{1,0:T(8,128)(2,1)}, bf16[128,4096]{1,0:T(8,128)(2,1)}, u32[]{:S(2)}, u32[]{:S(2)}) collective-permute-start(bf16[128,4096]{1,0:T(8,128)(2,1)} %get-tuple-element.22), channel_id=1, source_target_pairs={{0,4},{4,8},{8,12},{12,16},{16,20},{20,24},{24,28},{28,32},{32,36}... | collective-permute-start | bytes 3145736 | tf_op jit(solution)/shard_map/ppermute | solution.py:13
  52.8 1.6 %copy.48 = bf16[4096,128]{1,0:T(8,128)(2,1)S(1)} copy(bf16[4096,128]{0,1:T(8,128)(2,1)} %bitcast.118) | data formatting | bytes 2097152 | tf_op jit(solution)/shard_map/transpose | solution.py:120
  54.4 1.3 copy.49
  55.7 17.1 %collective-permute-done.1 = bf16[128,4096]{1,0:T(8,128)(2,1)} collective-permute-done((bf16[128,4096]{1,0:T(8,128)(2,1)}, bf16[128,4096]{1,0:T(8,128)(2,1)}, u32[]{:S(2)}, u32[]{:S(2)}) %collective-permute-start.1) | collective-permute-done | bytes 1048608 | tf_op jit(solution)/shard_map/ppermute | solution.py:13
  72.9 1.6 %copy.50 = bf16[4096,128]{1,0:T(8,128)(2,1)S(1)} copy(bf16[4096,128]{0,1:T(8,128)(2,1)} %bitcast.15) | data formatting | bytes 2097152 | tf_op jit(solution)/shard_map/transpose | solution.py:120
  75.9 1.1 copy-done.3
  77.2 2.2 %pad_maximum_fusion = (bf16[2048,512]{1,0:T(8,128)(2,1)}, bf16[2048,512]{1,0:T(8,128)(2,1)}) fusion(bf16[2048,256]{1,0:T(8,128)(2,1)S(1)} %copy-done.4, bf16[2048,128]{1,0:T(8,128)(2,1)S(1)} %get-tuple-element.29, bf16[2048,128]{1,0:T(8,128)(2,1)S(1)} %get-tuple-element.27, bf16[2048,256]{1,0:T(8,128)(2,1)S(1)} %copy-done.3, ...), kind=kLoop, calls=%fused_computation.5 | loop fusion | flops 12582912 | bytes 8388608 | tf_op jit(solution)/shard_map/concatenate | solution.py:174
  79.5 1.9 %collective-permute-start.2 = (bf16[2048,512]{1,0:T(8,128)(2,1)S(1)}, bf16[2048,512]{1,0:T(8,128)(2,1)}, u32[]{:S(2)}, u32[]{:S(2)}) collective-permute-start(bf16[2048,512]{1,0:T(8,128)(2,1)S(1)} %bitcast.104), channel_id=1, source_target_pairs={{0,4},{4,0},{8,12},{12,8},{16,20},{20,16},{24,28},{28,24},{32,36},... | collective-permute-start | bytes 6291464 | tf_op jit(solution)/shard_map/ppermute | solution.py:104
  81.8 3.0 %fusion.38 = f32[512,512]{0,1:T(8,128)S(1)} fusion(bf16[2048,512]{1,0:T(8,128)(2,1)} %get-tuple-element.15, bf16[2048,512]{1,0:T(8,128)(2,1)S(1)} %bitcast.105), kind=kOutput, calls=%fused_computation.69 | convolution fusion | flops 1073741824 | bytes 5242880 | tf_op jit(solution)/shard_map/dot_general | solution.py:144
  85.7 2.9 %fusion.6 = bf16[512,512]{0,1:T(8,128)(2,1)S(1)} fusion(f32[512,512]{0,1:T(8,128)S(1)} %fusion.38, bf16[2048,512]{1,0:T(8,128)(2,1)S(1)} %copy-done.6, bf16[2048,512]{1,0:T(8,128)(2,1)} %collective-permute-done.2), kind=kOutput, calls=%fused_computation.17 | convolution fusion | flops 1074266112 | bytes 5767168 | tf_op jit(solution)/shard_map/dot_general | solution.py:144
  90.7 1.3 convolution_convert_fusion.1
  92.0 2.0 %collective-permute-start.4 = (bf16[2048,512]{1,0:T(8,128)(2,1)S(1)}, bf16[2048,512]{1,0:T(8,128)(2,1)S(1)}, u32[]{:S(2)}, u32[]{:S(2)}) collective-permute-start(bf16[2048,512]{1,0:T(8,128)(2,1)S(1)} %convolution_convert_fusion.1), channel_id=1, source_target_pairs={{0,4},{4,0},{8,12},{12,8},{16,20},{20,16},{24,28},{28,24},{32,36},... | collective-permute-start | bytes 6291464 | tf_op jit(solution)/shard_map/ppermute | solution.py:104
  94.1 4.0 %collective-permute-done.4 = bf16[2048,512]{1,0:T(8,128)(2,1)S(1)} collective-permute-done((bf16[2048,512]{1,0:T(8,128)(2,1)S(1)}, bf16[2048,512]{1,0:T(8,128)(2,1)S(1)}, u32[]{:S(2)}, u32[]{:S(2)}) %collective-permute-start.4) | collective-permute-done | bytes 2097184 | tf_op jit(solution)/shard_map/ppermute | solution.py:104
  98.1 2.6 %add_convert_fusion = bf16[2048,512]{1,0:T(8,128)(2,1)} fusion(bf16[2048,512]{1,0:T(8,128)(2,1)S(1)} %collective-permute-done.4, bf16[2048,512]{1,0:T(8,128)(2,1)S(1)} %copy-done.5, bf16[256,256]{0,1:T(8,128)(2,1)S(1)} %bitcast.122, bf16[512,256]{0,1:T(8,128)(2,1)S(1)} %fusion.13), kind=kOutput, calls=%fused_computation.3 | convolution fusion | flops 1078460416 | bytes 6684672 | tf_op jit(solution)/shard_map/dot_general | solution.py:150
  100.7 6.7 %all-to-all-start.2 = ((bf16[8,256,512]{2,1,0:T(8,128)(2,1)}), bf16[8,256,512]{2,1,0:T(8,128)(2,1)S(1)}, u32[]{:S(2)}, u32[]{:S(2)}) async-start(bf16[8,256,512]{2,1,0:T(8,128)(2,1)} %bitcast.116), calls=%async_computation.2 | async-start | bytes 4194304 | tf_op jit(solution)/shard_map/all_to_all | solution.py:99
  107.4 1.9 %collective-permute-start.3 = (bf16[256,256]{0,1:T(8,128)(2,1)S(1)}, bf16[256,256]{0,1:T(8,128)(2,1)S(1)}, u32[]{:S(2)}, u32[]{:S(2)}) collective-permute-start(bf16[256,256]{0,1:T(8,128)(2,1)S(1)} %slice.41), channel_id=1, source_target_pairs={{4,0},{8,4},{12,8},{16,12},{20,16},{24,20},{28,24},{32,28},{36,32}... | collective-permute-start | bytes 393224 | tf_op jit(solution)/shard_map/ppermute | solution.py:13
  109.3 2.5 %broadcast_select_fusion.1 = (bf16[2048,512]{1,0:T(8,128)(2,1)S(1)}, bf16[2048,512]{1,0:T(8,128)(2,1)S(1)}) fusion(bf16[2048,512]{1,0:T(8,128)(2,1)} %bitcast.106, bf16[2048,512]{1,0:T(8,128)(2,1)} %collective-permute-done.2, pred[]{:T(512)S(6)} %eq.4), kind=kLoop, calls=%fused_computation.8 | loop fusion | flops 2097152 | bytes 8388609 | tf_op jit(solution)/shard_map/jit(_where)/select_n | solution.py:203
  112.2 2.5 %copy.61 = bf16[4,2,4,2,2,2,2,8,512]{8,7,6,5,4,3,2,1,0:T(8,128)(2,1)} copy(bf16[4,2,4,2,2,2,2,8,512]{8,7,5,2,0,6,3,1,4:T(8,128)(2,1)S(1)} %maximum_bitcast_fusion) | data formatting | bytes 8388608 | tf_op jit(solution)/shard_map/transpose | solution.py:127
  114.6 9.9 %all-to-all-done.2 = bf16[8,256,512]{2,1,0:T(8,128)(2,1)S(1)} async-done(((bf16[8,256,512]{2,1,0:T(8,128)(2,1)}), bf16[8,256,512]{2,1,0:T(8,128)(2,1)S(1)}, u32[]{:S(2)}, u32[]{:S(2)}) %all-to-all-start.2) | async-done | bytes 2097184 | tf_op jit(solution)/shard_map/all_to_all | solution.py:99
  124.5 1.1 reduce_sum.41
  125.6 8.2 %all-to-all-start.3 = ((bf16[32,8,512]{2,1,0:T(8,128)(2,1)}), bf16[32,8,512]{2,1,0:T(8,128)(2,1)S(1)}, u32[]{:S(2)}, u32[]{:S(2)}) async-start(bf16[32,8,512]{2,1,0:T(8,128)(2,1)} %bitcast.45), calls=%async_computation.3 | async-start | bytes 524288 | tf_op jit(solution)/shard_map/all_to_all | solution.py:99
  133.9 4.8 %fusion = bf16[1,256,4096]{2,1,0:T(8,128)(2,1)} fusion(bf16[4096,512]{1,0:T(8,128)(2,1)} %bitcast.101, bf16[256,256]{0,1:T(8,128)(2,1)S(1)} %fusion.22, bf16[256,256]{0,1:T(8,128)(2,1)S(1)} %bitcast.123), kind=kOutput, calls=%fused_computation.1 | convolution fusion | flops 1075314688 | bytes 6553600 | tf_op jit(solution)/shard_map/dot_general | solution.py:205
  138.7 9.7 %all-to-all-done.3 = bf16[32,8,512]{2,1,0:T(8,128)(2,1)S(1)} async-done(((bf16[32,8,512]{2,1,0:T(8,128)(2,1)}), bf16[32,8,512]{2,1,0:T(8,128)(2,1)S(1)}, u32[]{:S(2)}, u32[]{:S(2)}) %all-to-all-start.3) | async-done | bytes 262176 | tf_op jit(solution)/shard_map/all_to_all | solution.py:99
  (47 shorter events, 6.8 us)
Async XLA Ops:
  0.6 26.6 %copy-start = (bf16[1,256,4096]{2,1,0:T(8,128)(2,1)S(1)}, bf16[1,256,4096]{2,1,0:T(8,128)(2,1)}, u32[]{:S(2)}) copy-start(bf16[1,256,4096]{2,1,0:T(8,128)(2,1)} %param.4) | copy-start | bytes 6291460
  0.6 8.6 %copy-start.9 = (bf16[8,512]{1,0:T(8,128)(2,1)S(1)}, bf16[8,512]{1,0:T(8,128)(2,1)}, u32[]{:S(2)}) copy-start(bf16[8,512]{1,0:T(8,128)(2,1)} %param.6) | copy-start | bytes 24580
  3.9 39.8 %collective-permute-start = (bf16[128,4096]{1,0:T(8,128)(2,1)}, bf16[128,4096]{1,0:T(8,128)(2,1)S(1)}, u32[]{:S(2)}, u32[]{:S(2)}) collective-permute-start(bf16[128,4096]{1,0:T(8,128)(2,1)} %get-tuple-element.23), channel_id=1, source_target_pairs={{0,4},{4,8},{8,12},{12,16},{16,20},{20,24},{24,28},{28,32},{32,36}... | collective-permute-start | bytes 3145736 | tf_op jit(solution)/shard_map/ppermute | solution.py:13
  10.0 33.6 %all-to-all-start = ((bf16[32,8,512]{2,1,0:T(8,128)(2,1)}), bf16[32,8,512]{2,1,0:T(8,128)(2,1)S(1)}, u32[]{:S(2)}, u32[]{:S(2)}) async-start(bf16[32,8,512]{2,1,0:T(8,128)(2,1)} %broadcast_in_dim.12), calls=%async_computation | async-start | bytes 524288 | tf_op jit(solution)/shard_map/all_to_all | solution.py:99
  43.7 1.8 %copy-start.7 = (bf16[128,4096]{1,0:T(8,128)(2,1)}, bf16[128,4096]{1,0:T(8,128)(2,1)S(1)}, u32[]{:S(2)}) copy-start(bf16[128,4096]{1,0:T(8,128)(2,1)S(1)} %collective-permute-done) | copy-start | bytes 3145732
  45.4 34.0 %all-to-all-start.1 = ((bf16[8,256,512]{2,1,0:T(8,128)(2,1)}), bf16[8,256,512]{2,1,0:T(8,128)(2,1)S(1)}, u32[]{:S(2)}, u32[]{:S(2)}) async-start(bf16[8,256,512]{2,1,0:T(8,128)(2,1)} %broadcast_in_dim.17), calls=%async_computation.1 | async-start | bytes 4194304 | tf_op jit(solution)/shard_map/all_to_all | solution.py:99
  49.1 23.8 %collective-permute-start.1 = (bf16[128,4096]{1,0:T(8,128)(2,1)}, bf16[128,4096]{1,0:T(8,128)(2,1)}, u32[]{:S(2)}, u32[]{:S(2)}) collective-permute-start(bf16[128,4096]{1,0:T(8,128)(2,1)} %get-tuple-element.22), channel_id=1, source_target_pairs={{0,4},{4,8},{8,12},{12,16},{16,20},{20,24},{24,28},{28,32},{32,36}... | collective-permute-start | bytes 3145736 | tf_op jit(solution)/shard_map/ppermute | solution.py:13
  74.5 1.2 copy-start.2
  75.7 1.2 copy-start.3
  75.7 1.5 %copy-start.4 = (bf16[2048,256]{1,0:T(8,128)(2,1)S(1)}, bf16[2048,256]{1,0:T(8,128)(2,1)}, u32[]{:S(2)}) copy-start(bf16[2048,256]{1,0:T(8,128)(2,1)} %get-tuple-element.12) | copy-start | bytes 3145732
  77.2 4.2 %copy-start.8 = (bf16[1,256,256]{2,1,0:T(8,128)(2,1)S(1)}, bf16[1,256,256]{2,1,0:T(8,128)(2,1)}, u32[]{:S(2)}) copy-start(bf16[1,256,256]{2,1,0:T(8,128)(2,1)} %param.7) | copy-start | bytes 393220
  77.2 4.3 %copy-start.10 = (s32[1,256]{1,0:T(1,128)S(1)}, s32[1,256]{1,0:T(1,128)}, u32[]{:S(2)}) copy-start(s32[1,256]{1,0:T(1,128)} %param.5) | copy-start | bytes 3076
  79.5 5.3 %copy-start.1 = (bf16[8,256,512]{2,1,0:T(8,128)(2,1)}, bf16[8,256,512]{2,1,0:T(8,128)(2,1)S(1)}, u32[]{:S(2)}) copy-start(bf16[8,256,512]{2,1,0:T(8,128)(2,1)S(1)} %all-to-all-done.1) | copy-start | bytes 6291460
  79.5 6.2 %collective-permute-start.2 = (bf16[2048,512]{1,0:T(8,128)(2,1)S(1)}, bf16[2048,512]{1,0:T(8,128)(2,1)}, u32[]{:S(2)}, u32[]{:S(2)}) collective-permute-start(bf16[2048,512]{1,0:T(8,128)(2,1)S(1)} %bitcast.104), channel_id=1, source_target_pairs={{0,4},{4,0},{8,12},{12,8},{16,20},{20,16},{24,28},{28,24},{32,36},... | collective-permute-start | bytes 6291464 | tf_op jit(solution)/shard_map/ppermute | solution.py:104
  81.8 3.9 %copy-start.6 = (bf16[2048,512]{1,0:T(8,128)(2,1)S(1)}, bf16[2048,512]{1,0:T(8,128)(2,1)}, u32[]{:S(2)}) copy-start(bf16[2048,512]{1,0:T(8,128)(2,1)} %get-tuple-element.17) | copy-start | bytes 6291460
  90.7 7.3 %copy-start.5 = (bf16[2048,512]{1,0:T(8,128)(2,1)S(1)}, bf16[2048,512]{1,0:T(8,128)(2,1)}, u32[]{:S(2)}) copy-start(bf16[2048,512]{1,0:T(8,128)(2,1)} %get-tuple-element.15) | copy-start | bytes 6291460
  92.0 6.1 %collective-permute-start.4 = (bf16[2048,512]{1,0:T(8,128)(2,1)S(1)}, bf16[2048,512]{1,0:T(8,128)(2,1)S(1)}, u32[]{:S(2)}, u32[]{:S(2)}) collective-permute-start(bf16[2048,512]{1,0:T(8,128)(2,1)S(1)} %convolution_convert_fusion.1), channel_id=1, source_target_pairs={{0,4},{4,0},{8,12},{12,8},{16,20},{20,16},{24,28},{28,24},{32,36},... | collective-permute-start | bytes 6291464 | tf_op jit(solution)/shard_map/ppermute | solution.py:104
  100.7 23.9 %all-to-all-start.2 = ((bf16[8,256,512]{2,1,0:T(8,128)(2,1)}), bf16[8,256,512]{2,1,0:T(8,128)(2,1)S(1)}, u32[]{:S(2)}, u32[]{:S(2)}) async-start(bf16[8,256,512]{2,1,0:T(8,128)(2,1)} %bitcast.116), calls=%async_computation.2 | async-start | bytes 4194304 | tf_op jit(solution)/shard_map/all_to_all | solution.py:99
  107.4 26.4 %collective-permute-start.3 = (bf16[256,256]{0,1:T(8,128)(2,1)S(1)}, bf16[256,256]{0,1:T(8,128)(2,1)S(1)}, u32[]{:S(2)}, u32[]{:S(2)}) collective-permute-start(bf16[256,256]{0,1:T(8,128)(2,1)S(1)} %slice.41), channel_id=1, source_target_pairs={{4,0},{8,4},{12,8},{16,12},{20,16},{24,20},{28,24},{32,28},{36,32}... | collective-permute-start | bytes 393224 | tf_op jit(solution)/shard_map/ppermute | solution.py:13
  125.6 22.7 %all-to-all-start.3 = ((bf16[32,8,512]{2,1,0:T(8,128)(2,1)}), bf16[32,8,512]{2,1,0:T(8,128)(2,1)S(1)}, u32[]{:S(2)}, u32[]{:S(2)}) async-start(bf16[32,8,512]{2,1,0:T(8,128)(2,1)} %bitcast.45), calls=%async_computation.3 | async-start | bytes 524288 | tf_op jit(solution)/shard_map/all_to_all | solution.py:99

commit v5 on v3

--- a/solution.py
+++ b/solution.py
@@ -156,12 +156,16 @@
     doc_first = doc_start[0]
     positions = lax.axis_index("seq") * tok_rows + jnp.arange(tok_rows, dtype=jnp.int32)
     core = lax.axis_index("seq") & 1
-    x_prior = with_layout_constraint(from_behind(x_local, "seq", 1), Layout((0, 1)))
+    seq_count = lax.axis_size("seq")
+    chip_pairs = [[i, (i + 1) % seq_count] for i in range(1, seq_count, 2)]
+    x_before = lax.all_gather(x_local, "seq", axis_index_groups=chip_pairs)[0]
+    x_partner = with_layout_constraint(swap_cores(x_local), Layout((0, 1)))
     far = gather_far(w_qkv)
-    own_pair, x_prior, far = lax.optimization_barrier(
-        (core_pair(by_holder(x_local), core), x_prior, far)
+    own_pair, x_partner, far = lax.optimization_barrier(
+        (core_pair(by_holder(x_local), core), x_partner, far)
     )
     w_own = gather_near(far)
+    x_prior = jnp.where(core == 0, x_before, x_partner)
     prior_pair = core_pair(by_holder(x_prior), core)
     rows_own, rows_other = (
         jnp.concatenate([a, b], axis=1) for a, b in zip(prior_pair, own_pair)

time: 138 us -> 161 us (1.17)
  between operations: 0.92 us -> 14.3 us
  waiting for transfers between devices: 47.5 us -> 54.8 us
  other arithmetic: 7.4 us -> 9.75 us
    all_gather x0 -> x1, waiting for transfers between devices: none -> 21.3 us  [body(): x_before = lax.all_gather(x_local, 'seq', axis_index_groups=chip_pairs)[0]]
    all_to_all x4, waiting for transfers between devices: 43.3 us -> 28.6 us  [exchange(): return lax.all_to_all(blocks, AXES, 0, 0, axis_index_groups=groups)]
    ppermute x2 -> x3, starting transfers between devices: 4.06 us -> 12.9 us  [swap_cores(): return lax.ppermute(block, 'seq', [(i, i ^ 1) for i in range(count)])]
    ppermute x2 -> x1, starting transfers between devices: 7.4 us -> 1.91 us  [from_behind(): return lax.ppermute(block, axis, route)]
    all_to_all x4, starting transfers between devices: 35.7 us -> 32.9 us  [exchange(): return lax.all_to_all(blocks, AXES, 0, 0, axis_index_groups=groups)]
    transpose x0 -> x1, other arithmetic: none -> 2.44 us  [by_holder(): split = x_local.T.reshape(4, 2, 4, 2, 2, 2, 2, rows, tokens)]
    transpose x2, local copies, waits for them, and re-layouts: 2.13 us -> 3.93 us  [by_holder(): split.transpose(4, 1, 3, 6, 0, 2, 5, 7, 8).reshape(2, 256 * rows, tokens)]
    ppermute x2 -> x3, waiting for transfers between devices: 4.18 us -> 4.17 us  [swap_cores(): return lax.ppermute(block, 'seq', [(i, i ^ 1) for i in range(count)])]
  transfers between devices with their start and end apart: 8 -> 9, of which waited for: 6 -> 6; matrix products, arithmetic and copies ran while one was open for 22% -> 21% of each run, Pallas kernels for 0% -> 0%
where the time goes in v5:
time: 161 us; the launch traced here: 160 us
  waiting for transfers between devices  54.8 us (34%)
  starting transfers between devices  47.7 us (30%)
  local copies, waits for them, and re-layouts  17.9 us (11%)
  matrix products  15.5 us (10%)
  between operations  14.3 us (9%)
  other arithmetic  9.75 us (6%)
    all_to_all x4, starting transfers between devices, exchange(): return lax.all_to_all(blocks, AXES, 0, 0, axis_index_groups=groups)  32.9 us
    all_to_all x4, waiting for transfers between devices, exchange(): return lax.all_to_all(blocks, AXES, 0, 0, axis_index_groups=groups)  28.6 us
    all_gather x1, waiting for transfers between devices, body(): x_before = lax.all_gather(x_local, 'seq', axis_index_groups=chip_pairs)[0]  21.3 us
    ppermute x3, starting transfers between devices, swap_cores(): return lax.ppermute(block, 'seq', [(i, i ^ 1) for i in range(count)])  12.9 us
    transpose x2, local copies, waits for them, and re-layouts, by_holder(): split = x_local.T.reshape(4, 2, 4, 2, 2, 2, 2, rows, tokens)  6.72 us
    dot_general x2, matrix products, contract_rows(): lax.dot_general(a, b, (((0,), (0,)), ((), ())), preferred_element_type=jn...  4.97 us
    dot_general x1, matrix products, body(): lax.dot_general(grad_proj, full_weights, (((1,), (1,)), ((), ())), prefer...  4.82 us
    ppermute x3, waiting for transfers between devices, swap_cores(): return lax.ppermute(block, 'seq', [(i, i ^ 1) for i in range(count)])  4.17 us
  transfers between devices with their start and end apart: 9, of which 6 were waited for; matrix products, arithmetic and copies ran while one was open for 21% of the time, Pallas kernels for 0%

profile of v5, /device:TPU:1, one launch (start us, length us, event | category | flops | bytes accessed | tf_op | source)
XLA Modules:
  0.0 160.0 jit_solution(18103878199539185318)
XLA Ops:
  7.2 0.7 all-gather.2.cloned.1.call-update
  7.9 8.8 %collective-permute-start = (bf16[256,4096]{1,0:T(8,128)(2,1)}, bf16[256,4096]{1,0:T(8,128)(2,1)}, u32[]{:S(2)}, u32[]{:S(2)}) collective-permute-start(bf16[256,4096]{1,0:T(8,128)(2,1)} %bitcast.1), channel_id=1, source_target_pairs={{0,4},{4,0},{8,12},{12,8},{16,20},{20,16},{24,28},{28,24},{32,36},... | collective-permute-start | bytes 6291464 | tf_op jit(solution)/shard_map/ppermute | solution.py:100
  16.7 0.7 broadcast_in_dim.12
  17.4 12.8 %all-to-all-start = ((bf16[32,8,512]{2,1,0:T(8,128)(2,1)}), bf16[32,8,512]{2,1,0:T(8,128)(2,1)S(1)}, u32[]{:S(2)}, u32[]{:S(2)}) async-start(bf16[32,8,512]{2,1,0:T(8,128)(2,1)} %broadcast_in_dim.12), calls=%async_computation | async-start | bytes 524288 | tf_op jit(solution)/shard_map/all_to_all | solution.py:95
  30.2 4.2 %copy.56 = bf16[4096,256]{1,0:T(8,128)(2,1)} copy(bf16[4096,256]{0,1:T(8,128)(2,1)} %bitcast.2) | data formatting | bytes 4194304 | tf_op jit(solution)/shard_map/transpose | solution.py:116
  34.5 2.1 %copy.57 = bf16[2,2,2,2,4,4,2,8,256]{8,7,6,5,4,3,2,1,0:T(8,128)(2,1)S(1)} copy(bf16[2,2,2,2,4,4,2,8,256]{8,7,3,6,0,2,5,1,4:T(8,128)(2,1)} %bitcast.98) | data formatting | bytes 4194304 | tf_op jit(solution)/shard_map/transpose | solution.py:117
  36.5 1.2 dynamic-slice_bitcast_fusion.2
  37.8 8.7 %all-to-all-done = bf16[32,8,512]{2,1,0:T(8,128)(2,1)S(1)} async-done(((bf16[32,8,512]{2,1,0:T(8,128)(2,1)}), bf16[32,8,512]{2,1,0:T(8,128)(2,1)S(1)}, u32[]{:S(2)}, u32[]{:S(2)}) %all-to-all-start) | async-done | bytes 262176 | tf_op jit(solution)/shard_map/all_to_all | solution.py:95
  46.4 1.5 broadcast_in_dim.17
  47.9 4.3 %all-to-all-start.1 = ((bf16[8,256,512]{2,1,0:T(8,128)(2,1)}), bf16[8,256,512]{2,1,0:T(8,128)(2,1)}, u32[]{:S(2)}, u32[]{:S(2)}) async-start(bf16[8,256,512]{2,1,0:T(8,128)(2,1)} %broadcast_in_dim.17), calls=%async_computation.1 | async-start | bytes 4194304 | tf_op jit(solution)/shard_map/all_to_all | solution.py:95
  52.3 21.3 %all-gather.2.cloned.1.call-done = bf16[2,256,4096]{2,1,0:T(8,128)(2,1)} async-done(((bf16[1,256,4096]{2,1,0:T(8,128)(2,1)}), bf16[2,256,4096]{2,1,0:T(8,128)(2,1)}) %all-gather.2.cloned.1.call-update) | async-done | bytes 4194320 | tf_op jit(solution)/shard_map/all_gather | solution.py:161
  73.6 2.4 %fusion.2 = bf16[4096,256]{0,1:T(8,128)(2,1)S(1)} fusion(bf16[256,4096]{1,0:T(8,128)(2,1)} %collective-permute-done, bf16[2,256,4096]{2,1,0:T(8,128)(2,1)} %all-gather.2.cloned.1.call-done, pred[]{:T(512)S(6)} %eq.2), kind=kLoop, calls=%fused_computation.7 | loop fusion | flops 1048576 | bytes 6291457 | tf_op jit(solution)/shard_map/transpose | solution.py:116
  76.1 2.5 %copy.58 = bf16[4096,256]{1,0:T(8,128)(2,1)} copy(bf16[4096,256]{0,1:T(8,128)(2,1)S(1)} %fusion.2) | data formatting | bytes 4194304 | tf_op jit(solution)/shard_map/transpose | solution.py:116
  78.5 1.9 %copy.59 = bf16[2,2,2,2,4,4,2,8,256]{8,7,6,5,4,3,2,1,0:T(8,128)(2,1)S(1)} copy(bf16[2,2,2,2,4,4,2,8,256]{8,7,3,6,0,2,5,1,4:T(8,128)(2,1)} %bitcast.97) | data formatting | bytes 4194304 | tf_op jit(solution)/shard_map/transpose | solution.py:117
  80.6 1.1 copy-done
  81.6 2.3 %pad_maximum_fusion = (bf16[2048,512]{1,0:T(8,128)(2,1)}, bf16[2048,512]{1,0:T(8,128)(2,1)}) fusion(bf16[2048,256]{1,0:T(8,128)(2,1)S(1)} %copy-done, bf16[2048,256]{1,0:T(8,128)(2,1)S(1)} %get-tuple-element.23, bf16[2048,256]{1,0:T(8,128)(2,1)S(1)} %get-tuple-element.13, bf16[2048,256]{1,0:T(8,128)(2,1)S(1)} %get-tuple-element.22), kind=kLoop, calls=%fused_computation.8 | loop fusion | flops 8388608 | bytes 8388608 | tf_op jit(solution)/shard_map/concatenate | solution.py:171
  83.9 1.9 %collective-permute-start.1 = (bf16[2048,512]{1,0:T(8,128)(2,1)}, bf16[2048,512]{1,0:T(8,128)(2,1)S(1)}, u32[]{:S(2)}, u32[]{:S(2)}) collective-permute-start(bf16[2048,512]{1,0:T(8,128)(2,1)} %bitcast.15), channel_id=1, source_target_pairs={{0,4},{4,0},{8,12},{12,8},{16,20},{20,16},{24,28},{28,24},{32,36},... | collective-permute-start | bytes 6291464 | tf_op jit(solution)/shard_map/ppermute | solution.py:100
  86.2 3.7 %fusion.40 = f32[512,512]{0,1:T(8,128)S(1)} fusion(bf16[2048,512]{1,0:T(8,128)(2,1)} %get-tuple-element.15, bf16[2048,512]{1,0:T(8,128)(2,1)} %bitcast.15), kind=kOutput, calls=%fused_computation.68 | convolution fusion | flops 1073741824 | bytes 5242880 | tf_op jit(solution)/shard_map/dot_general | solution.py:140
  90.2 1.3 fusion.8
  93.7 1.3 convolution_convert_fusion.1
  94.9 2.1 %collective-permute-start.3 = (bf16[2048,512]{1,0:T(8,128)(2,1)S(1)}, bf16[2048,512]{1,0:T(8,128)(2,1)S(1)}, u32[]{:S(2)}, u32[]{:S(2)}) collective-permute-start(bf16[2048,512]{1,0:T(8,128)(2,1)S(1)} %convolution_convert_fusion.1), channel_id=1, source_target_pairs={{0,4},{4,0},{8,12},{12,8},{16,20},{20,16},{24,28},{28,24},{32,36},... | collective-permute-start | bytes 6291464 | tf_op jit(solution)/shard_map/ppermute | solution.py:100
  97.1 3.9 %collective-permute-done.3 = bf16[2048,512]{1,0:T(8,128)(2,1)S(1)} collective-permute-done((bf16[2048,512]{1,0:T(8,128)(2,1)S(1)}, bf16[2048,512]{1,0:T(8,128)(2,1)S(1)}, u32[]{:S(2)}, u32[]{:S(2)}) %collective-permute-start.3) | collective-permute-done | bytes 2097184 | tf_op jit(solution)/shard_map/ppermute | solution.py:100
  101.0 2.6 %add_convert_fusion = bf16[2048,512]{1,0:T(8,128)(2,1)} fusion(bf16[2048,512]{1,0:T(8,128)(2,1)S(1)} %collective-permute-done.3, bf16[2048,512]{1,0:T(8,128)(2,1)S(1)} %copy-done.2, bf16[256,256]{0,1:T(8,128)(2,1)S(1)} %bitcast.109, bf16[512,256]{0,1:T(8,128)(2,1)S(1)} %fusion.15), kind=kOutput, calls=%fused_computation.3 | convolution fusion | flops 1078460416 | bytes 6684672 | tf_op jit(solution)/shard_map/dot_general | solution.py:146
  103.6 7.5 %all-to-all-start.2 = ((bf16[8,256,512]{2,1,0:T(8,128)(2,1)}), bf16[8,256,512]{2,1,0:T(8,128)(2,1)S(1)}, u32[]{:S(2)}, u32[]{:S(2)}) async-start(bf16[8,256,512]{2,1,0:T(8,128)(2,1)} %bitcast.104), calls=%async_computation.2 | async-start | bytes 4194304 | tf_op jit(solution)/shard_map/all_to_all | solution.py:95
  111.1 1.9 %collective-permute-start.2 = (bf16[256,256]{0,1:T(8,128)(2,1)S(1)}, bf16[256,256]{0,1:T(8,128)(2,1)S(1)}, u32[]{:S(2)}, u32[]{:S(2)}) collective-permute-start(bf16[256,256]{0,1:T(8,128)(2,1)S(1)} %slice.30), channel_id=1, source_target_pairs={{4,0},{8,4},{12,8},{16,12},{20,16},{24,20},{28,24},{32,28},{36,32}... | collective-permute-start | bytes 393224 | tf_op jit(solution)/shard_map/ppermute | solution.py:13
  113.0 2.5 %broadcast_select_fusion.1 = (bf16[2048,512]{1,0:T(8,128)(2,1)S(1)}, bf16[2048,512]{1,0:T(8,128)(2,1)S(1)}) fusion(bf16[2048,512]{1,0:T(8,128)(2,1)} %bitcast.15, bf16[2048,512]{1,0:T(8,128)(2,1)} %copy-done.1, pred[]{:T(512)S(6)} %eq.2), kind=kLoop, calls=%fused_computation.11 | loop fusion | flops 2097152 | bytes 8388609 | tf_op jit(solution)/shard_map/jit(_where)/select_n | solution.py:200
  115.9 2.4 %copy.69 = bf16[4,2,4,2,2,2,2,8,512]{8,7,6,5,4,3,2,1,0:T(8,128)(2,1)} copy(bf16[4,2,4,2,2,2,2,8,512]{8,7,5,2,0,6,3,1,4:T(8,128)(2,1)S(1)} %maximum_bitcast_fusion) | data formatting | bytes 8388608 | tf_op jit(solution)/shard_map/transpose | solution.py:123
  118.4 9.9 %all-to-all-done.2 = bf16[8,256,512]{2,1,0:T(8,128)(2,1)S(1)} async-done(((bf16[8,256,512]{2,1,0:T(8,128)(2,1)}), bf16[8,256,512]{2,1,0:T(8,128)(2,1)S(1)}, u32[]{:S(2)}, u32[]{:S(2)}) %all-to-all-start.2) | async-done | bytes 2097184 | tf_op jit(solution)/shard_map/all_to_all | solution.py:95
  128.3 1.0 reduce_sum.41
  129.3 8.3 %all-to-all-start.3 = ((bf16[32,8,512]{2,1,0:T(8,128)(2,1)}), bf16[32,8,512]{2,1,0:T(8,128)(2,1)S(1)}, u32[]{:S(2)}, u32[]{:S(2)}) async-start(bf16[32,8,512]{2,1,0:T(8,128)(2,1)} %bitcast.38), calls=%async_computation.3 | async-start | bytes 524288 | tf_op jit(solution)/shard_map/all_to_all | solution.py:95
  137.6 4.8 %fusion = bf16[1,256,4096]{2,1,0:T(8,128)(2,1)} fusion(bf16[4096,512]{1,0:T(8,128)(2,1)} %bitcast.94, bf16[256,256]{0,1:T(8,128)(2,1)S(1)} %fusion.24, bf16[256,256]{0,1:T(8,128)(2,1)S(1)} %bitcast.110), kind=kOutput, calls=%fused_computation.1 | convolution fusion | flops 1075314688 | bytes 6553600 | tf_op jit(solution)/shard_map/dot_general | solution.py:202
  142.5 10.0 %all-to-all-done.3 = bf16[32,8,512]{2,1,0:T(8,128)(2,1)S(1)} async-done(((bf16[32,8,512]{2,1,0:T(8,128)(2,1)}), bf16[32,8,512]{2,1,0:T(8,128)(2,1)S(1)}, u32[]{:S(2)}, u32[]{:S(2)}) %all-to-all-start.3) | async-done | bytes 262176 | tf_op jit(solution)/shard_map/all_to_all | solution.py:95
  (37 shorter events, 4.0 us)
Async XLA Ops:
  7.2 9.5 %copy-start.5 = (bf16[8,512]{1,0:T(8,128)(2,1)S(1)}, bf16[8,512]{1,0:T(8,128)(2,1)}, u32[]{:S(2)}) copy-start(bf16[8,512]{1,0:T(8,128)(2,1)} %param.6) | copy-start | bytes 24580
  7.2 66.5 %all-gather.2.cloned.1.call-start = ((), (), s32[]{:S(2)}) async-start(), calls=%async_computation.4 | async-start | bytes 6291456 | tf_op jit(solution)/shard_map/all_gather | solution.py:161
  7.9 38.5 %collective-permute-start = (bf16[256,4096]{1,0:T(8,128)(2,1)}, bf16[256,4096]{1,0:T(8,128)(2,1)}, u32[]{:S(2)}, u32[]{:S(2)}) collective-permute-start(bf16[256,4096]{1,0:T(8,128)(2,1)} %bitcast.1), channel_id=1, source_target_pairs={{0,4},{4,0},{8,12},{12,8},{16,20},{20,16},{24,28},{28,24},{32,36},... | collective-permute-start | bytes 6291464 | tf_op jit(solution)/shard_map/ppermute | solution.py:100
  17.4 29.0 %all-to-all-start = ((bf16[32,8,512]{2,1,0:T(8,128)(2,1)}), bf16[32,8,512]{2,1,0:T(8,128)(2,1)S(1)}, u32[]{:S(2)}, u32[]{:S(2)}) async-start(bf16[32,8,512]{2,1,0:T(8,128)(2,1)} %broadcast_in_dim.12), calls=%async_computation | async-start | bytes 524288 | tf_op jit(solution)/shard_map/all_to_all | solution.py:95
  47.9 36.0 %all-to-all-start.1 = ((bf16[8,256,512]{2,1,0:T(8,128)(2,1)}), bf16[8,256,512]{2,1,0:T(8,128)(2,1)}, u32[]{:S(2)}, u32[]{:S(2)}) async-start(bf16[8,256,512]{2,1,0:T(8,128)(2,1)} %broadcast_in_dim.17), calls=%async_computation.1 | async-start | bytes 4194304 | tf_op jit(solution)/shard_map/all_to_all | solution.py:95
  80.4 1.2 copy-start
  81.6 4.2 %copy-start.4 = (bf16[1,256,256]{2,1,0:T(8,128)(2,1)S(1)}, bf16[1,256,256]{2,1,0:T(8,128)(2,1)}, u32[]{:S(2)}) copy-start(bf16[1,256,256]{2,1,0:T(8,128)(2,1)} %param.7) | copy-start | bytes 393220
  81.6 4.4 %copy-start.6 = (s32[1,256]{1,0:T(1,128)S(1)}, s32[1,256]{1,0:T(1,128)}, u32[]{:S(2)}) copy-start(s32[1,256]{1,0:T(1,128)} %param.5) | copy-start | bytes 3076
  83.9 6.3 %collective-permute-start.1 = (bf16[2048,512]{1,0:T(8,128)(2,1)}, bf16[2048,512]{1,0:T(8,128)(2,1)S(1)}, u32[]{:S(2)}, u32[]{:S(2)}) collective-permute-start(bf16[2048,512]{1,0:T(8,128)(2,1)} %bitcast.15), channel_id=1, source_target_pairs={{0,4},{4,0},{8,12},{12,8},{16,20},{20,16},{24,28},{28,24},{32,36},... | collective-permute-start | bytes 6291464 | tf_op jit(solution)/shard_map/ppermute | solution.py:100
  86.2 3.9 %copy-start.3 = (bf16[2048,512]{1,0:T(8,128)(2,1)S(1)}, bf16[2048,512]{1,0:T(8,128)(2,1)}, u32[]{:S(2)}) copy-start(bf16[2048,512]{1,0:T(8,128)(2,1)} %get-tuple-element.17) | copy-start | bytes 6291460
  90.2 1.3 copy-start.1
  93.7 7.3 %copy-start.2 = (bf16[2048,512]{1,0:T(8,128)(2,1)S(1)}, bf16[2048,512]{1,0:T(8,128)(2,1)}, u32[]{:S(2)}) copy-start(bf16[2048,512]{1,0:T(8,128)(2,1)} %get-tuple-element.15) | copy-start | bytes 6291460
  94.9 6.1 %collective-permute-start.3 = (bf16[2048,512]{1,0:T(8,128)(2,1)S(1)}, bf16[2048,512]{1,0:T(8,128)(2,1)S(1)}, u32[]{:S(2)}, u32[]{:S(2)}) collective-permute-start(bf16[2048,512]{1,0:T(8,128)(2,1)S(1)} %convolution_convert_fusion.1), channel_id=1, source_target_pairs={{0,4},{4,0},{8,12},{12,8},{16,20},{20,16},{24,28},{28,24},{32,36},... | collective-permute-start | bytes 6291464 | tf_op jit(solution)/shard_map/ppermute | solution.py:100
  103.6 24.7 %all-to-all-start.2 = ((bf16[8,256,512]{2,1,0:T(8,128)(2,1)}), bf16[8,256,512]{2,1,0:T(8,128)(2,1)S(1)}, u32[]{:S(2)}, u32[]{:S(2)}) async-start(bf16[8,256,512]{2,1,0:T(8,128)(2,1)} %bitcast.104), calls=%async_computation.2 | async-start | bytes 4194304 | tf_op jit(solution)/shard_map/all_to_all | solution.py:95
  111.1 26.5 %collective-permute-start.2 = (bf16[256,256]{0,1:T(8,128)(2,1)S(1)}, bf16[256,256]{0,1:T(8,128)(2,1)S(1)}, u32[]{:S(2)}, u32[]{:S(2)}) collective-permute-start(bf16[256,256]{0,1:T(8,128)(2,1)S(1)} %slice.30), channel_id=1, source_target_pairs={{4,0},{8,4},{12,8},{16,12},{20,16},{24,20},{28,24},{32,28},{36,32}... | collective-permute-start | bytes 393224 | tf_op jit(solution)/shard_map/ppermute | solution.py:13
  129.3 23.2 %all-to-all-start.3 = ((bf16[32,8,512]{2,1,0:T(8,128)(2,1)}), bf16[32,8,512]{2,1,0:T(8,128)(2,1)S(1)}, u32[]{:S(2)}, u32[]{:S(2)}) async-start(bf16[32,8,512]{2,1,0:T(8,128)(2,1)} %bitcast.38), calls=%async_computation.3 | async-start | bytes 524288 | tf_op jit(solution)/shard_map/all_to_all | solution.py:95
Sparse Core Ops, SparseCore 0:
  10.1 63.4 all-gather.1

commit v6 on v3

--- a/solution.py
+++ b/solution.py
@@ -131,9 +131,8 @@
     return jnp.sum(exchange(total, far_groups()).astype(jnp.float32), axis=0)
 
 
-def core_pair(rows, core):
-    own = lax.dynamic_index_in_dim(rows, core, 0, keepdims=False)
-    return own, lax.dynamic_index_in_dim(rows, 1 - core, 0, keepdims=False)
+def half_rows(rows, core):
+    return lax.dynamic_index_in_dim(rows, core, 0, keepdims=False)
 
 
 def contract_rows(a, b):
@@ -156,23 +155,30 @@
     doc_first = doc_start[0]
     positions = lax.axis_index("seq") * tok_rows + jnp.arange(tok_rows, dtype=jnp.int32)
     core = lax.axis_index("seq") & 1
-    x_prior = with_layout_constraint(from_behind(x_local, "seq", 1), Layout((0, 1)))
+    first = core == 0
     far = gather_far(w_qkv)
-    own_pair, x_prior, far = lax.optimization_barrier(
-        (core_pair(by_holder(x_local), core), x_prior, far)
-    )
-    w_own = gather_near(far)
-    prior_pair = core_pair(by_holder(x_prior), core)
-    rows_own, rows_other = (
-        jnp.concatenate([a, b], axis=1) for a, b in zip(prior_pair, own_pair)
-    )
-    rows_own, rows_other, w_own = lax.optimization_barrier((rows_own, rows_other, w_own))
-    w_other = swap_cores(w_own)
-    projected = contract_rows(rows_own, w_own) + contract_rows(rows_other, w_other)
-    projected = projected.astype(jnp.bfloat16)
-    queries = projected[tok_rows:, :q_width].reshape(tok_rows, heads, head_dim)
-    key_rows = projected[:, q_width : q_width + head_dim]
-    value_rows = projected[:, q_width + head_dim :]
+    x_partner = with_layout_constraint(swap_cores(x_local), Layout((0, 1)))
+    rows_mine, x_partner, far = lax.optimization_barrier(
+        (half_rows(by_holder(x_local), core), x_partner, far)
+    )
+    x_half = jnp.concatenate([rows_mine, half_rows(by_holder(x_partner), core)], axis=1)
+    w_half = gather_near(far)
+    x_half, w_half = lax.optimization_barrier((x_half, w_half))
+    partial = contract_rows(x_half, w_half)
+    mine, theirs = partial[:tok_rows], partial[tok_rows:]
+    got = swap_cores(
+        jnp.concatenate([theirs, mine[:, q_width:]], axis=1).astype(jnp.bfloat16)
+    ).astype(jnp.float32)
+    width = mine.shape[1]
+    projected = (mine + got[:, :width]).astype(jnp.bfloat16)
+    partner_kv = (theirs[:, q_width:] + got[:, width:]).astype(jnp.bfloat16)
+    queries = projected[:, :q_width].reshape(tok_rows, heads, head_dim)
+    key_value = projected[:, q_width:]
+    seq_count = lax.axis_size("seq")
+    before = lax.ppermute(key_value, "seq", [(i, i + 1) for i in range(1, seq_count - 1, 2)])
+    prior = jnp.where(first, before, partner_kv)
+    key_rows = jnp.concatenate([prior[:, :head_dim], key_value[:, :head_dim]], axis=0)
+    value_rows = jnp.concatenate([prior[:, head_dim:], key_value[:, head_dim:]], axis=0)
     key_pos = jnp.concatenate([positions - tok_rows, positions])
     grad_query, grad_keys, grad_values, log_total, row_dot = local_pass(
         queries, key_rows, value_rows, out_grad, doc_first, positions, key_pos
@@ -180,20 +186,25 @@
     low_query = grad_query.astype(jnp.bfloat16).reshape(tok_rows, q_width)
     grad_kv = jnp.concatenate([grad_keys, grad_values], axis=1)
     low_kv = grad_kv.astype(jnp.bfloat16)
-    low_all = jnp.concatenate(
-        [jnp.concatenate([jnp.zeros_like(low_query), low_query], axis=0), low_kv], axis=1
-    )
-    sent = dot32(rows_other, low_all).astype(jnp.bfloat16)
-    sent, far_kv = lax.optimization_barrier((sent, low_kv[:tok_rows]))
-    received = swap_cores(sent)
-    returned = from_behind(far_kv, "seq", -1).astype(jnp.float32)
-    total = dot32(rows_own, low_all) + received.astype(jnp.float32)
-    weight_grad = scatter_total(total.astype(jnp.bfloat16))
+    far_kv, own_kv = low_kv[:tok_rows], low_kv[tok_rows:]
+    got = swap_cores(jnp.concatenate([low_query, own_kv, far_kv], axis=1))
+    got_query, got_own = got[:, :q_width], got[:, q_width : 2 * q_width]
+    got_far = got[:, 2 * q_width :]
+    returned = from_behind(jnp.where(first, far_kv, got_far), "seq", -2)
+    mine_far = jnp.where(first, got_far, returned).astype(jnp.float32)
+    partner_far = jnp.where(first, returned, far_kv).astype(jnp.float32)
     grad_proj = jnp.concatenate(
-        [low_query, (grad_kv[tok_rows:] + returned).astype(jnp.bfloat16)], axis=1
-    )
+        [low_query, (grad_kv[tok_rows:] + mine_far).astype(jnp.bfloat16)], axis=1
+    )
+    partner_proj = jnp.concatenate(
+        [got_query, (got_own.astype(jnp.float32) + partner_far).astype(jnp.bfloat16)], axis=1
+    )
+    total = dot32(x_half, jnp.concatenate([grad_proj, partner_proj], axis=0))
+    w_half, total = lax.optimization_barrier((w_half, total.astype(jnp.bfloat16)))
+    weight_grad = scatter_total(total)
+    w_rest = swap_cores(w_half)
     full_weights = in_order(
-        jnp.where(core == 0, w_own, w_other), jnp.where(core == 0, w_other, w_own)
+        jnp.where(first, w_half, w_rest), jnp.where(first, w_rest, w_half)
     )
     input_grad = lax.dot_general(
         grad_proj, full_weights, (((1,), (1,)), ((), ())), preferred_element_type=jnp.float32

time: 138 us -> 142 us (1.029)
  waiting for transfers between devices: 47.5 us -> 54.9 us
  matrix products: 15.5 us -> 11 us
  local copies, waits for them, and re-layouts: 17.3 us -> 13.5 us
  other arithmetic: 7.4 us -> 11.1 us
  starting transfers between devices: 47.1 us -> 49.8 us
    ppermute x2 -> x4, starting transfers between devices: 4.06 us -> 15 us  [swap_cores(): return lax.ppermute(block, 'seq', [(i, i ^ 1) for i in range(count)])]
    ppermute x2 -> x1, waiting for transfers between devices: 0.01 us -> 6.36 us  [from_behind(): return lax.ppermute(block, axis, route)]
    ppermute x2 -> x1, starting transfers between devices: 7.4 us -> 1.29 us  [from_behind(): return lax.ppermute(block, axis, route)]
    all_to_all x4, starting transfers between devices: 35.7 us -> 29.7 us  [exchange(): return lax.all_to_all(blocks, AXES, 0, 0, axis_index_groups=groups)]
    ppermute x0 -> x1, starting transfers between devices: none -> 3.71 us  [body(): lax.ppermute(key_value, 'seq', [(i, i + 1) for i in range(1, seq_count -...]
    all_to_all x4, waiting for transfers between devices: 43.3 us -> 39.7 us  [exchange(): return lax.all_to_all(blocks, AXES, 0, 0, axis_index_groups=groups)]
    ppermute x2 -> x4, waiting for transfers between devices: 4.18 us -> 6.85 us  [swap_cores(): return lax.ppermute(block, 'seq', [(i, i ^ 1) for i in range(count)])]
    select_n x1 -> x2, other arithmetic: 2.5 us -> 4.87 us  [the longest x1 3.87 us: body(): jnp.where(first, w_half, w_rest)]
  transfers between devices with their start and end apart: 8 -> 10, of which waited for: 6 -> 9; matrix products, arithmetic and copies ran while one was open for 22% -> 15% of each run, Pallas kernels for 0% -> 0%
where the time goes in v6:
time: 142 us; the launch traced here: 141 us
  waiting for transfers between devices  54.9 us (39%)
  starting transfers between devices  49.8 us (35%)
  local copies, waits for them, and re-layouts  13.5 us (10%)
  other arithmetic  11.1 us (8%)
  matrix products  11 us (8%)
    all_to_all x4, waiting for transfers between devices, exchange(): return lax.all_to_all(blocks, AXES, 0, 0, axis_index_groups=groups)  39.7 us
    all_to_all x4, starting transfers between devices, exchange(): return lax.all_to_all(blocks, AXES, 0, 0, axis_index_groups=groups)  29.7 us
    ppermute x4, starting transfers between devices, swap_cores(): return lax.ppermute(block, 'seq', [(i, i ^ 1) for i in range(count)])  15 us
    ppermute x4, waiting for transfers between devices, swap_cores(): return lax.ppermute(block, 'seq', [(i, i ^ 1) for i in range(count)])  6.85 us
    transpose x2, local copies, waits for them, and re-layouts, by_holder(): split = x_local.T.reshape(4, 2, 4, 2, 2, 2, 2, rows, tokens)  6.55 us
    ppermute x1, waiting for transfers between devices, from_behind(): return lax.ppermute(block, axis, route)  6.36 us
    dot_general x1, matrix products, contract_rows(): lax.dot_general(a, b, (((0,), (0,)), ((), ())), preferred_element_type=jn...  3.89 us
    select_n x1, other arithmetic, body(): jnp.where(first, w_half, w_rest)  3.87 us
  transfers between devices with their start and end apart: 10, of which 9 were waited for; matrix products, arithmetic and copies ran while one was open for 15% of the time, Pallas kernels for 0%

profile of v6, /device:TPU:1, one launch (start us, length us, event | category | flops | bytes accessed | tf_op | source)
XLA Modules:
  0.0 141.1 jit_solution(2535448815222440776)
XLA Ops:
  0.6 8.8 %collective-permute-start = (bf16[256,4096]{1,0:T(8,128)(2,1)}, bf16[256,4096]{1,0:T(8,128)(2,1)}, u32[]{:S(2)}, u32[]{:S(2)}) collective-permute-start(bf16[256,4096]{1,0:T(8,128)(2,1)} %bitcast.90), channel_id=1, source_target_pairs={{0,4},{4,0},{8,12},{12,8},{16,20},{20,16},{24,28},{28,24},{32,36},... | collective-permute-start | bytes 6291464 | tf_op jit(solution)/shard_map/ppermute | solution.py:100
  9.4 1.4 %broadcast_in_dim.16 = bf16[32,8,512]{2,1,0:T(8,128)(2,1)} broadcast(bf16[8,512]{1,0:T(8,128)(2,1)} %param.6), dimensions={1,2} | broadcast | bytes 270336 | tf_op jit(solution)/shard_map/broadcast_in_dim | solution.py:104
  10.8 12.8 %all-to-all-start = ((bf16[32,8,512]{2,1,0:T(8,128)(2,1)}), bf16[32,8,512]{2,1,0:T(8,128)(2,1)S(1)}, u32[]{:S(2)}, u32[]{:S(2)}) async-start(bf16[32,8,512]{2,1,0:T(8,128)(2,1)} %broadcast_in_dim.16), calls=%async_computation | async-start | bytes 524288 | tf_op jit(solution)/shard_map/all_to_all | solution.py:95
  23.6 3.3 %copy.42 = bf16[4096,256]{1,0:T(8,128)(2,1)S(1)} copy(bf16[4096,256]{0,1:T(8,128)(2,1)} %bitcast.91) | data formatting | bytes 4194304 | tf_op jit(solution)/shard_map/transpose | solution.py:116
  26.9 1.6 %copy.43 = bf16[2,2,2,2,4,4,2,8,256]{8,7,6,5,4,3,2,1,0:T(8,128)(2,1)} copy(bf16[2,2,2,2,4,4,2,8,256]{8,7,3,6,0,2,5,1,4:T(8,128)(2,1)S(1)} %bitcast.82) | data formatting | bytes 4194304 | tf_op jit(solution)/shard_map/transpose | solution.py:117
  28.5 1.3 dynamic-slice_bitcast_fusion.1
  29.8 9.8 %all-to-all-done = bf16[32,8,512]{2,1,0:T(8,128)(2,1)S(1)} async-done(((bf16[32,8,512]{2,1,0:T(8,128)(2,1)}), bf16[32,8,512]{2,1,0:T(8,128)(2,1)S(1)}, u32[]{:S(2)}, u32[]{:S(2)}) %all-to-all-start) | async-done | bytes 262176 | tf_op jit(solution)/shard_map/all_to_all | solution.py:95
  39.6 1.5 %broadcast_in_dim.17 = bf16[8,256,512]{2,1,0:T(8,128)(2,1)} broadcast(bf16[256,512]{1,0:T(8,128)(2,1)S(1)} %bitcast.96), dimensions={1,2} | broadcast | bytes 2359296 | tf_op jit(solution)/shard_map/broadcast_in_dim | solution.py:109
  41.1 4.4 %all-to-all-start.1 = ((bf16[8,256,512]{2,1,0:T(8,128)(2,1)}), bf16[8,256,512]{2,1,0:T(8,128)(2,1)}, u32[]{:S(2)}, u32[]{:S(2)}) async-start(bf16[8,256,512]{2,1,0:T(8,128)(2,1)} %broadcast_in_dim.17), calls=%async_computation.1 | async-start | bytes 4194304 | tf_op jit(solution)/shard_map/all_to_all | solution.py:95
  45.4 3.3 %copy.44 = bf16[4096,256]{1,0:T(8,128)(2,1)S(1)} copy(bf16[4096,256]{0,1:T(8,128)(2,1)} %bitcast.7) | data formatting | bytes 4194304 | tf_op jit(solution)/shard_map/transpose | solution.py:116
  49.3 13.3 %all-to-all-done.1 = bf16[8,256,512]{2,1,0:T(8,128)(2,1)} async-done(((bf16[8,256,512]{2,1,0:T(8,128)(2,1)}), bf16[8,256,512]{2,1,0:T(8,128)(2,1)}, u32[]{:S(2)}, u32[]{:S(2)}) %all-to-all-start.1) | async-done | bytes 2097184 | tf_op jit(solution)/shard_map/all_to_all | solution.py:95
  62.6 3.9 %fusion.41 = (bf16[512,512]{0,1:T(8,128)(2,1)S(1)}, f32[512,512]{0,1:T(8,128)}) fusion(bf16[2048,512]{1,0:T(8,128)(2,1)S(1)} %pad_maximum_fusion, bf16[2048,512]{1,0:T(8,128)(2,1)} %bitcast.12), kind=kOutput, calls=%fused_computation.72 | convolution fusion | flops 1074003968 | bytes 5767168 | tf_op jit(solution)/shard_map/dot_general | solution.py:139
  66.6 2.2 %collective-permute-start.1 = (bf16[256,768]{0,1:T(8,128)(2,1)S(1)}, bf16[256,768]{0,1:T(8,128)(2,1)S(1)}, u32[]{:S(2)}, u32[]{:S(2)}) collective-permute-start(bf16[256,768]{0,1:T(8,128)(2,1)S(1)} %pad_maximum_fusion.2), channel_id=1, source_target_pairs={{0,4},{4,0},{8,12},{12,8},{16,20},{20,16},{24,28},{28,24},{32,36},... | collective-permute-start | bytes 1179656 | tf_op jit(solution)/shard_map/ppermute | solution.py:100
  69.2 1.0 collective-permute-done.1
  70.3 1.1 fusion.12
  71.4 3.7 %collective-permute-start.2 = (bf16[256,256]{0,1:T(8,128)(2,1)S(1)}, bf16[256,256]{0,1:T(8,128)(2,1)S(1)}, u32[]{:S(2)}, u32[]{:S(2)}) collective-permute-start(bf16[256,256]{0,1:T(8,128)(2,1)S(1)} %get-tuple-element.26), channel_id=1, source_target_pairs={{4,8},{12,16},{20,24},{28,32},{36,40},{44,48},{52,56},{60,64},{68,... | collective-permute-start | bytes 393224 | tf_op jit(solution)/shard_map/ppermute | solution.py:178
  75.1 1.9 %collective-permute-done.2 = bf16[256,256]{0,1:T(8,128)(2,1)S(1)} collective-permute-done((bf16[256,256]{0,1:T(8,128)(2,1)S(1)}, bf16[256,256]{0,1:T(8,128)(2,1)S(1)}, u32[]{:S(2)}, u32[]{:S(2)}) %collective-permute-start.2) | collective-permute-done | bytes 131104 | tf_op jit(solution)/shard_map/ppermute | solution.py:178
  80.2 1.9 %collective-permute-start.3 = (bf16[256,768]{0,1:T(8,128)(2,1)S(1)}, bf16[256,768]{0,1:T(8,128)(2,1)S(1)}, u32[]{:S(2)}, u32[]{:S(2)}) collective-permute-start(bf16[256,768]{0,1:T(8,128)(2,1)S(1)} %pad_maximum_fusion.3), channel_id=1, source_target_pairs={{0,4},{4,0},{8,12},{12,8},{16,20},{20,16},{24,28},{28,24},{32,36},... | collective-permute-start | bytes 1179656 | tf_op jit(solution)/shard_map/ppermute | solution.py:100
  82.2 1.7 %collective-permute-done.3 = bf16[256,768]{0,1:T(8,128)(2,1)S(1)} collective-permute-done((bf16[256,768]{0,1:T(8,128)(2,1)S(1)}, bf16[256,768]{0,1:T(8,128)(2,1)S(1)}, u32[]{:S(2)}, u32[]{:S(2)}) %collective-permute-start.3) | collective-permute-done | bytes 393248 | tf_op jit(solution)/shard_map/ppermute | solution.py:100
  83.9 1.3 collective-permute-start.4
  85.2 6.4 %collective-permute-done.4 = bf16[256,256]{0,1:T(8,128)(2,1)S(1)} collective-permute-done((bf16[256,256]{0,1:T(8,128)(2,1)S(1)}, bf16[256,256]{0,1:T(8,128)(2,1)S(1)}, u32[]{:S(2)}, u32[]{:S(2)}) %collective-permute-start.4) | collective-permute-done | bytes 131104 | tf_op jit(solution)/shard_map/ppermute | solution.py:13
  91.6 2.6 %convolution_convert_fusion.1 = bf16[2048,512]{1,0:T(8,128)(2,1)} fusion(bf16[2048,512]{1,0:T(8,128)(2,1)S(1)} %pad_maximum_fusion, bf16[256,256]{0,1:T(8,128)(2,1)S(1)} %get-tuple-element.19, bf16[256,256]{0,1:T(8,128)(2,1)S(1)} %get-tuple-element.20, bf16[256,256]{0,1:T(8,128)(2,1)S(1)} %get-tuple-element.18, bf16[256,256]{0,1:T(8,128)(2,1)S(1)} %bitcast.94), kind=kOutput, calls=%fused_computation.3 | convolution fusion | flops 1076887552 | bytes 4718592 | tf_op jit(solution)/shard_map/dot_general | solution.py:145
  94.2 5.8 %all-to-all-start.2 = ((bf16[8,256,512]{2,1,0:T(8,128)(2,1)}), bf16[8,256,512]{2,1,0:T(8,128)(2,1)S(1)}, u32[]{:S(2)}, u32[]{:S(2)}) async-start(bf16[8,256,512]{2,1,0:T(8,128)(2,1)} %bitcast.92), calls=%async_computation.2 | async-start | bytes 4194304 | tf_op jit(solution)/shard_map/all_to_all | solution.py:95
  100.1 2.1 %collective-permute-start.5 = (bf16[2048,512]{1,0:T(8,128)(2,1)}, bf16[2048,512]{1,0:T(8,128)(2,1)S(1)}, u32[]{:S(2)}, u32[]{:S(2)}) collective-permute-start(bf16[2048,512]{1,0:T(8,128)(2,1)} %bitcast.12), channel_id=1, source_target_pairs={{0,4},{4,0},{8,12},{12,8},{16,20},{20,16},{24,28},{28,24},{32,36},... | collective-permute-start | bytes 6291464 | tf_op jit(solution)/shard_map/ppermute | solution.py:100
  102.2 4.1 %collective-permute-done.5 = bf16[2048,512]{1,0:T(8,128)(2,1)S(1)} collective-permute-done((bf16[2048,512]{1,0:T(8,128)(2,1)}, bf16[2048,512]{1,0:T(8,128)(2,1)S(1)}, u32[]{:S(2)}, u32[]{:S(2)}) %collective-permute-start.5) | collective-permute-done | bytes 2097184 | tf_op jit(solution)/shard_map/ppermute | solution.py:100
  106.3 3.9 %broadcast_select_fusion.1 = (bf16[2048,512]{1,0:T(8,128)(2,1)}, bf16[2048,512]{1,0:T(8,128)(2,1)}) fusion(bf16[2048,512]{1,0:T(8,128)(2,1)} %bitcast.12, bf16[2048,512]{1,0:T(8,128)(2,1)S(1)} %collective-permute-done.5, pred[]{:T(512)S(6)} %eq.3), kind=kLoop, calls=%fused_computation.6 | loop fusion | flops 2097152 | bytes 8388609 | tf_op jit(solution)/shard_map/jit(_where)/select_n | solution.py:207
  110.2 7.0 %all-to-all-done.2 = bf16[8,256,512]{2,1,0:T(8,128)(2,1)S(1)} async-done(((bf16[8,256,512]{2,1,0:T(8,128)(2,1)}), bf16[8,256,512]{2,1,0:T(8,128)(2,1)S(1)}, u32[]{:S(2)}, u32[]{:S(2)}) %all-to-all-start.2) | async-done | bytes 2097184 | tf_op jit(solution)/shard_map/all_to_all | solution.py:95
  117.3 1.1 reduce_sum.41
  118.3 6.8 %all-to-all-start.3 = ((bf16[32,8,512]{2,1,0:T(8,128)(2,1)}), bf16[32,8,512]{2,1,0:T(8,128)(2,1)S(1)}, u32[]{:S(2)}, u32[]{:S(2)}) async-start(bf16[32,8,512]{2,1,0:T(8,128)(2,1)} %bitcast.35), calls=%async_computation.3 | async-start | bytes 524288 | tf_op jit(solution)/shard_map/all_to_all | solution.py:95
  125.1 2.6 %maximum_bitcast_fusion = bf16[4,2,4,2,2,2,2,8,512]{8,7,5,2,0,6,3,1,4:T(8,128)(2,1)S(1)} fusion(bf16[1,2,2,2,4,4,2,8,512]{8,7,6,5,4,3,2,1,0:T(8,128)(2,1)} %bitcast.84, bf16[1,2,2,2,4,4,2,8,512]{8,7,6,5,4,3,2,1,0:T(8,128)(2,1)} %bitcast.83), kind=kLoop, calls=%fused_computation.2 | loop fusion | flops 2097152 | bytes 8388608 | tf_op jit(solution)/shard_map/transpose | solution.py:123
  128.2 2.6 %fusion = bf16[1,256,4096]{2,1,0:T(8,128)(2,1)} fusion(bf16[4096,512]{1,0:T(8,128)(2,1)S(1)} %bitcast.80, bf16[256,256]{0,1:T(8,128)(2,1)S(1)} %get-tuple-element.18, bf16[256,256]{0,1:T(8,128)(2,1)S(1)} %bitcast.95), kind=kOutput, calls=%fused_computation.1 | convolution fusion | flops 1075314688 | bytes 6553600 | tf_op jit(solution)/shard_map/dot_general | solution.py:209
  130.9 9.6 %all-to-all-done.3 = bf16[32,8,512]{2,1,0:T(8,128)(2,1)S(1)} async-done(((bf16[32,8,512]{2,1,0:T(8,128)(2,1)}), bf16[32,8,512]{2,1,0:T(8,128)(2,1)S(1)}, u32[]{:S(2)}, u32[]{:S(2)}) %all-to-all-start.3) | async-done | bytes 262176 | tf_op jit(solution)/shard_map/all_to_all | solution.py:95
  (35 shorter events, 5.4 us)
Async XLA Ops:
  0.6 38.9 %collective-permute-start = (bf16[256,4096]{1,0:T(8,128)(2,1)}, bf16[256,4096]{1,0:T(8,128)(2,1)}, u32[]{:S(2)}, u32[]{:S(2)}) collective-permute-start(bf16[256,4096]{1,0:T(8,128)(2,1)} %bitcast.90), channel_id=1, source_target_pairs={{0,4},{4,0},{8,12},{12,8},{16,20},{20,16},{24,28},{28,24},{32,36},... | collective-permute-start | bytes 6291464 | tf_op jit(solution)/shard_map/ppermute | solution.py:100
  10.8 28.7 %all-to-all-start = ((bf16[32,8,512]{2,1,0:T(8,128)(2,1)}), bf16[32,8,512]{2,1,0:T(8,128)(2,1)S(1)}, u32[]{:S(2)}, u32[]{:S(2)}) async-start(bf16[32,8,512]{2,1,0:T(8,128)(2,1)} %broadcast_in_dim.16), calls=%async_computation | async-start | bytes 524288 | tf_op jit(solution)/shard_map/all_to_all | solution.py:95
  41.1 21.5 %all-to-all-start.1 = ((bf16[8,256,512]{2,1,0:T(8,128)(2,1)}), bf16[8,256,512]{2,1,0:T(8,128)(2,1)}, u32[]{:S(2)}, u32[]{:S(2)}) async-start(bf16[8,256,512]{2,1,0:T(8,128)(2,1)} %broadcast_in_dim.17), calls=%async_computation.1 | async-start | bytes 4194304 | tf_op jit(solution)/shard_map/all_to_all | solution.py:95
  62.6 6.2 %copy-start = (bf16[1,256,256]{2,1,0:T(8,128)(2,1)S(1)}, bf16[1,256,256]{2,1,0:T(8,128)(2,1)}, u32[]{:S(2)}) copy-start(bf16[1,256,256]{2,1,0:T(8,128)(2,1)} %param.7) | copy-start | bytes 393220
  62.6 6.3 %copy-start.1 = (s32[1,256]{1,0:T(1,128)S(1)}, s32[1,256]{1,0:T(1,128)}, u32[]{:S(2)}) copy-start(s32[1,256]{1,0:T(1,128)} %param.5) | copy-start | bytes 3076
  66.6 3.6 %collective-permute-start.1 = (bf16[256,768]{0,1:T(8,128)(2,1)S(1)}, bf16[256,768]{0,1:T(8,128)(2,1)S(1)}, u32[]{:S(2)}, u32[]{:S(2)}) collective-permute-start(bf16[256,768]{0,1:T(8,128)(2,1)S(1)} %pad_maximum_fusion.2), channel_id=1, source_target_pairs={{0,4},{4,0},{8,12},{12,8},{16,20},{20,16},{24,28},{28,24},{32,36},... | collective-permute-start | bytes 1179656 | tf_op jit(solution)/shard_map/ppermute | solution.py:100
  71.4 5.6 %collective-permute-start.2 = (bf16[256,256]{0,1:T(8,128)(2,1)S(1)}, bf16[256,256]{0,1:T(8,128)(2,1)S(1)}, u32[]{:S(2)}, u32[]{:S(2)}) collective-permute-start(bf16[256,256]{0,1:T(8,128)(2,1)S(1)} %get-tuple-element.26), channel_id=1, source_target_pairs={{4,8},{12,16},{20,24},{28,32},{36,40},{44,48},{52,56},{60,64},{68,... | collective-permute-start | bytes 393224 | tf_op jit(solution)/shard_map/ppermute | solution.py:178
  80.2 3.6 %collective-permute-start.3 = (bf16[256,768]{0,1:T(8,128)(2,1)S(1)}, bf16[256,768]{0,1:T(8,128)(2,1)S(1)}, u32[]{:S(2)}, u32[]{:S(2)}) collective-permute-start(bf16[256,768]{0,1:T(8,128)(2,1)S(1)} %pad_maximum_fusion.3), channel_id=1, source_target_pairs={{0,4},{4,0},{8,12},{12,8},{16,20},{20,16},{24,28},{28,24},{32,36},... | collective-permute-start | bytes 1179656 | tf_op jit(solution)/shard_map/ppermute | solution.py:100
  83.9 7.7 %collective-permute-start.4 = (bf16[256,256]{0,1:T(8,128)(2,1)S(1)}, bf16[256,256]{0,1:T(8,128)(2,1)S(1)}, u32[]{:S(2)}, u32[]{:S(2)}) collective-permute-start(bf16[256,256]{0,1:T(8,128)(2,1)S(1)} %get-tuple-element.21), channel_id=1, source_target_pairs={{8,0},{12,4},{16,8},{20,12},{24,16},{28,20},{32,24},{36,28},{40,32... | collective-permute-start | bytes 393224 | tf_op jit(solution)/shard_map/ppermute | solution.py:13
  94.2 23.0 %all-to-all-start.2 = ((bf16[8,256,512]{2,1,0:T(8,128)(2,1)}), bf16[8,256,512]{2,1,0:T(8,128)(2,1)S(1)}, u32[]{:S(2)}, u32[]{:S(2)}) async-start(bf16[8,256,512]{2,1,0:T(8,128)(2,1)} %bitcast.92), calls=%async_computation.2 | async-start | bytes 4194304 | tf_op jit(solution)/shard_map/all_to_all | solution.py:95
  100.1 6.3 %collective-permute-start.5 = (bf16[2048,512]{1,0:T(8,128)(2,1)}, bf16[2048,512]{1,0:T(8,128)(2,1)S(1)}, u32[]{:S(2)}, u32[]{:S(2)}) collective-permute-start(bf16[2048,512]{1,0:T(8,128)(2,1)} %bitcast.12), channel_id=1, source_target_pairs={{0,4},{4,0},{8,12},{12,8},{16,20},{20,16},{24,28},{28,24},{32,36},... | collective-permute-start | bytes 6291464 | tf_op jit(solution)/shard_map/ppermute | solution.py:100
  118.3 22.1 %all-to-all-start.3 = ((bf16[32,8,512]{2,1,0:T(8,128)(2,1)}), bf16[32,8,512]{2,1,0:T(8,128)(2,1)S(1)}, u32[]{:S(2)}, u32[]{:S(2)}) async-start(bf16[32,8,512]{2,1,0:T(8,128)(2,1)} %bitcast.35), calls=%async_computation.3 | async-start | bytes 524288 | tf_op jit(solution)/shard_map/all_to_all | solution.py:95

commit v7 on v2

--- a/solution.py
+++ b/solution.py
@@ -152,11 +152,11 @@
     x_own, x_other = rows_own.T, rows_other.T
     w_own = gather_near(far)
     w_other = swap_cores(w_own)
-    projected = dot32(x_own, w_own) + dot32(x_other, w_other)
-    projected = projected.astype(jnp.bfloat16)
-    queries = projected[:, :q_width].reshape(tok_rows, heads, head_dim)
-    key_value = projected[:, q_width:]
+    key_value = dot32(x_own, w_own[:, q_width:]) + dot32(x_other, w_other[:, q_width:])
+    key_value = key_value.astype(jnp.bfloat16)
     prior = from_behind(key_value, "seq", 1)
+    queries = dot32(x_own, w_own[:, :q_width]) + dot32(x_other, w_other[:, :q_width])
+    queries = queries.astype(jnp.bfloat16).reshape(tok_rows, heads, head_dim)
     key_rows = jnp.concatenate([prior[:, :head_dim], key_value[:, :head_dim]], axis=0)
     value_rows = jnp.concatenate([prior[:, head_dim:], key_value[:, head_dim:]], axis=0)
     key_pos = jnp.concatenate([positions - tok_rows, positions])
@@ -174,11 +174,14 @@
     far_values = returned[:, head_dim:]
     key_grad = (grad_keys[tok_rows:] + far_keys).astype(jnp.bfloat16)
     value_grad = (grad_values[tok_rows:] + far_values).astype(jnp.bfloat16)
-    grad_proj = jnp.concatenate(
-        [grad_query.astype(jnp.bfloat16).reshape(tok_rows, q_width), key_grad, value_grad], axis=1
-    )
-    received = swap_cores(dot32(rows_other, grad_proj).astype(jnp.bfloat16))
-    total = dot32(rows_own, grad_proj) + received.astype(jnp.float32)
+    low_query = grad_query.astype(jnp.bfloat16).reshape(tok_rows, q_width)
+    low_kv = jnp.concatenate([key_grad, value_grad], axis=1)
+    grad_proj = jnp.concatenate([low_query, low_kv], axis=1)
+    received = [
+        swap_cores(dot32(rows_other, part).astype(jnp.bfloat16)) for part in (low_query, low_kv)
+    ]
+    own = lax.optimization_barrier(dot32(rows_own, grad_proj).astype(jnp.bfloat16))
+    total = own.astype(jnp.float32) + jnp.concatenate(received, axis=1).astype(jnp.float32)
     weight_grad = scatter_total(total.astype(jnp.bfloat16))
     full_weights = in_order(
         jnp.where(core == 0, w_own, w_other), jnp.where(core == 0, w_other, w_own)

time: 137 us -> 136 us (level)
  waiting for transfers between devices: 41.8 us -> 37.5 us
  other arithmetic: 9.29 us -> 11.5 us
  starting transfers between devices: 41 us -> 43 us
    ppermute x2, waiting for transfers between devices: 6.61 us -> 2.83 us  [from_behind(): return lax.ppermute(block, axis, route)]
    ppermute x2 -> x3, waiting for transfers between devices: 5.85 us -> 3.25 us  [swap_cores(): return lax.ppermute(block, 'seq', [(i, i ^ 1) for i in range(count)])]
    all_to_all x3, waiting for transfers between devices: 29.3 us -> 31.4 us  [exchange(): return lax.all_to_all(blocks, AXES, 0, 0, axis_index_groups=groups)]
    ppermute x2 -> x3, starting transfers between devices: 4.03 us -> 5.95 us  [swap_cores(): return lax.ppermute(block, 'seq', [(i, i ^ 1) for i in range(count)])]
    convert_element_type x0 -> x1, other arithmetic: none -> 1.89 us  [body(): weight_grad = scatter_total(total.astype(jnp.bfloat16))]
    reduce_sum x1, other arithmetic: 1.04 us -> 2.66 us  [scatter_total(): total = jnp.sum(total.astype(jnp.float32), axis=0)]
    dot_general x4 -> x7, matrix products: 7.1 us -> 7.4 us  [dot32(): return jnp.dot(a, b, preferred_element_type=jnp.float32)]
  transfers between devices with their start and end apart: 7 -> 8, of which waited for: 7 -> 7; matrix products, arithmetic and copies ran while one was open for 15% -> 16% of each run, Pallas kernels for 0% -> 0%
where the time goes in v7:
time: 136 us
  starting transfers between devices  43 us (32%)
  waiting for transfers between devices  37.5 us (28%)
  blocking collectives  21.5 us (16%)
  matrix products  11.8 us (9%)
  other arithmetic  11.5 us (8%)
  local copies, waits for them, and re-layouts  9.34 us (7%)
    all_to_all x3, starting transfers between devices, exchange(): return lax.all_to_all(blocks, AXES, 0, 0, axis_index_groups=groups)  32.8 us
    all_to_all x3, waiting for transfers between devices, exchange(): return lax.all_to_all(blocks, AXES, 0, 0, axis_index_groups=groups)  31.4 us
    all_to_all x1, blocking collectives, exchange(): return lax.all_to_all(blocks, AXES, 0, 0, axis_index_groups=groups)  21.5 us
    dot_general x7, matrix products, dot32(): return jnp.dot(a, b, preferred_element_type=jnp.float32)  7.4 us
    ppermute x3, starting transfers between devices, swap_cores(): return lax.ppermute(block, 'seq', [(i, i ^ 1) for i in range(count)])  5.95 us
    ppermute x2, starting transfers between devices, from_behind(): return lax.ppermute(block, axis, route)  4.21 us
    unnamed x10, local copies, waits for them, and re-layouts  4.2 us
    select_n x1, other arithmetic, body(): jnp.where(core == 0, w_own, w_other)  3.86 us
  transfers between devices with their start and end apart: 8, of which 7 were waited for; matrix products, arithmetic and copies ran while one was open for 16% of the time, Pallas kernels for 0%

profile of v7, /device:TPU:1, one launch (start us, length us, event | category | flops | bytes accessed | tf_op | source)
XLA Modules:
  0.0 135.6 jit_solution(17192039651642027830)
XLA Ops:
  0.6 1.4 %broadcast_in_dim.16 = bf16[32,8,512]{2,1,0:T(8,128)(2,1)} broadcast(bf16[8,512]{1,0:T(8,128)(2,1)} %param.6), dimensions={1,2} | broadcast | bytes 270336 | tf_op jit(solution)/shard_map/broadcast_in_dim | solution.py:103
  2.0 19.0 %all-to-all-start = ((bf16[32,8,512]{2,1,0:T(8,128)(2,1)}), bf16[32,8,512]{2,1,0:T(8,128)(2,1)S(1)}, u32[]{:S(2)}, u32[]{:S(2)}) async-start(bf16[32,8,512]{2,1,0:T(8,128)(2,1)} %broadcast_in_dim.16), calls=%async_computation | async-start | bytes 524288 | tf_op jit(solution)/shard_map/all_to_all | solution.py:94
  21.0 4.1 %copy.38 = bf16[1,256,4096]{1,2,0:T(8,128)(2,1)} copy(bf16[1,256,4096]{2,1,0:T(8,128)(2,1)} %param.4) | data formatting | bytes 4194304 | tf_op args[0]
  25.1 1.9 %copy.39 = bf16[2,2,2,2,4,4,2,8,256]{8,7,6,5,4,3,2,1,0:T(8,128)(2,1)S(1)} copy(bf16[2,2,2,2,4,4,2,8,256]{8,7,3,6,0,2,5,1,4:T(8,128)(2,1)} %bitcast.89) | data formatting | bytes 4194304 | tf_op jit(solution)/shard_map/transpose | solution.py:116
  27.0 1.1 dynamic-slice_bitcast_fusion
  28.1 7.8 %all-to-all-done = bf16[32,8,512]{2,1,0:T(8,128)(2,1)S(1)} async-done(((bf16[32,8,512]{2,1,0:T(8,128)(2,1)}), bf16[32,8,512]{2,1,0:T(8,128)(2,1)S(1)}, u32[]{:S(2)}, u32[]{:S(2)}) %all-to-all-start) | async-done | bytes 262176 | tf_op jit(solution)/shard_map/all_to_all | solution.py:94
  36.0 21.5 %all_to_all.20 = bf16[8,256,512]{2,1,0:T(8,128)(2,1)S(1)} all-to-all(bf16[8,256,512]{2,1,0:T(8,128)(2,1)S(1)} %broadcast_in_dim.17), channel_id=1, replica_groups={{0,1,8,9,64,65,72,73},{2,3,10,11,66,67,74,75},{16,17,24,25,80,81,88,89}..., dimensions={0} | all-to-all | bytes 4194304 | tf_op jit(solution)/shard_map/all_to_all | solution.py:94
  57.6 2.1 %collective-permute-start = (bf16[2048,512]{1,0:T(8,128)(2,1)S(1)}, bf16[2048,512]{1,0:T(8,128)(2,1)}, u32[]{:S(2)}, u32[]{:S(2)}) collective-permute-start(bf16[2048,512]{1,0:T(8,128)(2,1)S(1)} %bitcast.84), channel_id=1, source_target_pairs={{0,4},{4,0},{8,12},{12,8},{16,20},{20,16},{24,28},{28,24},{32,36},... | collective-permute-start | bytes 6291464 | tf_op jit(solution)/shard_map/ppermute | solution.py:99
  60.1 1.7 %fusion.16 = f32[256,256]{1,0:T(8,128)S(1)} fusion(bf16[2048,256]{1,0:T(8,128)(2,1)} %get-tuple-element.5, bf16[2048,512]{1,0:T(8,128)(2,1)S(1)} %bitcast.85), kind=kOutput, calls=%fused_computation.32 | convolution fusion | flops 268435456 | bytes 2359296 | tf_op jit(solution)/shard_map/dot_general | solution.py:134
  61.8 0.5 fusion.13
  62.4 1.4 %collective-permute-done = bf16[2048,512]{1,0:T(8,128)(2,1)} collective-permute-done((bf16[2048,512]{1,0:T(8,128)(2,1)S(1)}, bf16[2048,512]{1,0:T(8,128)(2,1)}, u32[]{:S(2)}, u32[]{:S(2)}) %collective-permute-start) | collective-permute-done | bytes 2097184 | tf_op jit(solution)/shard_map/ppermute | solution.py:99
  63.7 1.7 %fusion.8 = bf16[256,256]{1,0:T(8,128)(2,1)S(1)} fusion(f32[256,256]{1,0:T(8,128)S(1)} %fusion.16, bf16[2048,256]{1,0:T(8,128)(2,1)S(1)} %get-tuple-element.7, bf16[2048,512]{1,0:T(8,128)(2,1)} %collective-permute-done), kind=kOutput, calls=%fused_computation.24 | convolution fusion | flops 268566528 | bytes 2490368 | tf_op jit(solution)/shard_map/dot_general | solution.py:134
  65.4 2.3 %collective-permute-start.1 = (bf16[256,256]{1,0:T(8,128)(2,1)S(1)}, bf16[256,256]{1,0:T(8,128)(2,1)S(1)}, u32[]{:S(2)}, u32[]{:S(2)}) collective-permute-start(bf16[256,256]{1,0:T(8,128)(2,1)S(1)} %fusion.8), channel_id=1, source_target_pairs={{0,4},{4,8},{8,12},{12,16},{16,20},{20,24},{24,28},{28,32},{32,36}... | collective-permute-start | bytes 393224 | tf_op jit(solution)/shard_map/ppermute | solution.py:12
  67.7 1.8 %fusion.9 = bf16[256,256]{0,1:T(8,128)(2,1)S(1)} fusion(f32[256,256]{0,1:T(8,128)S(1)} %fusion.13, bf16[2048,256]{1,0:T(8,128)(2,1)S(1)} %get-tuple-element.7, bf16[2048,512]{1,0:T(8,128)(2,1)} %collective-permute-done), kind=kOutput, calls=%fused_computation.25 | convolution fusion | flops 268566528 | bytes 2490368 | tf_op jit(solution)/shard_map/dot_general | solution.py:134
  71.7 1.9 %collective-permute-start.2 = (bf16[256,256]{0,1:T(8,128)(2,1)S(1)}, bf16[256,256]{0,1:T(8,128)(2,1)S(1)}, u32[]{:S(2)}, u32[]{:S(2)}) collective-permute-start(bf16[256,256]{0,1:T(8,128)(2,1)S(1)} %pad_maximum_fusion.1), channel_id=1, source_target_pairs={{4,0},{8,4},{12,8},{16,12},{20,16},{24,20},{28,24},{32,28},{36,32}... | collective-permute-start | bytes 393224 | tf_op jit(solution)/shard_map/ppermute | solution.py:12
  74.1 1.9 %collective-permute-start.3 = (bf16[2048,256]{1,0:T(8,128)(2,1)S(1)}, bf16[2048,256]{1,0:T(8,128)(2,1)S(1)}, u32[]{:S(2)}, u32[]{:S(2)}) collective-permute-start(bf16[2048,256]{1,0:T(8,128)(2,1)S(1)} %convolution_convert_fusion.3), channel_id=1, source_target_pairs={{0,4},{4,0},{8,12},{12,8},{16,20},{20,16},{24,28},{28,24},{32,36},... | collective-permute-start | bytes 3145736 | tf_op jit(solution)/shard_map/ppermute | solution.py:99
  76.1 2.7 %collective-permute-done.2 = bf16[256,256]{0,1:T(8,128)(2,1)S(1)} collective-permute-done((bf16[256,256]{0,1:T(8,128)(2,1)S(1)}, bf16[256,256]{0,1:T(8,128)(2,1)S(1)}, u32[]{:S(2)}, u32[]{:S(2)}) %collective-permute-start.2) | collective-permute-done | bytes 131104 | tf_op jit(solution)/shard_map/ppermute | solution.py:12
  78.8 0.5 convolution_convert_fusion.2
  79.3 1.9 %collective-permute-start.4 = (bf16[2048,256]{1,0:T(8,128)(2,1)S(1)}, bf16[2048,256]{1,0:T(8,128)(2,1)S(1)}, u32[]{:S(2)}, u32[]{:S(2)}) collective-permute-start(bf16[2048,256]{1,0:T(8,128)(2,1)S(1)} %convolution_convert_fusion.2), channel_id=1, source_target_pairs={{0,4},{4,0},{8,12},{12,8},{16,20},{20,16},{24,28},{28,24},{32,36},... | collective-permute-start | bytes 3145736 | tf_op jit(solution)/shard_map/ppermute | solution.py:99
  81.2 0.7 convolution_convert_fusion.1
  82.0 1.9 %collective-permute-done.4 = bf16[2048,256]{1,0:T(8,128)(2,1)S(1)} collective-permute-done((bf16[2048,256]{1,0:T(8,128)(2,1)S(1)}, bf16[2048,256]{1,0:T(8,128)(2,1)S(1)}, u32[]{:S(2)}, u32[]{:S(2)}) %collective-permute-start.4) | collective-permute-done | bytes 1048608 | tf_op jit(solution)/shard_map/ppermute | solution.py:99
  83.9 1.9 %add_convert_fusion = bf16[2048,512]{1,0:T(8,128)(2,1)} fusion(bf16[2048,512]{1,0:T(8,128)(2,1)S(1)} %convolution_convert_fusion.1, bf16[2048,256]{1,0:T(8,128)(2,1)S(1)} %collective-permute-done.4, bf16[2048,256]{1,0:T(8,128)(2,1)S(1)} %collective-permute-done.3), kind=kLoop, calls=%fused_computation.3 | loop fusion | flops 7340032 | bytes 6291456 | tf_op jit(solution)/shard_map/convert_element_type | solution.py:185
  85.7 6.7 %all-to-all-start.2 = ((bf16[8,256,512]{2,1,0:T(8,128)(2,1)}), bf16[8,256,512]{2,1,0:T(8,128)(2,1)}, u32[]{:S(2)}, u32[]{:S(2)}) async-start(bf16[8,256,512]{2,1,0:T(8,128)(2,1)} %bitcast.87), calls=%async_computation.2 | async-start | bytes 4194304 | tf_op jit(solution)/shard_map/all_to_all | solution.py:94
  92.4 3.9 %broadcast_select_fusion.1 = (bf16[2048,512]{1,0:T(8,128)(2,1)}, bf16[2048,512]{1,0:T(8,128)(2,1)}) fusion(bf16[2048,512]{1,0:T(8,128)(2,1)} %collective-permute-done, pred[]{:T(512)S(6)} %eq.4, bf16[8,256,512]{2,1,0:T(8,128)(2,1)S(1)} %all_to_all.20), kind=kLoop, calls=%fused_computation.8 | loop fusion | flops 2097152 | bytes 8388609 | tf_op jit(solution)/shard_map/jit(_where)/select_n | solution.py:187
  96.3 13.4 %all-to-all-done.2 = bf16[8,256,512]{2,1,0:T(8,128)(2,1)} async-done(((bf16[8,256,512]{2,1,0:T(8,128)(2,1)}), bf16[8,256,512]{2,1,0:T(8,128)(2,1)}, u32[]{:S(2)}, u32[]{:S(2)}) %all-to-all-start.2) | async-done | bytes 2097184 | tf_op jit(solution)/shard_map/all_to_all | solution.py:94
  109.7 2.7 %reduce_sum.41 = bf16[256,512]{1,0:T(8,128)(2,1)} reduce(bf16[8,256,512]{2,1,0:T(8,128)(2,1)} %all-to-all-done.2, bf16[]{:T(256)} %constant.35.clone.1), dimensions={0}, to_apply=%region_3.4 | reduce | flops 917504 | bytes 2359298 | tf_op jit(solution)/shard_map/reduce_sum | solution.py:128
  112.4 7.2 %all-to-all-start.3 = ((bf16[32,8,512]{2,1,0:T(8,128)(2,1)}), bf16[32,8,512]{2,1,0:T(8,128)(2,1)S(1)}, u32[]{:S(2)}, u32[]{:S(2)}) async-start(bf16[32,8,512]{2,1,0:T(8,128)(2,1)} %bitcast.31), calls=%async_computation.3 | async-start | bytes 524288 | tf_op jit(solution)/shard_map/all_to_all | solution.py:94
  119.6 2.0 %maximum_bitcast_fusion = bf16[4,2,4,2,2,2,2,8,512]{8,7,5,2,0,6,3,1,4:T(8,128)(2,1)S(1)} fusion(bf16[1,2,2,2,4,4,2,8,512]{8,7,6,5,4,3,2,1,0:T(8,128)(2,1)} %bitcast.91, bf16[1,2,2,2,4,4,2,8,512]{8,7,6,5,4,3,2,1,0:T(8,128)(2,1)S(1)} %bitcast.90), kind=kLoop, calls=%fused_computation.2 | loop fusion | flops 2097152 | bytes 8388608 | tf_op jit(solution)/shard_map/transpose | solution.py:122
  121.5 0.5 copy.49
  122.1 2.6 %fusion = bf16[1,256,4096]{2,1,0:T(8,128)(2,1)} fusion(bf16[4096,512]{1,0:T(8,128)(2,1)S(1)} %bitcast.83, bf16[256,128]{0,1:T(8,128)(2,1)S(1)} %get-tuple-element.13, bf16[256,128]{0,1:T(8,128)(2,1)S(1)} %get-tuple-element.12, bf16[256,256]{0,1:T(8,128)(2,1)S(1)} %bitcast.97), kind=kOutput, calls=%fused_computation.1 | convolution fusion | flops 1075576832 | bytes 6553600 | tf_op jit(solution)/shard_map/dot_general | solution.py:189
  124.7 10.2 %all-to-all-done.3 = bf16[32,8,512]{2,1,0:T(8,128)(2,1)S(1)} async-done(((bf16[32,8,512]{2,1,0:T(8,128)(2,1)}), bf16[32,8,512]{2,1,0:T(8,128)(2,1)S(1)}, u32[]{:S(2)}, u32[]{:S(2)}) %all-to-all-start.3) | async-done | bytes 262176 | tf_op jit(solution)/shard_map/all_to_all | solution.py:94
  135.0 0.7 convert_reduce_fusion
  (31 shorter events, 3.2 us)
Async XLA Ops:
  2.0 33.8 %all-to-all-start = ((bf16[32,8,512]{2,1,0:T(8,128)(2,1)}), bf16[32,8,512]{2,1,0:T(8,128)(2,1)S(1)}, u32[]{:S(2)}, u32[]{:S(2)}) async-start(bf16[32,8,512]{2,1,0:T(8,128)(2,1)} %broadcast_in_dim.16), calls=%async_computation | async-start | bytes 524288 | tf_op jit(solution)/shard_map/all_to_all | solution.py:94
  36.0 23.7 %copy-start.2 = (bf16[1,256,256]{2,1,0:T(8,128)(2,1)S(1)}, bf16[1,256,256]{2,1,0:T(8,128)(2,1)}, u32[]{:S(2)}) copy-start(bf16[1,256,256]{2,1,0:T(8,128)(2,1)} %param.7) | copy-start | bytes 393220
  36.0 23.8 %copy-start.3 = (s32[1,256]{1,0:T(1,128)S(1)}, s32[1,256]{1,0:T(1,128)}, u32[]{:S(2)}) copy-start(s32[1,256]{1,0:T(1,128)} %param.5) | copy-start | bytes 3076
  57.6 6.2 %collective-permute-start = (bf16[2048,512]{1,0:T(8,128)(2,1)S(1)}, bf16[2048,512]{1,0:T(8,128)(2,1)}, u32[]{:S(2)}, u32[]{:S(2)}) collective-permute-start(bf16[2048,512]{1,0:T(8,128)(2,1)S(1)} %bitcast.84), channel_id=1, source_target_pairs={{0,4},{4,0},{8,12},{12,8},{16,20},{20,16},{24,28},{28,24},{32,36},... | collective-permute-start | bytes 6291464 | tf_op jit(solution)/shard_map/ppermute | solution.py:99
  59.8 2.0 %copy-start = (bf16[2048,256]{1,0:T(8,128)(2,1)S(1)}, bf16[2048,256]{1,0:T(8,128)(2,1)}, u32[]{:S(2)}) copy-start(bf16[2048,256]{1,0:T(8,128)(2,1)} %get-tuple-element.5) | copy-start | bytes 3145732
  65.4 4.2 %collective-permute-start.1 = (bf16[256,256]{1,0:T(8,128)(2,1)S(1)}, bf16[256,256]{1,0:T(8,128)(2,1)S(1)}, u32[]{:S(2)}, u32[]{:S(2)}) collective-permute-start(bf16[256,256]{1,0:T(8,128)(2,1)S(1)} %fusion.8), channel_id=1, source_target_pairs={{0,4},{4,8},{8,12},{12,16},{16,20},{20,24},{24,28},{28,32},{32,36}... | collective-permute-start | bytes 393224 | tf_op jit(solution)/shard_map/ppermute | solution.py:12
  71.7 7.0 %collective-permute-start.2 = (bf16[256,256]{0,1:T(8,128)(2,1)S(1)}, bf16[256,256]{0,1:T(8,128)(2,1)S(1)}, u32[]{:S(2)}, u32[]{:S(2)}) collective-permute-start(bf16[256,256]{0,1:T(8,128)(2,1)S(1)} %pad_maximum_fusion.1), channel_id=1, source_target_pairs={{4,0},{8,4},{12,8},{16,12},{20,16},{24,20},{28,24},{32,28},{36,32}... | collective-permute-start | bytes 393224 | tf_op jit(solution)/shard_map/ppermute | solution.py:12
  74.1 7.8 %collective-permute-start.3 = (bf16[2048,256]{1,0:T(8,128)(2,1)S(1)}, bf16[2048,256]{1,0:T(8,128)(2,1)S(1)}, u32[]{:S(2)}, u32[]{:S(2)}) collective-permute-start(bf16[2048,256]{1,0:T(8,128)(2,1)S(1)} %convolution_convert_fusion.3), channel_id=1, source_target_pairs={{0,4},{4,0},{8,12},{12,8},{16,20},{20,16},{24,28},{28,24},{32,36},... | collective-permute-start | bytes 3145736 | tf_op jit(solution)/shard_map/ppermute | solution.py:99
  79.3 4.6 %collective-permute-start.4 = (bf16[2048,256]{1,0:T(8,128)(2,1)S(1)}, bf16[2048,256]{1,0:T(8,128)(2,1)S(1)}, u32[]{:S(2)}, u32[]{:S(2)}) collective-permute-start(bf16[2048,256]{1,0:T(8,128)(2,1)S(1)} %convolution_convert_fusion.2), channel_id=1, source_target_pairs={{0,4},{4,0},{8,12},{12,8},{16,20},{20,16},{24,28},{28,24},{32,36},... | collective-permute-start | bytes 3145736 | tf_op jit(solution)/shard_map/ppermute | solution.py:99
  85.7 24.0 %all-to-all-start.2 = ((bf16[8,256,512]{2,1,0:T(8,128)(2,1)}), bf16[8,256,512]{2,1,0:T(8,128)(2,1)}, u32[]{:S(2)}, u32[]{:S(2)}) async-start(bf16[8,256,512]{2,1,0:T(8,128)(2,1)} %bitcast.87), calls=%async_computation.2 | async-start | bytes 4194304 | tf_op jit(solution)/shard_map/all_to_all | solution.py:94
  96.3 23.3 %copy-start.1 = (bf16[2048,512]{1,0:T(8,128)(2,1)S(1)}, bf16[2048,512]{1,0:T(8,128)(2,1)}, u32[]{:S(2)}) copy-start(bf16[2048,512]{1,0:T(8,128)(2,1)} %get-tuple-element.8) | copy-start | bytes 6291460
  112.4 22.6 %all-to-all-start.3 = ((bf16[32,8,512]{2,1,0:T(8,128)(2,1)}), bf16[32,8,512]{2,1,0:T(8,128)(2,1)S(1)}, u32[]{:S(2)}, u32[]{:S(2)}) async-start(bf16[32,8,512]{2,1,0:T(8,128)(2,1)} %bitcast.31), calls=%async_computation.3 | async-start | bytes 524288 | tf_op jit(solution)/shard_map/all_to_all | solution.py:94

commit v8 on v7

--- a/solution.py
+++ b/solution.py
@@ -116,17 +116,23 @@
     return split.transpose(4, 1, 3, 6, 0, 2, 5, 7, 8).reshape(2, 256 * rows, tokens)
 
 
-def in_order(first, second):
-    rows, width = first.shape[0] // 256, first.shape[1]
-    both = jnp.stack([first, second]).reshape(2, 2, 2, 2, 4, 4, 2, rows, width)
-    return both.transpose(4, 1, 5, 2, 0, 6, 3, 7, 8).reshape(512 * rows, width)
-
-
-def scatter_total(total):
-    rows, width = total.shape[0] // 256, total.shape[1]
-    total = exchange(total.reshape(8, 32 * rows, width), near_groups())
-    total = jnp.sum(total.astype(jnp.float32), axis=0)
-    total = total.astype(jnp.bfloat16).reshape(32, rows, width)
+def in_order(own, other, core):
+    rows, width = own.shape[0] // 256, own.shape[1]
+    full = jnp.zeros((4, 2, 4, 2, 2, 2, 2, rows, width), own.dtype)
+    for part, place in ((own, core), (other, 1 - core)):
+        part = part.reshape(2, 2, 2, 4, 4, 2, rows, width).transpose(3, 0, 4, 1, 5, 2, 6, 7)
+        full = lax.dynamic_update_slice_in_dim(full, part[:, :, :, :, None], place, 4)
+    return full.reshape(512 * rows, width)
+
+
+def scatter_near(total):
+    rows, width = total.shape[0] // 8, total.shape[1]
+    return exchange(total.reshape(8, rows, width), near_groups())
+
+
+def scatter_far(blocks):
+    total = jnp.sum(blocks.astype(jnp.float32), axis=0).astype(jnp.bfloat16)
+    total = total.reshape(32, total.shape[0] // 32, total.shape[1])
     return jnp.sum(exchange(total, far_groups()).astype(jnp.float32), axis=0)
 
 
@@ -152,11 +158,11 @@
     x_own, x_other = rows_own.T, rows_other.T
     w_own = gather_near(far)
     w_other = swap_cores(w_own)
-    key_value = dot32(x_own, w_own[:, q_width:]) + dot32(x_other, w_other[:, q_width:])
-    key_value = key_value.astype(jnp.bfloat16)
+    projected = dot32(x_own, w_own) + dot32(x_other, w_other)
+    projected = projected.astype(jnp.bfloat16)
+    queries = projected[:, :q_width].reshape(tok_rows, heads, head_dim)
+    key_value = projected[:, q_width:]
     prior = from_behind(key_value, "seq", 1)
-    queries = dot32(x_own, w_own[:, :q_width]) + dot32(x_other, w_other[:, :q_width])
-    queries = queries.astype(jnp.bfloat16).reshape(tok_rows, heads, head_dim)
     key_rows = jnp.concatenate([prior[:, :head_dim], key_value[:, :head_dim]], axis=0)
     value_rows = jnp.concatenate([prior[:, head_dim:], key_value[:, head_dim:]], axis=0)
     key_pos = jnp.concatenate([positions - tok_rows, positions])
@@ -182,10 +188,10 @@
     ]
     own = lax.optimization_barrier(dot32(rows_own, grad_proj).astype(jnp.bfloat16))
     total = own.astype(jnp.float32) + jnp.concatenate(received, axis=1).astype(jnp.float32)
-    weight_grad = scatter_total(total.astype(jnp.bfloat16))
-    full_weights = in_order(
-        jnp.where(core == 0, w_own, w_other), jnp.where(core == 0, w_other, w_own)
-    )
+    blocks = scatter_near(total.astype(jnp.bfloat16))
+    blocks, w_own, w_other = lax.optimization_barrier((blocks, w_own, w_other))
+    weight_grad = scatter_far(blocks)
+    full_weights = in_order(w_own, w_other, core)
     input_grad = lax.dot_general(
         grad_proj, full_weights, (((1,), (1,)), ((), ())), preferred_element_type=jnp.float32
     )

time: 136 us -> 135 us (level)
  blocking collectives: 21.5 us -> 46.9 us
  waiting for transfers between devices: 37.5 us -> 24.1 us
  other arithmetic: 11.5 us -> 2.69 us
  starting transfers between devices: 43 us -> 36.4 us
  local copies, waits for them, and re-layouts: 9.34 us -> 12.7 us
  matrix products: 11.8 us -> 10.4 us
    all_to_all x1 -> x2, blocking collectives: 21.5 us -> 46.9 us  [exchange(): return lax.all_to_all(blocks, AXES, 0, 0, axis_index_groups=groups)]
    all_to_all x3 -> x2, waiting for transfers between devices: 31.4 us -> 16.1 us  [exchange(): return lax.all_to_all(blocks, AXES, 0, 0, axis_index_groups=groups)]
    all_to_all x3 -> x2, starting transfers between devices: 32.8 us -> 26.1 us  [exchange(): return lax.all_to_all(blocks, AXES, 0, 0, axis_index_groups=groups)]
    select_n x1 -> x0, other arithmetic: 3.86 us -> none  [body(): jnp.where(core == 0, w_own, w_other)]
    dynamic_update_slice x0 -> x2, local copies, waits for them, and re-layouts: none -> 2.12 us  [in_order(): lax.dynamic_update_slice_in_dim(full, part[:, :, :, :, None], place, 4)]
    transpose x1 -> x0, other arithmetic: 1.98 us -> none  [in_order(): return both.transpose(4, 1, 5, 2, 0, 6, 3, 7, 8).reshape(512 * rows, width)]
    reduce_sum x2, other arithmetic: 3.31 us -> 1.7 us  [the longest x1 1.04 us: scatter_far(): total = jnp.sum(blocks.astype(jnp.float32), axis=0).astype(jnp.bfloat16)]
    ppermute x2, waiting for transfers between devices: 2.83 us -> 4.43 us  [from_behind(): return lax.ppermute(block, axis, route)]
  transfers between devices with their start and end apart: 8 -> 7, of which waited for: 7 -> 6; matrix products, arithmetic and copies ran while one was open for 16% -> 12% of each run, Pallas kernels for 0% -> 0%
where the time goes in v8:
time: 135 us; the launch traced here: 134 us
  blocking collectives  46.9 us (35%)
  starting transfers between devices  36.4 us (27%)
  waiting for transfers between devices  24.1 us (18%)
  local copies, waits for them, and re-layouts  12.7 us (9%)
  matrix products  10.4 us (8%)
  other arithmetic  2.69 us (2%)
    all_to_all x2, blocking collectives, exchange(): return lax.all_to_all(blocks, AXES, 0, 0, axis_index_groups=groups)  46.9 us
    all_to_all x2, starting transfers between devices, exchange(): return lax.all_to_all(blocks, AXES, 0, 0, axis_index_groups=groups)  26.1 us
    all_to_all x2, waiting for transfers between devices, exchange(): return lax.all_to_all(blocks, AXES, 0, 0, axis_index_groups=groups)  16.1 us
    ppermute x3, starting transfers between devices, swap_cores(): return lax.ppermute(block, 'seq', [(i, i ^ 1) for i in range(count)])  6.08 us
    dot_general x5, matrix products, dot32(): return jnp.dot(a, b, preferred_element_type=jnp.float32)  5.93 us
    unnamed x12, local copies, waits for them, and re-layouts  5.25 us
    ppermute x2, waiting for transfers between devices, from_behind(): return lax.ppermute(block, axis, route)  4.43 us
    ppermute x2, starting transfers between devices, from_behind(): return lax.ppermute(block, axis, route)  4.21 us
  transfers between devices with their start and end apart: 7, of which 6 were waited for; matrix products, arithmetic and copies ran while one was open for 12% of the time, Pallas kernels for 0%

profile of v8, /device:TPU:1, one launch (start us, length us, event | category | flops | bytes accessed | tf_op | source)
XLA Modules:
  0.0 134.1 jit_solution(5949972822469734464)
XLA Ops:
  0.6 1.4 %broadcast_in_dim.36 = bf16[32,8,512]{2,1,0:T(8,128)(2,1)} broadcast(bf16[8,512]{1,0:T(8,128)(2,1)} %param.6), dimensions={1,2} | broadcast | bytes 270336 | tf_op jit(solution)/shard_map/broadcast_in_dim | solution.py:103
  2.0 19.0 %all-to-all-start = ((bf16[32,8,512]{2,1,0:T(8,128)(2,1)}), bf16[32,8,512]{2,1,0:T(8,128)(2,1)S(1)}, u32[]{:S(2)}, u32[]{:S(2)}) async-start(bf16[32,8,512]{2,1,0:T(8,128)(2,1)} %broadcast_in_dim.36), calls=%async_computation | async-start | bytes 524288 | tf_op jit(solution)/shard_map/all_to_all | solution.py:94
  21.0 4.1 %copy.42 = bf16[1,256,4096]{1,2,0:T(8,128)(2,1)} copy(bf16[1,256,4096]{2,1,0:T(8,128)(2,1)} %param.4) | data formatting | bytes 4194304 | tf_op args[0]
  25.1 1.9 %copy.43 = bf16[2,2,2,2,4,4,2,8,256]{8,7,6,5,4,3,2,1,0:T(8,128)(2,1)S(1)} copy(bf16[2,2,2,2,4,4,2,8,256]{8,7,3,6,0,2,5,1,4:T(8,128)(2,1)} %bitcast.93) | data formatting | bytes 4194304 | tf_op jit(solution)/shard_map/transpose | solution.py:116
  27.0 1.1 dynamic-slice_bitcast_fusion
  28.1 7.7 %all-to-all-done = bf16[32,8,512]{2,1,0:T(8,128)(2,1)S(1)} async-done(((bf16[32,8,512]{2,1,0:T(8,128)(2,1)}), bf16[32,8,512]{2,1,0:T(8,128)(2,1)S(1)}, u32[]{:S(2)}, u32[]{:S(2)}) %all-to-all-start) | async-done | bytes 262176 | tf_op jit(solution)/shard_map/all_to_all | solution.py:94
  36.0 21.5 %all_to_all.20 = bf16[8,256,512]{2,1,0:T(8,128)(2,1)S(1)} all-to-all(bf16[8,256,512]{2,1,0:T(8,128)(2,1)S(1)} %broadcast_in_dim.37), channel_id=1, replica_groups={{0,1,8,9,64,65,72,73},{2,3,10,11,66,67,74,75},{16,17,24,25,80,81,88,89}..., dimensions={0} | all-to-all | bytes 4194304 | tf_op jit(solution)/shard_map/all_to_all | solution.py:94
  57.6 2.1 %collective-permute-start = (bf16[2048,512]{1,0:T(8,128)(2,1)S(1)}, bf16[2048,512]{1,0:T(8,128)(2,1)}, u32[]{:S(2)}, u32[]{:S(2)}) collective-permute-start(bf16[2048,512]{1,0:T(8,128)(2,1)S(1)} %bitcast.90), channel_id=1, source_target_pairs={{0,4},{4,0},{8,12},{12,8},{16,20},{20,16},{24,28},{28,24},{32,36},... | collective-permute-start | bytes 6291464 | tf_op jit(solution)/shard_map/ppermute | solution.py:99
  60.0 1.9 %fusion.30 = f32[256,512]{1,0:T(8,128)S(1)} fusion(bf16[2048,256]{1,0:T(8,128)(2,1)} %get-tuple-element.8, bf16[2048,512]{1,0:T(8,128)(2,1)S(1)} %bitcast.91), kind=kOutput, calls=%fused_computation.60 | convolution fusion | flops 536870912 | bytes 3670016 | tf_op jit(solution)/shard_map/dot_general | solution.py:140
  62.0 1.7 %collective-permute-done = bf16[2048,512]{1,0:T(8,128)(2,1)} collective-permute-done((bf16[2048,512]{1,0:T(8,128)(2,1)S(1)}, bf16[2048,512]{1,0:T(8,128)(2,1)}, u32[]{:S(2)}, u32[]{:S(2)}) %collective-permute-start) | collective-permute-done | bytes 2097184 | tf_op jit(solution)/shard_map/ppermute | solution.py:99
  63.7 2.3 %fusion.6 = bf16[256,512]{1,0:T(8,128)(2,1)S(1)} fusion(f32[256,512]{1,0:T(8,128)S(1)} %fusion.30, bf16[2048,256]{1,0:T(8,128)(2,1)S(1)} %get-tuple-element.10, bf16[2048,512]{1,0:T(8,128)(2,1)} %collective-permute-done), kind=kOutput, calls=%fused_computation.16 | convolution fusion | flops 537133056 | bytes 3932160 | tf_op jit(solution)/shard_map/dot_general | solution.py:140
  66.2 2.3 %collective-permute-start.1 = (bf16[256,256]{1,0:T(8,128)(2,1)S(1)}, bf16[256,256]{1,0:T(8,128)(2,1)S(1)}, u32[]{:S(2)}, u32[]{:S(2)}) collective-permute-start(bf16[256,256]{1,0:T(8,128)(2,1)S(1)} %get-tuple-element.20), channel_id=1, source_target_pairs={{0,4},{4,8},{8,12},{12,16},{16,20},{20,24},{24,28},{28,32},{32,36}... | collective-permute-start | bytes 393224 | tf_op jit(solution)/shard_map/ppermute | solution.py:12
  68.5 1.9 %collective-permute-done.1 = bf16[256,256]{1,0:T(8,128)(2,1)S(1)} collective-permute-done((bf16[256,256]{1,0:T(8,128)(2,1)S(1)}, bf16[256,256]{1,0:T(8,128)(2,1)S(1)}, u32[]{:S(2)}, u32[]{:S(2)}) %collective-permute-start.1) | collective-permute-done | bytes 131104 | tf_op jit(solution)/shard_map/ppermute | solution.py:12
  71.2 0.3 fusion.10
  72.5 1.9 %collective-permute-start.2 = (bf16[256,256]{0,1:T(8,128)(2,1)S(1)}, bf16[256,256]{0,1:T(8,128)(2,1)S(1)}, u32[]{:S(2)}, u32[]{:S(2)}) collective-permute-start(bf16[256,256]{0,1:T(8,128)(2,1)S(1)} %pad_maximum_fusion.1), channel_id=1, source_target_pairs={{4,0},{8,4},{12,8},{16,12},{20,16},{24,20},{28,24},{32,28},{36,32}... | collective-permute-start | bytes 393224 | tf_op jit(solution)/shard_map/ppermute | solution.py:12
  74.4 0.5 convolution_convert_fusion.3
  74.9 2.1 %collective-permute-start.3 = (bf16[2048,256]{1,0:T(8,128)(2,1)S(1)}, bf16[2048,256]{1,0:T(8,128)(2,1)S(1)}, u32[]{:S(2)}, u32[]{:S(2)}) collective-permute-start(bf16[2048,256]{1,0:T(8,128)(2,1)S(1)} %convolution_convert_fusion.3), channel_id=1, source_target_pairs={{0,4},{4,0},{8,12},{12,8},{16,20},{20,16},{24,28},{28,24},{32,36},... | collective-permute-start | bytes 3145736 | tf_op jit(solution)/shard_map/ppermute | solution.py:99
  77.0 2.5 %collective-permute-done.2 = bf16[256,256]{0,1:T(8,128)(2,1)S(1)} collective-permute-done((bf16[256,256]{0,1:T(8,128)(2,1)S(1)}, bf16[256,256]{0,1:T(8,128)(2,1)S(1)}, u32[]{:S(2)}, u32[]{:S(2)}) %collective-permute-start.2) | collective-permute-done | bytes 131104 | tf_op jit(solution)/shard_map/ppermute | solution.py:12
  79.6 0.5 convolution_convert_fusion.2
  80.0 1.9 %collective-permute-start.4 = (bf16[2048,256]{1,0:T(8,128)(2,1)S(1)}, bf16[2048,256]{1,0:T(8,128)(2,1)S(1)}, u32[]{:S(2)}, u32[]{:S(2)}) collective-permute-start(bf16[2048,256]{1,0:T(8,128)(2,1)S(1)} %convolution_convert_fusion.2), channel_id=1, source_target_pairs={{0,4},{4,0},{8,12},{12,8},{16,20},{20,16},{24,28},{28,24},{32,36},... | collective-permute-start | bytes 3145736 | tf_op jit(solution)/shard_map/ppermute | solution.py:99
  82.0 0.7 convolution_convert_fusion.1
  82.7 1.9 %collective-permute-done.4 = bf16[2048,256]{1,0:T(8,128)(2,1)S(1)} collective-permute-done((bf16[2048,256]{1,0:T(8,128)(2,1)S(1)}, bf16[2048,256]{1,0:T(8,128)(2,1)S(1)}, u32[]{:S(2)}, u32[]{:S(2)}) %collective-permute-start.4) | collective-permute-done | bytes 1048608 | tf_op jit(solution)/shard_map/ppermute | solution.py:99
  84.6 0.5 add_convert_fusion
  85.1 25.4 %all_to_all.21 = bf16[8,256,512]{2,1,0:T(8,128)(2,1)S(1)} all-to-all(bf16[8,256,512]{2,1,0:T(8,128)(2,1)S(1)} %bitcast.88), channel_id=1, replica_groups={{0,1,8,9,64,65,72,73},{2,3,10,11,66,67,74,75},{16,17,24,25,80,81,88,89}..., dimensions={0} | all-to-all | bytes 4194304 | tf_op jit(solution)/shard_map/all_to_all | solution.py:94
  110.5 1.0 reduce_sum.41
  111.6 7.2 %all-to-all-start.3 = ((bf16[32,8,512]{2,1,0:T(8,128)(2,1)}), bf16[32,8,512]{2,1,0:T(8,128)(2,1)S(1)}, u32[]{:S(2)}, u32[]{:S(2)}) async-start(bf16[32,8,512]{2,1,0:T(8,128)(2,1)} %bitcast.33), calls=%async_computation.3 | async-start | bytes 524288 | tf_op jit(solution)/shard_map/all_to_all | solution.py:94
  118.8 0.5 broadcast_in_dim.40
  119.3 1.1 copy-done.1
  120.6 1.9 %copy_dynamic-update-slice_fusion = bf16[4,2,4,2,2,2,2,8,512]{8,7,6,5,4,3,2,1,0:T(8,128)(2,1)S(1)} fusion(bf16[4,2,4,2,2,2,2,8,512]{8,7,6,5,4,3,2,1,0:T(8,128)(2,1)S(1)} %copy_dynamic-update-slice_fusion.1, s32[]{:T(128)S(6)} %select_n.14, bf16[4,2,4,2,1,2,2,8,512]{8,7,5,2,0,6,3,1,4:T(8,128)(2,1)} %bitcast.30), kind=kLoop, calls=%fused_computation.6 | loop fusion | bytes 4194308 | tf_op jit(solution)/shard_map/dynamic_update_slice | solution.py:124
  122.5 2.6 %fusion = bf16[1,256,4096]{2,1,0:T(8,128)(2,1)} fusion(bf16[4096,512]{1,0:T(8,128)(2,1)S(1)} %bitcast.87, bf16[256,128]{0,1:T(8,128)(2,1)S(1)} %get-tuple-element.17, bf16[256,128]{0,1:T(8,128)(2,1)S(1)} %get-tuple-element.16, bf16[256,256]{0,1:T(8,128)(2,1)S(1)} %bitcast.99), kind=kOutput, calls=%fused_computation.1 | convolution fusion | flops 1075576832 | bytes 6553600 | tf_op jit(solution)/shard_map/dot_general | solution.py:195
  125.1 8.3 %all-to-all-done.3 = bf16[32,8,512]{2,1,0:T(8,128)(2,1)S(1)} async-done(((bf16[32,8,512]{2,1,0:T(8,128)(2,1)}), bf16[32,8,512]{2,1,0:T(8,128)(2,1)S(1)}, u32[]{:S(2)}, u32[]{:S(2)}) %all-to-all-start.3) | async-done | bytes 262176 | tf_op jit(solution)/shard_map/all_to_all | solution.py:94
  133.5 0.7 convert_reduce_fusion
  (32 shorter events, 2.7 us)
Async XLA Ops:
  2.0 33.8 %all-to-all-start = ((bf16[32,8,512]{2,1,0:T(8,128)(2,1)}), bf16[32,8,512]{2,1,0:T(8,128)(2,1)S(1)}, u32[]{:S(2)}, u32[]{:S(2)}) async-start(bf16[32,8,512]{2,1,0:T(8,128)(2,1)} %broadcast_in_dim.36), calls=%async_computation | async-start | bytes 524288 | tf_op jit(solution)/shard_map/all_to_all | solution.py:94
  36.0 23.7 %copy-start.3 = (bf16[1,256,256]{2,1,0:T(8,128)(2,1)S(1)}, bf16[1,256,256]{2,1,0:T(8,128)(2,1)}, u32[]{:S(2)}) copy-start(bf16[1,256,256]{2,1,0:T(8,128)(2,1)} %param.7) | copy-start | bytes 393220
  36.0 23.8 %copy-start.4 = (s32[1,256]{1,0:T(1,128)S(1)}, s32[1,256]{1,0:T(1,128)}, u32[]{:S(2)}) copy-start(s32[1,256]{1,0:T(1,128)} %param.5) | copy-start | bytes 3076
  57.6 4.4 %copy-start = (bf16[8,256,512]{2,1,0:T(8,128)(2,1)}, bf16[8,256,512]{2,1,0:T(8,128)(2,1)S(1)}, u32[]{:S(2)}) copy-start(bf16[8,256,512]{2,1,0:T(8,128)(2,1)S(1)} %all_to_all.20) | copy-start | bytes 6291460
  57.6 6.2 %collective-permute-start = (bf16[2048,512]{1,0:T(8,128)(2,1)S(1)}, bf16[2048,512]{1,0:T(8,128)(2,1)}, u32[]{:S(2)}, u32[]{:S(2)}) collective-permute-start(bf16[2048,512]{1,0:T(8,128)(2,1)S(1)} %bitcast.90), channel_id=1, source_target_pairs={{0,4},{4,0},{8,12},{12,8},{16,20},{20,16},{24,28},{28,24},{32,36},... | collective-permute-start | bytes 6291464 | tf_op jit(solution)/shard_map/ppermute | solution.py:99
  66.2 4.2 %collective-permute-start.1 = (bf16[256,256]{1,0:T(8,128)(2,1)S(1)}, bf16[256,256]{1,0:T(8,128)(2,1)S(1)}, u32[]{:S(2)}, u32[]{:S(2)}) collective-permute-start(bf16[256,256]{1,0:T(8,128)(2,1)S(1)} %get-tuple-element.20), channel_id=1, source_target_pairs={{0,4},{4,8},{8,12},{12,16},{16,20},{20,24},{24,28},{28,32},{32,36}... | collective-permute-start | bytes 393224 | tf_op jit(solution)/shard_map/ppermute | solution.py:12
  72.5 7.0 %collective-permute-start.2 = (bf16[256,256]{0,1:T(8,128)(2,1)S(1)}, bf16[256,256]{0,1:T(8,128)(2,1)S(1)}, u32[]{:S(2)}, u32[]{:S(2)}) collective-permute-start(bf16[256,256]{0,1:T(8,128)(2,1)S(1)} %pad_maximum_fusion.1), channel_id=1, source_target_pairs={{4,0},{8,4},{12,8},{16,12},{20,16},{24,20},{28,24},{32,28},{36,32}... | collective-permute-start | bytes 393224 | tf_op jit(solution)/shard_map/ppermute | solution.py:12
  74.9 7.1 %copy-start.2 = (bf16[2048,256]{1,0:T(8,128)(2,1)S(1)}, bf16[2048,256]{1,0:T(8,128)(2,1)}, u32[]{:S(2)}) copy-start(bf16[2048,256]{1,0:T(8,128)(2,1)} %get-tuple-element.8) | copy-start | bytes 3145732
  74.9 7.8 %collective-permute-start.3 = (bf16[2048,256]{1,0:T(8,128)(2,1)S(1)}, bf16[2048,256]{1,0:T(8,128)(2,1)S(1)}, u32[]{:S(2)}, u32[]{:S(2)}) collective-permute-start(bf16[2048,256]{1,0:T(8,128)(2,1)S(1)} %convolution_convert_fusion.3), channel_id=1, source_target_pairs={{0,4},{4,0},{8,12},{12,8},{16,20},{20,16},{24,28},{28,24},{32,36},... | collective-permute-start | bytes 3145736 | tf_op jit(solution)/shard_map/ppermute | solution.py:99
  80.0 4.6 %collective-permute-start.4 = (bf16[2048,256]{1,0:T(8,128)(2,1)S(1)}, bf16[2048,256]{1,0:T(8,128)(2,1)S(1)}, u32[]{:S(2)}, u32[]{:S(2)}) collective-permute-start(bf16[2048,256]{1,0:T(8,128)(2,1)S(1)} %convolution_convert_fusion.2), channel_id=1, source_target_pairs={{0,4},{4,0},{8,12},{12,8},{16,20},{20,16},{24,28},{28,24},{32,36},... | collective-permute-start | bytes 3145736 | tf_op jit(solution)/shard_map/ppermute | solution.py:99
  111.6 21.9 %all-to-all-start.3 = ((bf16[32,8,512]{2,1,0:T(8,128)(2,1)}), bf16[32,8,512]{2,1,0:T(8,128)(2,1)S(1)}, u32[]{:S(2)}, u32[]{:S(2)}) async-start(bf16[32,8,512]{2,1,0:T(8,128)(2,1)} %bitcast.33), calls=%async_computation.3 | async-start | bytes 524288 | tf_op jit(solution)/shard_map/all_to_all | solution.py:94
  118.8 1.6 %copy-start.1 = (bf16[8,256,512]{2,1,0:T(8,128)(2,1)S(1)}, bf16[8,256,512]{2,1,0:T(8,128)(2,1)}, u32[]{:S(2)}) copy-start(bf16[8,256,512]{2,1,0:T(8,128)(2,1)} %copy-done) | copy-start | bytes 6291460

commit v9 on v8

--- a/solution.py
+++ b/solution.py
@@ -162,7 +162,9 @@
     projected = projected.astype(jnp.bfloat16)
     queries = projected[:, :q_width].reshape(tok_rows, heads, head_dim)
     key_value = projected[:, q_width:]
-    prior = from_behind(key_value, "seq", 1)
+    prior, full_weights = lax.optimization_barrier(
+        (from_behind(key_value, "seq", 1), in_order(w_own, w_other, core))
+    )
     key_rows = jnp.concatenate([prior[:, :head_dim], key_value[:, :head_dim]], axis=0)
     value_rows = jnp.concatenate([prior[:, head_dim:], key_value[:, head_dim:]], axis=0)
     key_pos = jnp.concatenate([positions - tok_rows, positions])
@@ -189,9 +191,8 @@
     own = lax.optimization_barrier(dot32(rows_own, grad_proj).astype(jnp.bfloat16))
     total = own.astype(jnp.float32) + jnp.concatenate(received, axis=1).astype(jnp.float32)
     blocks = scatter_near(total.astype(jnp.bfloat16))
-    blocks, w_own, w_other = lax.optimization_barrier((blocks, w_own, w_other))
+    blocks, full_weights = lax.optimization_barrier((blocks, full_weights))
     weight_grad = scatter_far(blocks)
-    full_weights = in_order(w_own, w_other, core)
     input_grad = lax.dot_general(
         grad_proj, full_weights, (((1,), (1,)), ((), ())), preferred_element_type=jnp.float32
     )

time: 135 us -> 136 us (level)
  matrix products: 10.4 us -> 13.1 us
  waiting for transfers between devices: 24.1 us -> 21.9 us
    ppermute x2, waiting for transfers between devices: 4.43 us -> 1.48 us  [from_behind(): return lax.ppermute(block, axis, route)]
    dot_general x1, matrix products: 2.64 us -> 4.82 us  [body(): lax.dot_general(grad_proj, full_weights, (((1,), (1,)), ((), ())), prefer...]
    all_to_all x2, waiting for transfers between devices: 16.1 us -> 17.7 us  [exchange(): return lax.all_to_all(blocks, AXES, 0, 0, axis_index_groups=groups)]
    dynamic_update_slice x2, local copies, waits for them, and re-layouts: 2.12 us -> 3.52 us  [in_order(): lax.dynamic_update_slice_in_dim(full, part[:, :, :, :, None], place, 4)]
    unnamed x12 -> x10, local copies, waits for them, and re-layouts: 5.25 us -> 4.2 us
  transfers between devices with their start and end apart: 7 -> 7, of which waited for: 6 -> 5; matrix products, arithmetic and copies ran while one was open for 12% -> 15% of each run, Pallas kernels for 0% -> 0%
where the time goes in v9:
time: 136 us
  blocking collectives  47.3 us (35%)
  starting transfers between devices  36.6 us (27%)
  waiting for transfers between devices  21.9 us (16%)
  matrix products  13.1 us (10%)
  local copies, waits for them, and re-layouts  13 us (10%)
  other arithmetic  2.69 us (2%)
    all_to_all x2, blocking collectives, exchange(): return lax.all_to_all(blocks, AXES, 0, 0, axis_index_groups=groups)  47.3 us
    all_to_all x2, starting transfers between devices, exchange(): return lax.all_to_all(blocks, AXES, 0, 0, axis_index_groups=groups)  26.2 us
    all_to_all x2, waiting for transfers between devices, exchange(): return lax.all_to_all(blocks, AXES, 0, 0, axis_index_groups=groups)  17.7 us
    dot_general x5, matrix products, dot32(): return jnp.dot(a, b, preferred_element_type=jnp.float32)  6.46 us
    ppermute x3, starting transfers between devices, swap_cores(): return lax.ppermute(block, 'seq', [(i, i ^ 1) for i in range(count)])  6.08 us
    dot_general x1, matrix products, body(): lax.dot_general(grad_proj, full_weights, (((1,), (1,)), ((), ())), prefer...  4.82 us
    ppermute x2, starting transfers between devices, from_behind(): return lax.ppermute(block, axis, route)  4.32 us
    unnamed x10, local copies, waits for them, and re-layouts  4.2 us
  transfers between devices with their start and end apart: 7, of which 5 were waited for; matrix products, arithmetic and copies ran while one was open for 15% of the time, Pallas kernels for 0%

profile of v9, /device:TPU:1, one launch (start us, length us, event | category | flops | bytes accessed | tf_op | source)
XLA Modules:
  0.0 135.5 jit_solution(14929358774450524132)
XLA Ops:
  0.6 1.4 %broadcast_in_dim.36 = bf16[32,8,512]{2,1,0:T(8,128)(2,1)} broadcast(bf16[8,512]{1,0:T(8,128)(2,1)} %param.6), dimensions={1,2} | broadcast | bytes 270336 | tf_op jit(solution)/shard_map/broadcast_in_dim | solution.py:103
  2.0 19.0 %all-to-all-start = ((bf16[32,8,512]{2,1,0:T(8,128)(2,1)}), bf16[32,8,512]{2,1,0:T(8,128)(2,1)S(1)}, u32[]{:S(2)}, u32[]{:S(2)}) async-start(bf16[32,8,512]{2,1,0:T(8,128)(2,1)} %broadcast_in_dim.36), calls=%async_computation | async-start | bytes 524288 | tf_op jit(solution)/shard_map/all_to_all | solution.py:94
  21.0 4.1 %copy.42 = bf16[1,256,4096]{1,2,0:T(8,128)(2,1)} copy(bf16[1,256,4096]{2,1,0:T(8,128)(2,1)} %param.4) | data formatting | bytes 4194304 | tf_op args[0]
  25.1 1.9 %copy.43 = bf16[2,2,2,2,4,4,2,8,256]{8,7,6,5,4,3,2,1,0:T(8,128)(2,1)S(1)} copy(bf16[2,2,2,2,4,4,2,8,256]{8,7,3,6,0,2,5,1,4:T(8,128)(2,1)} %bitcast.93) | data formatting | bytes 4194304 | tf_op jit(solution)/shard_map/transpose | solution.py:116
  27.0 1.1 dynamic-slice_bitcast_fusion
  28.1 7.8 %all-to-all-done = bf16[32,8,512]{2,1,0:T(8,128)(2,1)S(1)} async-done(((bf16[32,8,512]{2,1,0:T(8,128)(2,1)}), bf16[32,8,512]{2,1,0:T(8,128)(2,1)S(1)}, u32[]{:S(2)}, u32[]{:S(2)}) %all-to-all-start) | async-done | bytes 262176 | tf_op jit(solution)/shard_map/all_to_all | solution.py:94
  36.0 21.5 %all_to_all.20 = bf16[8,256,512]{2,1,0:T(8,128)(2,1)S(1)} all-to-all(bf16[8,256,512]{2,1,0:T(8,128)(2,1)S(1)} %broadcast_in_dim.37), channel_id=1, replica_groups={{0,1,8,9,64,65,72,73},{2,3,10,11,66,67,74,75},{16,17,24,25,80,81,88,89}..., dimensions={0} | all-to-all | bytes 4194304 | tf_op jit(solution)/shard_map/all_to_all | solution.py:94
  57.6 2.1 %collective-permute-start = (bf16[2048,512]{1,0:T(8,128)(2,1)S(1)}, bf16[2048,512]{1,0:T(8,128)(2,1)}, u32[]{:S(2)}, u32[]{:S(2)}) collective-permute-start(bf16[2048,512]{1,0:T(8,128)(2,1)S(1)} %bitcast.90), channel_id=1, source_target_pairs={{0,4},{4,0},{8,12},{12,8},{16,20},{20,16},{24,28},{28,24},{32,36},... | collective-permute-start | bytes 6291464 | tf_op jit(solution)/shard_map/ppermute | solution.py:99
  60.0 1.9 %fusion.30 = f32[256,512]{1,0:T(8,128)S(1)} fusion(bf16[2048,256]{1,0:T(8,128)(2,1)} %get-tuple-element.9, bf16[2048,512]{1,0:T(8,128)(2,1)S(1)} %bitcast.91), kind=kOutput, calls=%fused_computation.60 | convolution fusion | flops 536870912 | bytes 3670016 | tf_op jit(solution)/shard_map/dot_general | solution.py:140
  62.0 0.5 broadcast_in_dim.38
  62.8 0.9 collective-permute-done
  63.7 2.8 %fusion.6 = bf16[256,512]{1,0:T(8,128)(2,1)S(1)} fusion(f32[256,512]{1,0:T(8,128)S(1)} %fusion.30, bf16[2048,256]{1,0:T(8,128)(2,1)S(1)} %get-tuple-element.11, bf16[2048,512]{1,0:T(8,128)(2,1)} %collective-permute-done), kind=kOutput, calls=%fused_computation.16 | convolution fusion | flops 537133056 | bytes 3932160 | tf_op jit(solution)/shard_map/dot_general | solution.py:140
  66.6 2.1 %collective-permute-start.1 = (bf16[256,256]{1,0:T(8,128)(2,1)S(1)}, bf16[256,256]{1,0:T(8,128)(2,1)S(1)}, u32[]{:S(2)}, u32[]{:S(2)}) collective-permute-start(bf16[256,256]{1,0:T(8,128)(2,1)S(1)} %get-tuple-element.22), channel_id=1, source_target_pairs={{0,4},{4,8},{8,12},{12,16},{16,20},{20,24},{24,28},{28,32},{32,36}... | collective-permute-start | bytes 393224 | tf_op jit(solution)/shard_map/ppermute | solution.py:12
  68.8 3.2 %copy_dynamic-update-slice_fusion = bf16[4,2,4,2,2,2,2,8,512]{8,7,6,5,4,3,2,1,0:T(8,128)(2,1)} fusion(bf16[4,2,4,2,2,2,2,8,512]{8,7,6,5,4,3,2,1,0:T(8,128)(2,1)} %copy-done, s32[]{:T(128)S(6)} %select_n.14, bf16[4,2,4,2,1,2,2,8,512]{8,7,5,2,0,6,3,1,4:T(8,128)(2,1)} %bitcast.14), kind=kLoop, calls=%fused_computation.6 | loop fusion | bytes 4194308 | tf_op jit(solution)/shard_map/dynamic_update_slice | solution.py:124
  72.6 0.3 fusion.10
  73.5 0.3 fusion.7
  73.8 0.3 convolution_bitcast_fusion.1
  74.2 2.3 %collective-permute-start.2 = (bf16[256,256]{0,1:T(8,128)(2,1)S(1)}, bf16[256,256]{0,1:T(8,128)(2,1)S(1)}, u32[]{:S(2)}, u32[]{:S(2)}) collective-permute-start(bf16[256,256]{0,1:T(8,128)(2,1)S(1)} %pad_maximum_fusion.1), channel_id=1, source_target_pairs={{4,0},{8,4},{12,8},{16,12},{20,16},{24,20},{28,24},{32,28},{36,32}... | collective-permute-start | bytes 393224 | tf_op jit(solution)/shard_map/ppermute | solution.py:12
  76.4 0.5 convolution_convert_fusion.3
  76.9 2.1 %collective-permute-start.3 = (bf16[2048,256]{1,0:T(8,128)(2,1)S(1)}, bf16[2048,256]{1,0:T(8,128)(2,1)S(1)}, u32[]{:S(2)}, u32[]{:S(2)}) collective-permute-start(bf16[2048,256]{1,0:T(8,128)(2,1)S(1)} %convolution_convert_fusion.3), channel_id=1, source_target_pairs={{0,4},{4,0},{8,12},{12,8},{16,20},{20,16},{24,28},{28,24},{32,36},... | collective-permute-start | bytes 3145736 | tf_op jit(solution)/shard_map/ppermute | solution.py:99
  79.0 1.5 %collective-permute-done.2 = bf16[256,256]{0,1:T(8,128)(2,1)S(1)} collective-permute-done((bf16[256,256]{0,1:T(8,128)(2,1)S(1)}, bf16[256,256]{0,1:T(8,128)(2,1)S(1)}, u32[]{:S(2)}, u32[]{:S(2)}) %collective-permute-start.2) | collective-permute-done | bytes 131104 | tf_op jit(solution)/shard_map/ppermute | solution.py:12
  80.5 0.5 convolution_convert_fusion.2
  81.0 1.9 %collective-permute-start.4 = (bf16[2048,256]{1,0:T(8,128)(2,1)S(1)}, bf16[2048,256]{1,0:T(8,128)(2,1)S(1)}, u32[]{:S(2)}, u32[]{:S(2)}) collective-permute-start(bf16[2048,256]{1,0:T(8,128)(2,1)S(1)} %convolution_convert_fusion.2), channel_id=1, source_target_pairs={{0,4},{4,0},{8,12},{12,8},{16,20},{20,16},{24,28},{28,24},{32,36},... | collective-permute-start | bytes 3145736 | tf_op jit(solution)/shard_map/ppermute | solution.py:99
  82.9 0.7 convolution_convert_fusion.1
  83.7 1.9 %collective-permute-done.4 = bf16[2048,256]{1,0:T(8,128)(2,1)S(1)} collective-permute-done((bf16[2048,256]{1,0:T(8,128)(2,1)S(1)}, bf16[2048,256]{1,0:T(8,128)(2,1)S(1)}, u32[]{:S(2)}, u32[]{:S(2)}) %collective-permute-start.4) | collective-permute-done | bytes 1048608 | tf_op jit(solution)/shard_map/ppermute | solution.py:99
  85.5 0.5 add_convert_fusion
  86.1 25.8 %all_to_all.21 = bf16[8,256,512]{2,1,0:T(8,128)(2,1)S(1)} all-to-all(bf16[8,256,512]{2,1,0:T(8,128)(2,1)S(1)} %bitcast.88), channel_id=1, replica_groups={{0,1,8,9,64,65,72,73},{2,3,10,11,66,67,74,75},{16,17,24,25,80,81,88,89}..., dimensions={0} | all-to-all | bytes 4194304 | tf_op jit(solution)/shard_map/all_to_all | solution.py:94
  111.8 1.0 reduce_sum.41
  112.9 7.2 %all-to-all-start.3 = ((bf16[32,8,512]{2,1,0:T(8,128)(2,1)}), bf16[32,8,512]{2,1,0:T(8,128)(2,1)S(1)}, u32[]{:S(2)}, u32[]{:S(2)}) async-start(bf16[32,8,512]{2,1,0:T(8,128)(2,1)} %bitcast.33), calls=%async_computation.3 | async-start | bytes 524288 | tf_op jit(solution)/shard_map/all_to_all | solution.py:94
  120.1 4.8 %fusion = bf16[1,256,4096]{2,1,0:T(8,128)(2,1)} fusion(bf16[4096,512]{1,0:T(8,128)(2,1)} %bitcast.87, bf16[256,128]{0,1:T(8,128)(2,1)S(1)} %get-tuple-element.19, bf16[256,128]{0,1:T(8,128)(2,1)S(1)} %get-tuple-element.18, bf16[256,256]{0,1:T(8,128)(2,1)S(1)} %bitcast.99), kind=kOutput, calls=%fused_computation.1 | convolution fusion | flops 1075576832 | bytes 6553600 | tf_op jit(solution)/shard_map/dot_general | solution.py:196
  124.9 9.9 %all-to-all-done.3 = bf16[32,8,512]{2,1,0:T(8,128)(2,1)S(1)} async-done(((bf16[32,8,512]{2,1,0:T(8,128)(2,1)}), bf16[32,8,512]{2,1,0:T(8,128)(2,1)S(1)}, u32[]{:S(2)}, u32[]{:S(2)}) %all-to-all-start.3) | async-done | bytes 262176 | tf_op jit(solution)/shard_map/all_to_all | solution.py:94
  134.8 0.7 convert_reduce_fusion
  (30 shorter events, 2.1 us)
Async XLA Ops:
  2.0 33.8 %all-to-all-start = ((bf16[32,8,512]{2,1,0:T(8,128)(2,1)}), bf16[32,8,512]{2,1,0:T(8,128)(2,1)S(1)}, u32[]{:S(2)}, u32[]{:S(2)}) async-start(bf16[32,8,512]{2,1,0:T(8,128)(2,1)} %broadcast_in_dim.36), calls=%async_computation | async-start | bytes 524288 | tf_op jit(solution)/shard_map/all_to_all | solution.py:94
  36.0 23.7 %copy-start.2 = (bf16[1,256,256]{2,1,0:T(8,128)(2,1)S(1)}, bf16[1,256,256]{2,1,0:T(8,128)(2,1)}, u32[]{:S(2)}) copy-start(bf16[1,256,256]{2,1,0:T(8,128)(2,1)} %param.7) | copy-start | bytes 393220
  36.0 23.8 %copy-start.3 = (s32[1,256]{1,0:T(1,128)S(1)}, s32[1,256]{1,0:T(1,128)}, u32[]{:S(2)}) copy-start(s32[1,256]{1,0:T(1,128)} %param.5) | copy-start | bytes 3076
  57.6 6.2 %collective-permute-start = (bf16[2048,512]{1,0:T(8,128)(2,1)S(1)}, bf16[2048,512]{1,0:T(8,128)(2,1)}, u32[]{:S(2)}, u32[]{:S(2)}) collective-permute-start(bf16[2048,512]{1,0:T(8,128)(2,1)S(1)} %bitcast.90), channel_id=1, source_target_pairs={{0,4},{4,0},{8,12},{12,8},{16,20},{20,16},{24,28},{28,24},{32,36},... | collective-permute-start | bytes 6291464 | tf_op jit(solution)/shard_map/ppermute | solution.py:99
  62.8 3.8 %copy-start = (bf16[4,2,4,2,2,2,2,8,512]{8,7,6,5,4,3,2,1,0:T(8,128)(2,1)}, bf16[4,2,4,2,2,2,2,8,512]{8,7,6,5,4,3,2,1,0:T(8,128)(2,1)S(1)}, u32[]{:S(2)}) copy-start(bf16[4,2,4,2,2,2,2,8,512]{8,7,6,5,4,3,2,1,0:T(8,128)(2,1)S(1)} %copy_dynamic-update-slice_fusion.1) | copy-start | bytes 12582916
  66.6 5.4 %collective-permute-start.1 = (bf16[256,256]{1,0:T(8,128)(2,1)S(1)}, bf16[256,256]{1,0:T(8,128)(2,1)S(1)}, u32[]{:S(2)}, u32[]{:S(2)}) collective-permute-start(bf16[256,256]{1,0:T(8,128)(2,1)S(1)} %get-tuple-element.22), channel_id=1, source_target_pairs={{0,4},{4,8},{8,12},{12,16},{16,20},{20,24},{24,28},{28,32},{32,36}... | collective-permute-start | bytes 393224 | tf_op jit(solution)/shard_map/ppermute | solution.py:12
  74.2 6.3 %collective-permute-start.2 = (bf16[256,256]{0,1:T(8,128)(2,1)S(1)}, bf16[256,256]{0,1:T(8,128)(2,1)S(1)}, u32[]{:S(2)}, u32[]{:S(2)}) collective-permute-start(bf16[256,256]{0,1:T(8,128)(2,1)S(1)} %pad_maximum_fusion.1), channel_id=1, source_target_pairs={{4,0},{8,4},{12,8},{16,12},{20,16},{24,20},{28,24},{32,28},{36,32}... | collective-permute-start | bytes 393224 | tf_op jit(solution)/shard_map/ppermute | solution.py:12
  76.9 6.0 %copy-start.1 = (bf16[2048,256]{1,0:T(8,128)(2,1)S(1)}, bf16[2048,256]{1,0:T(8,128)(2,1)}, u32[]{:S(2)}) copy-start(bf16[2048,256]{1,0:T(8,128)(2,1)} %get-tuple-element.9) | copy-start | bytes 3145732
  76.9 6.8 %collective-permute-start.3 = (bf16[2048,256]{1,0:T(8,128)(2,1)S(1)}, bf16[2048,256]{1,0:T(8,128)(2,1)S(1)}, u32[]{:S(2)}, u32[]{:S(2)}) collective-permute-start(bf16[2048,256]{1,0:T(8,128)(2,1)S(1)} %convolution_convert_fusion.3), channel_id=1, source_target_pairs={{0,4},{4,0},{8,12},{12,8},{16,20},{20,16},{24,28},{28,24},{32,36},... | collective-permute-start | bytes 3145736 | tf_op jit(solution)/shard_map/ppermute | solution.py:99
  81.0 4.6 %collective-permute-start.4 = (bf16[2048,256]{1,0:T(8,128)(2,1)S(1)}, bf16[2048,256]{1,0:T(8,128)(2,1)S(1)}, u32[]{:S(2)}, u32[]{:S(2)}) collective-permute-start(bf16[2048,256]{1,0:T(8,128)(2,1)S(1)} %convolution_convert_fusion.2), channel_id=1, source_target_pairs={{0,4},{4,0},{8,12},{12,8},{16,20},{20,16},{24,28},{28,24},{32,36},... | collective-permute-start | bytes 3145736 | tf_op jit(solution)/shard_map/ppermute | solution.py:99
  112.9 22.0 %all-to-all-start.3 = ((bf16[32,8,512]{2,1,0:T(8,128)(2,1)}), bf16[32,8,512]{2,1,0:T(8,128)(2,1)S(1)}, u32[]{:S(2)}, u32[]{:S(2)}) async-start(bf16[32,8,512]{2,1,0:T(8,128)(2,1)} %bitcast.33), calls=%async_computation.3 | async-start | bytes 524288 | tf_op jit(solution)/shard_map/all_to_all | solution.py:94

commit v10 on v8

--- a/solution.py
+++ b/solution.py
@@ -1,6 +1,8 @@
 import jax
 import jax.numpy as jnp
 from jax import lax
+from jax.experimental import pallas as pl
+from jax.experimental.pallas import tpu as pltpu
 from jax.sharding import PartitionSpec as P
 
 WIN = 256
@@ -140,6 +142,49 @@
     return jnp.dot(a, b, preferred_element_type=jnp.float32)
 
 
+def add_product_kernel(start_ref, rows_ref, weights_ref, out_ref, sum_ref):
+    step = pl.program_id(0)
+
+    @pl.when(step == 0)
+    def _():
+        sum_ref[...] = start_ref[...]
+
+    sum_ref[...] += lax.dot_general(
+        rows_ref[...],
+        weights_ref[...],
+        (((0,), (0,)), ((), ())),
+        preferred_element_type=jnp.float32,
+    )
+
+    @pl.when(step == pl.num_programs(0) - 1)
+    def _():
+        out_ref[...] = sum_ref[...].astype(out_ref.dtype)
+
+
+def add_product(start, rows, weights):
+    depth, tokens = rows.shape
+    width = weights.shape[1]
+    chunk = depth // 4
+    whole = pl.BlockSpec((tokens, width), lambda i: (0, 0))
+    return pl.pallas_call(
+        add_product_kernel,
+        out_shape=jax.ShapeDtypeStruct((tokens, width), jnp.bfloat16),
+        grid=(depth // chunk,),
+        in_specs=[
+            whole,
+            pl.BlockSpec((chunk, tokens), lambda i: (i, 0)),
+            pl.BlockSpec((chunk, width), lambda i: (i, 0)),
+        ],
+        out_specs=whole,
+        scratch_shapes=[pltpu.VMEM((tokens, width), jnp.float32)],
+        cost_estimate=pl.CostEstimate(
+            flops=2 * depth * tokens * width,
+            bytes_accessed=2 * depth * (tokens + width) + 6 * tokens * width,
+            transcendentals=0,
+        ),
+    )(start, rows, weights)
+
+
 def body(layer_inputs, doc_start, w_qkv, d_context):
     x_local = layer_inputs[0]
     tok_rows = x_local.shape[0]
@@ -155,11 +200,9 @@
     rows_other = lax.dynamic_index_in_dim(x_rows, 1 - core, 0, keepdims=False)
     far = gather_far(w_qkv)
     rows_own, rows_other, far = lax.optimization_barrier((rows_own, rows_other, far))
-    x_own, x_other = rows_own.T, rows_other.T
     w_own = gather_near(far)
     w_other = swap_cores(w_own)
-    projected = dot32(x_own, w_own) + dot32(x_other, w_other)
-    projected = projected.astype(jnp.bfloat16)
+    projected = add_product(dot32(rows_own.T, w_own), rows_other, w_other)
     queries = projected[:, :q_width].reshape(tok_rows, heads, head_dim)
     key_value = projected[:, q_width:]
     prior = from_behind(key_value, "seq", 1)

time: 135 us -> 138 us (1.022)
  Pallas kernels: 0 us -> 4.23 us
  matrix products: 10.4 us -> 7.61 us
  local copies, waits for them, and re-layouts: 12.7 us -> 14.5 us
    pallas_call x0 -> x1, Pallas kernels: none -> 4.23 us  [add_product(): pl.pallas_call(add_product_kernel, out_shape=jax.ShapeDtypeStruct((tokens...]
    dot_general x5 -> x4, matrix products: 5.93 us -> 3.19 us  [dot32(): return jnp.dot(a, b, preferred_element_type=jnp.float32)]
where the time goes in v10:
time: 138 us; the launch traced here: 137 us
  blocking collectives  46.9 us (34%)
  starting transfers between devices  36.3 us (26%)
  waiting for transfers between devices  23.8 us (17%)
  local copies, waits for them, and re-layouts  14.5 us (11%)
  matrix products  7.61 us (6%)
  Pallas kernels  4.23 us (3%)
  other arithmetic  2.68 us (2%)
    all_to_all x2, blocking collectives, exchange(): return lax.all_to_all(blocks, AXES, 0, 0, axis_index_groups=groups)  46.9 us
    all_to_all x2, starting transfers between devices, exchange(): return lax.all_to_all(blocks, AXES, 0, 0, axis_index_groups=groups)  26.1 us
    all_to_all x2, waiting for transfers between devices, exchange(): return lax.all_to_all(blocks, AXES, 0, 0, axis_index_groups=groups)  16.1 us
    ppermute x3, starting transfers between devices, swap_cores(): return lax.ppermute(block, 'seq', [(i, i ^ 1) for i in range(count)])  5.95 us
    unnamed x12, local copies, waits for them, and re-layouts  5.25 us
    pallas_call x1, Pallas kernels, add_product(): pl.pallas_call(add_product_kernel, out_shape=jax.ShapeDtypeStruct((tokens...  4.23 us
    ppermute x2, starting transfers between devices, from_behind(): return lax.ppermute(block, axis, route)  4.21 us
    ppermute x3, waiting for transfers between devices, swap_cores(): return lax.ppermute(block, 'seq', [(i, i ^ 1) for i in range(count)])  4.04 us
  transfers between devices with their start and end apart: 7, of which 6 were waited for; matrix products, arithmetic and copies ran while one was open for 12% of the time, Pallas kernels for 0%

profile of v10, /device:TPU:1, one launch (start us, length us, event | category | flops | bytes accessed | tf_op | source)
XLA Modules:
  0.0 137.0 jit_solution(17085211740429841903)
XLA Ops:
  0.6 1.4 %broadcast_in_dim.36 = bf16[32,8,512]{2,1,0:T(8,128)(2,1)} broadcast(bf16[8,512]{1,0:T(8,128)(2,1)} %param.6), dimensions={1,2} | broadcast | bytes 270336 | tf_op jit(solution)/shard_map/broadcast_in_dim | solution.py:105
  2.0 19.0 %all-to-all-start = ((bf16[32,8,512]{2,1,0:T(8,128)(2,1)}), bf16[32,8,512]{2,1,0:T(8,128)(2,1)S(1)}, u32[]{:S(2)}, u32[]{:S(2)}) async-start(bf16[32,8,512]{2,1,0:T(8,128)(2,1)} %broadcast_in_dim.36), calls=%async_computation | async-start | bytes 524288 | tf_op jit(solution)/shard_map/all_to_all | solution.py:96
  21.0 4.1 %copy.44 = bf16[1,256,4096]{1,2,0:T(8,128)(2,1)} copy(bf16[1,256,4096]{2,1,0:T(8,128)(2,1)} %param.4) | data formatting | bytes 4194304 | tf_op args[0]
  25.1 1.9 %copy.45 = bf16[2,2,2,2,4,4,2,8,256]{8,7,6,5,4,3,2,1,0:T(8,128)(2,1)S(1)} copy(bf16[2,2,2,2,4,4,2,8,256]{8,7,3,6,0,2,5,1,4:T(8,128)(2,1)} %bitcast.91) | data formatting | bytes 4194304 | tf_op jit(solution)/shard_map/transpose | solution.py:118
  27.0 1.1 dynamic-slice_bitcast_fusion
  28.1 7.7 %all-to-all-done = bf16[32,8,512]{2,1,0:T(8,128)(2,1)S(1)} async-done(((bf16[32,8,512]{2,1,0:T(8,128)(2,1)}), bf16[32,8,512]{2,1,0:T(8,128)(2,1)S(1)}, u32[]{:S(2)}, u32[]{:S(2)}) %all-to-all-start) | async-done | bytes 262176 | tf_op jit(solution)/shard_map/all_to_all | solution.py:96
  36.0 21.5 %all_to_all.20 = bf16[8,256,512]{2,1,0:T(8,128)(2,1)S(1)} all-to-all(bf16[8,256,512]{2,1,0:T(8,128)(2,1)S(1)} %broadcast_in_dim.37), channel_id=1, replica_groups={{0,1,8,9,64,65,72,73},{2,3,10,11,66,67,74,75},{16,17,24,25,80,81,88,89}..., dimensions={0} | all-to-all | bytes 4194304 | tf_op jit(solution)/shard_map/all_to_all | solution.py:96
  57.6 2.1 %collective-permute-start = (bf16[2048,512]{1,0:T(8,128)(2,1)S(1)}, bf16[2048,512]{1,0:T(8,128)(2,1)}, u32[]{:S(2)}, u32[]{:S(2)}) collective-permute-start(bf16[2048,512]{1,0:T(8,128)(2,1)S(1)} %bitcast.88), channel_id=1, source_target_pairs={{0,4},{4,0},{8,12},{12,8},{16,20},{20,16},{24,28},{28,24},{32,36},... | collective-permute-start | bytes 6291464 | tf_op jit(solution)/shard_map/ppermute | solution.py:101
  60.0 1.5 %fusion.29.start_ref = f32[256,512]{1,0:T(8,128)} fusion(bf16[2048,256]{1,0:T(8,128)(2,1)S(1)} %get-tuple-element.8, bf16[2048,512]{1,0:T(8,128)(2,1)S(1)} %bitcast.89), kind=kOutput, calls=%fused_computation.58 | convolution fusion | flops 536870912 | bytes 3670016 | tf_op jit(solution)/shard_map/dot_general | solution.py:142
  61.6 2.2 %collective-permute-done.weights_ref = bf16[2048,512]{1,0:T(8,128)(2,1)} collective-permute-done((bf16[2048,512]{1,0:T(8,128)(2,1)S(1)}, bf16[2048,512]{1,0:T(8,128)(2,1)}, u32[]{:S(2)}, u32[]{:S(2)}) %collective-permute-start) | collective-permute-done | bytes 2097184 | tf_op jit(solution)/shard_map/ppermute | solution.py:101
  63.7 4.2 %shard_map.59 = bf16[256,512]{1,0:T(8,128)(2,1)} custom-call(f32[256,512]{1,0:T(8,128)} %fusion.29.start_ref, bf16[2048,256]{1,0:T(8,128)(2,1)} %get-tuple-element.10.rows_ref, bf16[2048,512]{1,0:T(8,128)(2,1)} %collective-permute-done.weights_ref), custom_call_target="tpu_custom_call" | custom-call | flops 536870912 | bytes 3932160 | tf_op jit(solution)/shard_map/pallas_call | solution.py:169
  68.0 1.0 fusion.26
  69.1 2.3 %collective-permute-start.1 = (bf16[256,256]{1,0:T(8,128)(2,1)S(1)}, bf16[256,256]{1,0:T(8,128)(2,1)S(1)}, u32[]{:S(2)}, u32[]{:S(2)}) collective-permute-start(bf16[256,256]{1,0:T(8,128)(2,1)S(1)} %get-tuple-element.20), channel_id=1, source_target_pairs={{0,4},{4,8},{8,12},{12,16},{16,20},{20,24},{24,28},{28,32},{32,36}... | collective-permute-start | bytes 393224 | tf_op jit(solution)/shard_map/ppermute | solution.py:14
  71.4 0.9 fusion.25
  72.2 1.0 collective-permute-done.1
  75.4 1.9 %collective-permute-start.2 = (bf16[256,256]{0,1:T(8,128)(2,1)S(1)}, bf16[256,256]{0,1:T(8,128)(2,1)S(1)}, u32[]{:S(2)}, u32[]{:S(2)}) collective-permute-start(bf16[256,256]{0,1:T(8,128)(2,1)S(1)} %pad_maximum_fusion.1), channel_id=1, source_target_pairs={{4,0},{8,4},{12,8},{16,12},{20,16},{24,20},{28,24},{32,28},{36,32}... | collective-permute-start | bytes 393224 | tf_op jit(solution)/shard_map/ppermute | solution.py:14
  77.3 0.5 convolution_convert_fusion.3
  77.8 1.9 %collective-permute-start.3 = (bf16[2048,256]{1,0:T(8,128)(2,1)S(1)}, bf16[2048,256]{1,0:T(8,128)(2,1)S(1)}, u32[]{:S(2)}, u32[]{:S(2)}) collective-permute-start(bf16[2048,256]{1,0:T(8,128)(2,1)S(1)} %convolution_convert_fusion.3), channel_id=1, source_target_pairs={{0,4},{4,0},{8,12},{12,8},{16,20},{20,16},{24,28},{28,24},{32,36},... | collective-permute-start | bytes 3145736 | tf_op jit(solution)/shard_map/ppermute | solution.py:101
  79.7 2.7 %collective-permute-done.2 = bf16[256,256]{0,1:T(8,128)(2,1)S(1)} collective-permute-done((bf16[256,256]{0,1:T(8,128)(2,1)S(1)}, bf16[256,256]{0,1:T(8,128)(2,1)S(1)}, u32[]{:S(2)}, u32[]{:S(2)}) %collective-permute-start.2) | collective-permute-done | bytes 131104 | tf_op jit(solution)/shard_map/ppermute | solution.py:14
  82.9 1.9 %collective-permute-start.4 = (bf16[2048,256]{1,0:T(8,128)(2,1)S(1)}, bf16[2048,256]{1,0:T(8,128)(2,1)S(1)}, u32[]{:S(2)}, u32[]{:S(2)}) collective-permute-start(bf16[2048,256]{1,0:T(8,128)(2,1)S(1)} %convolution_convert_fusion.2), channel_id=1, source_target_pairs={{0,4},{4,0},{8,12},{12,8},{16,20},{20,16},{24,28},{28,24},{32,36},... | collective-permute-start | bytes 3145736 | tf_op jit(solution)/shard_map/ppermute | solution.py:101
  84.8 0.7 convolution_convert_fusion.1
  85.6 1.9 %collective-permute-done.4 = bf16[2048,256]{1,0:T(8,128)(2,1)S(1)} collective-permute-done((bf16[2048,256]{1,0:T(8,128)(2,1)S(1)}, bf16[2048,256]{1,0:T(8,128)(2,1)S(1)}, u32[]{:S(2)}, u32[]{:S(2)}) %collective-permute-start.4) | collective-permute-done | bytes 1048608 | tf_op jit(solution)/shard_map/ppermute | solution.py:101
  87.5 0.5 add_convert_fusion
  88.0 25.4 %all_to_all.21 = bf16[8,256,512]{2,1,0:T(8,128)(2,1)S(1)} all-to-all(bf16[8,256,512]{2,1,0:T(8,128)(2,1)S(1)} %bitcast.86), channel_id=1, replica_groups={{0,1,8,9,64,65,72,73},{2,3,10,11,66,67,74,75},{16,17,24,25,80,81,88,89}..., dimensions={0} | all-to-all | bytes 4194304 | tf_op jit(solution)/shard_map/all_to_all | solution.py:96
  113.4 1.0 reduce_sum.41
  114.5 7.2 %all-to-all-start.3 = ((bf16[32,8,512]{2,1,0:T(8,128)(2,1)}), bf16[32,8,512]{2,1,0:T(8,128)(2,1)S(1)}, u32[]{:S(2)}, u32[]{:S(2)}) async-start(bf16[32,8,512]{2,1,0:T(8,128)(2,1)} %bitcast.33), calls=%async_computation.3 | async-start | bytes 524288 | tf_op jit(solution)/shard_map/all_to_all | solution.py:96
  121.6 0.5 broadcast_in_dim.40
  122.2 1.1 copy-done.2
  123.5 1.9 %bitcast_dynamic-update-slice_fusion = bf16[4,2,4,2,2,2,2,8,512]{8,7,6,5,4,3,2,1,0:T(8,128)(2,1)S(1)} fusion(bf16[4,2,4,2,2,2,2,8,512]{8,7,6,5,4,3,2,1,0:T(8,128)(2,1)S(1)} %bitcast_dynamic-update-slice_fusion.1, s32[]{:T(128)S(6)} %select_n.14, bf16[2,2,2,4,4,2,8,512]{7,6,5,4,3,2,1,0:T(8,128)(2,1)} %bitcast.28), kind=kLoop, calls=%fused_computation.6 | loop fusion | bytes 4194308 | tf_op jit(solution)/shard_map/dynamic_update_slice | solution.py:126
  125.4 2.6 %fusion = bf16[1,256,4096]{2,1,0:T(8,128)(2,1)} fusion(bf16[4096,512]{1,0:T(8,128)(2,1)S(1)} %bitcast.85, bf16[256,128]{0,1:T(8,128)(2,1)S(1)} %get-tuple-element.17, bf16[256,128]{0,1:T(8,128)(2,1)S(1)} %get-tuple-element.16, bf16[256,256]{0,1:T(8,128)(2,1)S(1)} %bitcast.97), kind=kOutput, calls=%fused_computation.1 | convolution fusion | flops 1075576832 | bytes 6553600 | tf_op jit(solution)/shard_map/dot_general | solution.py:238
  128.0 8.4 %all-to-all-done.3 = bf16[32,8,512]{2,1,0:T(8,128)(2,1)S(1)} async-done(((bf16[32,8,512]{2,1,0:T(8,128)(2,1)}), bf16[32,8,512]{2,1,0:T(8,128)(2,1)S(1)}, u32[]{:S(2)}, u32[]{:S(2)}) %all-to-all-start.3) | async-done | bytes 262176 | tf_op jit(solution)/shard_map/all_to_all | solution.py:96
  136.4 0.7 convert_reduce_fusion
  (32 shorter events, 3.4 us)
Async XLA Ops:
  2.0 33.8 %all-to-all-start = ((bf16[32,8,512]{2,1,0:T(8,128)(2,1)}), bf16[32,8,512]{2,1,0:T(8,128)(2,1)S(1)}, u32[]{:S(2)}, u32[]{:S(2)}) async-start(bf16[32,8,512]{2,1,0:T(8,128)(2,1)} %broadcast_in_dim.36), calls=%async_computation | async-start | bytes 524288 | tf_op jit(solution)/shard_map/all_to_all | solution.py:96
  36.0 23.7 %copy-start.3 = (bf16[1,256,256]{2,1,0:T(8,128)(2,1)S(1)}, bf16[1,256,256]{2,1,0:T(8,128)(2,1)}, u32[]{:S(2)}) copy-start(bf16[1,256,256]{2,1,0:T(8,128)(2,1)} %param.7) | copy-start | bytes 393220
  36.0 23.8 %copy-start.4 = (s32[1,256]{1,0:T(1,128)S(1)}, s32[1,256]{1,0:T(1,128)}, u32[]{:S(2)}) copy-start(s32[1,256]{1,0:T(1,128)} %param.5) | copy-start | bytes 3076
  57.6 4.0 %copy-start.1 = (bf16[8,256,512]{2,1,0:T(8,128)(2,1)}, bf16[8,256,512]{2,1,0:T(8,128)(2,1)S(1)}, u32[]{:S(2)}) copy-start(bf16[8,256,512]{2,1,0:T(8,128)(2,1)S(1)} %all_to_all.20) | copy-start | bytes 6291460
  57.6 6.2 %collective-permute-start = (bf16[2048,512]{1,0:T(8,128)(2,1)S(1)}, bf16[2048,512]{1,0:T(8,128)(2,1)}, u32[]{:S(2)}, u32[]{:S(2)}) collective-permute-start(bf16[2048,512]{1,0:T(8,128)(2,1)S(1)} %bitcast.88), channel_id=1, source_target_pairs={{0,4},{4,0},{8,12},{12,8},{16,20},{20,16},{24,28},{28,24},{32,36},... | collective-permute-start | bytes 6291464 | tf_op jit(solution)/shard_map/ppermute | solution.py:101
  69.1 4.2 %collective-permute-start.1 = (bf16[256,256]{1,0:T(8,128)(2,1)S(1)}, bf16[256,256]{1,0:T(8,128)(2,1)S(1)}, u32[]{:S(2)}, u32[]{:S(2)}) collective-permute-start(bf16[256,256]{1,0:T(8,128)(2,1)S(1)} %get-tuple-element.20), channel_id=1, source_target_pairs={{0,4},{4,8},{8,12},{12,16},{16,20},{20,24},{24,28},{28,32},{32,36}... | collective-permute-start | bytes 393224 | tf_op jit(solution)/shard_map/ppermute | solution.py:14
  74.4 2.9 %copy-start = (bf16[2048,256]{1,0:T(8,128)(2,1)S(1)}, bf16[2048,256]{1,0:T(8,128)(2,1)}, u32[]{:S(2)}) copy-start(bf16[2048,256]{1,0:T(8,128)(2,1)} %get-tuple-element.10.rows_ref) | copy-start | bytes 3145732
  75.4 7.0 %collective-permute-start.2 = (bf16[256,256]{0,1:T(8,128)(2,1)S(1)}, bf16[256,256]{0,1:T(8,128)(2,1)S(1)}, u32[]{:S(2)}, u32[]{:S(2)}) collective-permute-start(bf16[256,256]{0,1:T(8,128)(2,1)S(1)} %pad_maximum_fusion.1), channel_id=1, source_target_pairs={{4,0},{8,4},{12,8},{16,12},{20,16},{24,20},{28,24},{32,28},{36,32}... | collective-permute-start | bytes 393224 | tf_op jit(solution)/shard_map/ppermute | solution.py:14
  77.8 7.8 %collective-permute-start.3 = (bf16[2048,256]{1,0:T(8,128)(2,1)S(1)}, bf16[2048,256]{1,0:T(8,128)(2,1)S(1)}, u32[]{:S(2)}, u32[]{:S(2)}) collective-permute-start(bf16[2048,256]{1,0:T(8,128)(2,1)S(1)} %convolution_convert_fusion.3), channel_id=1, source_target_pairs={{0,4},{4,0},{8,12},{12,8},{16,20},{20,16},{24,28},{28,24},{32,36},... | collective-permute-start | bytes 3145736 | tf_op jit(solution)/shard_map/ppermute | solution.py:101
  82.9 4.6 %collective-permute-start.4 = (bf16[2048,256]{1,0:T(8,128)(2,1)S(1)}, bf16[2048,256]{1,0:T(8,128)(2,1)S(1)}, u32[]{:S(2)}, u32[]{:S(2)}) collective-permute-start(bf16[2048,256]{1,0:T(8,128)(2,1)S(1)} %convolution_convert_fusion.2), channel_id=1, source_target_pairs={{0,4},{4,0},{8,12},{12,8},{16,20},{20,16},{24,28},{28,24},{32,36},... | collective-permute-start | bytes 3145736 | tf_op jit(solution)/shard_map/ppermute | solution.py:101
  114.5 21.9 %all-to-all-start.3 = ((bf16[32,8,512]{2,1,0:T(8,128)(2,1)}), bf16[32,8,512]{2,1,0:T(8,128)(2,1)S(1)}, u32[]{:S(2)}, u32[]{:S(2)}) async-start(bf16[32,8,512]{2,1,0:T(8,128)(2,1)} %bitcast.33), calls=%async_computation.3 | async-start | bytes 524288 | tf_op jit(solution)/shard_map/all_to_all | solution.py:96
  121.6 1.6 %copy-start.2 = (bf16[8,256,512]{2,1,0:T(8,128)(2,1)S(1)}, bf16[8,256,512]{2,1,0:T(8,128)(2,1)}, u32[]{:S(2)}) copy-start(bf16[8,256,512]{2,1,0:T(8,128)(2,1)} %copy-done.1) | copy-start | bytes 6291460

commit v11 on v8

--- a/solution.py
+++ b/solution.py
@@ -75,16 +75,16 @@
 def near_groups():
     groups = []
     for core in range(2):
+        pair = [[(k, 2 - k if odd else k) for k in range(2)] for odd in (core, 1 - core, core)]
         for y in range(4):
             for z in range(4):
                 for x in range(2):
-                    low = [(k, k) if core == 0 else (k, 2 - k) for k in range(2)]
                     groups.append(
                         [
                             spot(2 * y + a[1], 2 * z + b[1], core, 2 * x + d[1])
-                            for a in low
-                            for b in low
-                            for d in low
+                            for a in pair[0]
+                            for b in pair[1]
+                            for d in pair[2]
                         ]
                     )
     return groups

time: 135 us -> 136 us (level)
  blocking collectives: 46.9 us -> 43.5 us
  starting transfers between devices: 36.4 us -> 39.7 us
    all_to_all x2, blocking collectives: 46.9 us -> 43.5 us  [exchange(): return lax.all_to_all(blocks, AXES, 0, 0, axis_index_groups=groups)]
    all_to_all x2, starting transfers between devices: 26.1 us -> 28.1 us  [exchange(): return lax.all_to_all(blocks, AXES, 0, 0, axis_index_groups=groups)]
    ppermute x3, starting transfers between devices: 6.08 us -> 7.85 us  [swap_cores(): return lax.ppermute(block, 'seq', [(i, i ^ 1) for i in range(count)])]
where the time goes in v11:
time: 136 us; the launch traced here: 135 us
  blocking collectives  43.5 us (32%)
  starting transfers between devices  39.7 us (29%)
  waiting for transfers between devices  25.1 us (18%)
  local copies, waits for them, and re-layouts  12.7 us (9%)
  matrix products  10.4 us (8%)
  other arithmetic  2.69 us (2%)
    all_to_all x2, blocking collectives, exchange(): return lax.all_to_all(blocks, AXES, 0, 0, axis_index_groups=groups)  43.5 us
    all_to_all x2, starting transfers between devices, exchange(): return lax.all_to_all(blocks, AXES, 0, 0, axis_index_groups=groups)  28.1 us
    all_to_all x2, waiting for transfers between devices, exchange(): return lax.all_to_all(blocks, AXES, 0, 0, axis_index_groups=groups)  17.3 us
    ppermute x3, starting transfers between devices, swap_cores(): return lax.ppermute(block, 'seq', [(i, i ^ 1) for i in range(count)])  7.85 us
    dot_general x5, matrix products, dot32(): return jnp.dot(a, b, preferred_element_type=jnp.float32)  5.93 us
    unnamed x12, local copies, waits for them, and re-layouts  5.25 us
    ppermute x2, waiting for transfers between devices, from_behind(): return lax.ppermute(block, axis, route)  4.43 us
    ppermute x2, starting transfers between devices, from_behind(): return lax.ppermute(block, axis, route)  3.84 us
  transfers between devices with their start and end apart: 7, of which 6 were waited for; matrix products, arithmetic and copies ran while one was open for 12% of the time, Pallas kernels for 0%

profile of v11, /device:TPU:1, one launch (start us, length us, event | category | flops | bytes accessed | tf_op | source)
XLA Modules:
  0.0 135.1 jit_solution(16027865316899127322)
XLA Ops:
  0.6 1.4 %broadcast_in_dim.36 = bf16[32,8,512]{2,1,0:T(8,128)(2,1)} broadcast(bf16[8,512]{1,0:T(8,128)(2,1)} %param.6), dimensions={1,2} | broadcast | bytes 270336 | tf_op jit(solution)/shard_map/broadcast_in_dim | solution.py:103
  2.0 19.0 %all-to-all-start = ((bf16[32,8,512]{2,1,0:T(8,128)(2,1)}), bf16[32,8,512]{2,1,0:T(8,128)(2,1)S(1)}, u32[]{:S(2)}, u32[]{:S(2)}) async-start(bf16[32,8,512]{2,1,0:T(8,128)(2,1)} %broadcast_in_dim.36), calls=%async_computation | async-start | bytes 524288 | tf_op jit(solution)/shard_map/all_to_all | solution.py:94
  21.0 4.1 %copy.42 = bf16[1,256,4096]{1,2,0:T(8,128)(2,1)} copy(bf16[1,256,4096]{2,1,0:T(8,128)(2,1)} %param.4) | data formatting | bytes 4194304 | tf_op args[0]
  25.1 1.9 %copy.43 = bf16[2,2,2,2,4,4,2,8,256]{8,7,6,5,4,3,2,1,0:T(8,128)(2,1)S(1)} copy(bf16[2,2,2,2,4,4,2,8,256]{8,7,3,6,0,2,5,1,4:T(8,128)(2,1)} %bitcast.93) | data formatting | bytes 4194304 | tf_op jit(solution)/shard_map/transpose | solution.py:116
  27.0 1.1 dynamic-slice_bitcast_fusion
  28.1 7.7 %all-to-all-done = bf16[32,8,512]{2,1,0:T(8,128)(2,1)S(1)} async-done(((bf16[32,8,512]{2,1,0:T(8,128)(2,1)}), bf16[32,8,512]{2,1,0:T(8,128)(2,1)S(1)}, u32[]{:S(2)}, u32[]{:S(2)}) %all-to-all-start) | async-done | bytes 262176 | tf_op jit(solution)/shard_map/all_to_all | solution.py:94
  36.0 20.9 %all_to_all.20 = bf16[8,256,512]{2,1,0:T(8,128)(2,1)S(1)} all-to-all(bf16[8,256,512]{2,1,0:T(8,128)(2,1)S(1)} %broadcast_in_dim.37), channel_id=1, replica_groups={{16,17,8,9,80,81,72,73},{18,19,10,11,82,83,74,75},{32,33,24,25,96,97,88..., dimensions={0} | all-to-all | bytes 4194304 | tf_op jit(solution)/shard_map/all_to_all | solution.py:94
  56.9 3.9 %collective-permute-start = (bf16[2048,512]{1,0:T(8,128)(2,1)S(1)}, bf16[2048,512]{1,0:T(8,128)(2,1)}, u32[]{:S(2)}, u32[]{:S(2)}) collective-permute-start(bf16[2048,512]{1,0:T(8,128)(2,1)S(1)} %bitcast.90), channel_id=1, source_target_pairs={{0,4},{4,0},{8,12},{12,8},{16,20},{20,16},{24,28},{28,24},{32,36},... | collective-permute-start | bytes 6291464 | tf_op jit(solution)/shard_map/ppermute | solution.py:99
  61.2 1.9 %fusion.30 = f32[256,512]{1,0:T(8,128)S(1)} fusion(bf16[2048,256]{1,0:T(8,128)(2,1)} %get-tuple-element.8, bf16[2048,512]{1,0:T(8,128)(2,1)S(1)} %bitcast.91), kind=kOutput, calls=%fused_computation.60 | convolution fusion | flops 536870912 | bytes 3670016 | tf_op jit(solution)/shard_map/dot_general | solution.py:140
  63.1 1.6 %collective-permute-done = bf16[2048,512]{1,0:T(8,128)(2,1)} collective-permute-done((bf16[2048,512]{1,0:T(8,128)(2,1)S(1)}, bf16[2048,512]{1,0:T(8,128)(2,1)}, u32[]{:S(2)}, u32[]{:S(2)}) %collective-permute-start) | collective-permute-done | bytes 2097184 | tf_op jit(solution)/shard_map/ppermute | solution.py:99
  64.7 2.3 %fusion.6 = bf16[256,512]{1,0:T(8,128)(2,1)S(1)} fusion(f32[256,512]{1,0:T(8,128)S(1)} %fusion.30, bf16[2048,256]{1,0:T(8,128)(2,1)S(1)} %get-tuple-element.10, bf16[2048,512]{1,0:T(8,128)(2,1)} %collective-permute-done), kind=kOutput, calls=%fused_computation.16 | convolution fusion | flops 537133056 | bytes 3932160 | tf_op jit(solution)/shard_map/dot_general | solution.py:140
  67.1 1.9 %collective-permute-start.1 = (bf16[256,256]{1,0:T(8,128)(2,1)S(1)}, bf16[256,256]{1,0:T(8,128)(2,1)S(1)}, u32[]{:S(2)}, u32[]{:S(2)}) collective-permute-start(bf16[256,256]{1,0:T(8,128)(2,1)S(1)} %get-tuple-element.20), channel_id=1, source_target_pairs={{0,4},{4,8},{8,12},{12,16},{16,20},{20,24},{24,28},{28,32},{32,36}... | collective-permute-start | bytes 393224 | tf_op jit(solution)/shard_map/ppermute | solution.py:12
  69.1 1.9 %collective-permute-done.1 = bf16[256,256]{1,0:T(8,128)(2,1)S(1)} collective-permute-done((bf16[256,256]{1,0:T(8,128)(2,1)S(1)}, bf16[256,256]{1,0:T(8,128)(2,1)S(1)}, u32[]{:S(2)}, u32[]{:S(2)}) %collective-permute-start.1) | collective-permute-done | bytes 131104 | tf_op jit(solution)/shard_map/ppermute | solution.py:12
  71.8 0.3 fusion.10
  73.1 1.9 %collective-permute-start.2 = (bf16[256,256]{0,1:T(8,128)(2,1)S(1)}, bf16[256,256]{0,1:T(8,128)(2,1)S(1)}, u32[]{:S(2)}, u32[]{:S(2)}) collective-permute-start(bf16[256,256]{0,1:T(8,128)(2,1)S(1)} %pad_maximum_fusion.1), channel_id=1, source_target_pairs={{4,0},{8,4},{12,8},{16,12},{20,16},{24,20},{28,24},{32,28},{36,32}... | collective-permute-start | bytes 393224 | tf_op jit(solution)/shard_map/ppermute | solution.py:12
  75.0 0.5 convolution_convert_fusion.3
  75.5 2.1 %collective-permute-start.3 = (bf16[2048,256]{1,0:T(8,128)(2,1)S(1)}, bf16[2048,256]{1,0:T(8,128)(2,1)S(1)}, u32[]{:S(2)}, u32[]{:S(2)}) collective-permute-start(bf16[2048,256]{1,0:T(8,128)(2,1)S(1)} %convolution_convert_fusion.3), channel_id=1, source_target_pairs={{0,4},{4,0},{8,12},{12,8},{16,20},{20,16},{24,28},{28,24},{32,36},... | collective-permute-start | bytes 3145736 | tf_op jit(solution)/shard_map/ppermute | solution.py:99
  77.6 2.5 %collective-permute-done.2 = bf16[256,256]{0,1:T(8,128)(2,1)S(1)} collective-permute-done((bf16[256,256]{0,1:T(8,128)(2,1)S(1)}, bf16[256,256]{0,1:T(8,128)(2,1)S(1)}, u32[]{:S(2)}, u32[]{:S(2)}) %collective-permute-start.2) | collective-permute-done | bytes 131104 | tf_op jit(solution)/shard_map/ppermute | solution.py:12
  80.2 0.5 convolution_convert_fusion.2
  80.6 1.9 %collective-permute-start.4 = (bf16[2048,256]{1,0:T(8,128)(2,1)S(1)}, bf16[2048,256]{1,0:T(8,128)(2,1)S(1)}, u32[]{:S(2)}, u32[]{:S(2)}) collective-permute-start(bf16[2048,256]{1,0:T(8,128)(2,1)S(1)} %convolution_convert_fusion.2), channel_id=1, source_target_pairs={{0,4},{4,0},{8,12},{12,8},{16,20},{20,16},{24,28},{28,24},{32,36},... | collective-permute-start | bytes 3145736 | tf_op jit(solution)/shard_map/ppermute | solution.py:99
  82.6 0.7 convolution_convert_fusion.1
  83.3 1.9 %collective-permute-done.4 = bf16[2048,256]{1,0:T(8,128)(2,1)S(1)} collective-permute-done((bf16[2048,256]{1,0:T(8,128)(2,1)S(1)}, bf16[2048,256]{1,0:T(8,128)(2,1)S(1)}, u32[]{:S(2)}, u32[]{:S(2)}) %collective-permute-start.4) | collective-permute-done | bytes 1048608 | tf_op jit(solution)/shard_map/ppermute | solution.py:99
  85.2 0.5 add_convert_fusion
  85.7 22.6 %all_to_all.21 = bf16[8,256,512]{2,1,0:T(8,128)(2,1)S(1)} all-to-all(bf16[8,256,512]{2,1,0:T(8,128)(2,1)S(1)} %bitcast.88), channel_id=1, replica_groups={{16,17,8,9,80,81,72,73},{18,19,10,11,82,83,74,75},{32,33,24,25,96,97,88..., dimensions={0} | all-to-all | bytes 4194304 | tf_op jit(solution)/shard_map/all_to_all | solution.py:94
  108.3 1.0 reduce_sum.41
  109.4 9.1 %all-to-all-start.3 = ((bf16[32,8,512]{2,1,0:T(8,128)(2,1)}), bf16[32,8,512]{2,1,0:T(8,128)(2,1)S(1)}, u32[]{:S(2)}, u32[]{:S(2)}) async-start(bf16[32,8,512]{2,1,0:T(8,128)(2,1)} %bitcast.33), calls=%async_computation.3 | async-start | bytes 524288 | tf_op jit(solution)/shard_map/all_to_all | solution.py:94
  118.5 0.5 broadcast_in_dim.40
  119.0 1.1 copy-done.1
  120.3 1.9 %copy_dynamic-update-slice_fusion = bf16[4,2,4,2,2,2,2,8,512]{8,7,6,5,4,3,2,1,0:T(8,128)(2,1)S(1)} fusion(bf16[4,2,4,2,2,2,2,8,512]{8,7,6,5,4,3,2,1,0:T(8,128)(2,1)S(1)} %copy_dynamic-update-slice_fusion.1, s32[]{:T(128)S(6)} %select_n.14, bf16[4,2,4,2,1,2,2,8,512]{8,7,5,2,0,6,3,1,4:T(8,128)(2,1)} %bitcast.30), kind=kLoop, calls=%fused_computation.6 | loop fusion | bytes 4194308 | tf_op jit(solution)/shard_map/dynamic_update_slice | solution.py:124
  122.2 2.6 %fusion = bf16[1,256,4096]{2,1,0:T(8,128)(2,1)} fusion(bf16[4096,512]{1,0:T(8,128)(2,1)S(1)} %bitcast.87, bf16[256,128]{0,1:T(8,128)(2,1)S(1)} %get-tuple-element.17, bf16[256,128]{0,1:T(8,128)(2,1)S(1)} %get-tuple-element.16, bf16[256,256]{0,1:T(8,128)(2,1)S(1)} %bitcast.99), kind=kOutput, calls=%fused_computation.1 | convolution fusion | flops 1075576832 | bytes 6553600 | tf_op jit(solution)/shard_map/dot_general | solution.py:195
  124.9 9.5 %all-to-all-done.3 = bf16[32,8,512]{2,1,0:T(8,128)(2,1)S(1)} async-done(((bf16[32,8,512]{2,1,0:T(8,128)(2,1)}), bf16[32,8,512]{2,1,0:T(8,128)(2,1)S(1)}, u32[]{:S(2)}, u32[]{:S(2)}) %all-to-all-start.3) | async-done | bytes 262176 | tf_op jit(solution)/shard_map/all_to_all | solution.py:94
  134.4 0.7 convert_reduce_fusion
  (32 shorter events, 2.7 us)
Async XLA Ops:
  2.0 33.8 %all-to-all-start = ((bf16[32,8,512]{2,1,0:T(8,128)(2,1)}), bf16[32,8,512]{2,1,0:T(8,128)(2,1)S(1)}, u32[]{:S(2)}, u32[]{:S(2)}) async-start(bf16[32,8,512]{2,1,0:T(8,128)(2,1)} %broadcast_in_dim.36), calls=%async_computation | async-start | bytes 524288 | tf_op jit(solution)/shard_map/all_to_all | solution.py:94
  36.0 24.8 %copy-start.3 = (bf16[1,256,256]{2,1,0:T(8,128)(2,1)S(1)}, bf16[1,256,256]{2,1,0:T(8,128)(2,1)}, u32[]{:S(2)}) copy-start(bf16[1,256,256]{2,1,0:T(8,128)(2,1)} %param.7) | copy-start | bytes 393220
  36.0 24.9 %copy-start.4 = (s32[1,256]{1,0:T(1,128)S(1)}, s32[1,256]{1,0:T(1,128)}, u32[]{:S(2)}) copy-start(s32[1,256]{1,0:T(1,128)} %param.5) | copy-start | bytes 3076
  56.9 6.2 %copy-start = (bf16[8,256,512]{2,1,0:T(8,128)(2,1)}, bf16[8,256,512]{2,1,0:T(8,128)(2,1)S(1)}, u32[]{:S(2)}) copy-start(bf16[8,256,512]{2,1,0:T(8,128)(2,1)S(1)} %all_to_all.20) | copy-start | bytes 6291460
  56.9 7.8 %collective-permute-start = (bf16[2048,512]{1,0:T(8,128)(2,1)S(1)}, bf16[2048,512]{1,0:T(8,128)(2,1)}, u32[]{:S(2)}, u32[]{:S(2)}) collective-permute-start(bf16[2048,512]{1,0:T(8,128)(2,1)S(1)} %bitcast.90), channel_id=1, source_target_pairs={{0,4},{4,0},{8,12},{12,8},{16,20},{20,16},{24,28},{28,24},{32,36},... | collective-permute-start | bytes 6291464 | tf_op jit(solution)/shard_map/ppermute | solution.py:99
  67.1 3.9 %collective-permute-start.1 = (bf16[256,256]{1,0:T(8,128)(2,1)S(1)}, bf16[256,256]{1,0:T(8,128)(2,1)S(1)}, u32[]{:S(2)}, u32[]{:S(2)}) collective-permute-start(bf16[256,256]{1,0:T(8,128)(2,1)S(1)} %get-tuple-element.20), channel_id=1, source_target_pairs={{0,4},{4,8},{8,12},{12,16},{16,20},{20,24},{24,28},{28,32},{32,36}... | collective-permute-start | bytes 393224 | tf_op jit(solution)/shard_map/ppermute | solution.py:12
  73.1 7.0 %collective-permute-start.2 = (bf16[256,256]{0,1:T(8,128)(2,1)S(1)}, bf16[256,256]{0,1:T(8,128)(2,1)S(1)}, u32[]{:S(2)}, u32[]{:S(2)}) collective-permute-start(bf16[256,256]{0,1:T(8,128)(2,1)S(1)} %pad_maximum_fusion.1), channel_id=1, source_target_pairs={{4,0},{8,4},{12,8},{16,12},{20,16},{24,20},{28,24},{32,28},{36,32}... | collective-permute-start | bytes 393224 | tf_op jit(solution)/shard_map/ppermute | solution.py:12
  75.5 7.1 %copy-start.2 = (bf16[2048,256]{1,0:T(8,128)(2,1)S(1)}, bf16[2048,256]{1,0:T(8,128)(2,1)}, u32[]{:S(2)}) copy-start(bf16[2048,256]{1,0:T(8,128)(2,1)} %get-tuple-element.8) | copy-start | bytes 3145732
  75.5 7.8 %collective-permute-start.3 = (bf16[2048,256]{1,0:T(8,128)(2,1)S(1)}, bf16[2048,256]{1,0:T(8,128)(2,1)S(1)}, u32[]{:S(2)}, u32[]{:S(2)}) collective-permute-start(bf16[2048,256]{1,0:T(8,128)(2,1)S(1)} %convolution_convert_fusion.3), channel_id=1, source_target_pairs={{0,4},{4,0},{8,12},{12,8},{16,20},{20,16},{24,28},{28,24},{32,36},... | collective-permute-start | bytes 3145736 | tf_op jit(solution)/shard_map/ppermute | solution.py:99
  80.6 4.6 %collective-permute-start.4 = (bf16[2048,256]{1,0:T(8,128)(2,1)S(1)}, bf16[2048,256]{1,0:T(8,128)(2,1)S(1)}, u32[]{:S(2)}, u32[]{:S(2)}) collective-permute-start(bf16[2048,256]{1,0:T(8,128)(2,1)S(1)} %convolution_convert_fusion.2), channel_id=1, source_target_pairs={{0,4},{4,0},{8,12},{12,8},{16,20},{20,16},{24,28},{28,24},{32,36},... | collective-permute-start | bytes 3145736 | tf_op jit(solution)/shard_map/ppermute | solution.py:99
  109.4 25.0 %all-to-all-start.3 = ((bf16[32,8,512]{2,1,0:T(8,128)(2,1)}), bf16[32,8,512]{2,1,0:T(8,128)(2,1)S(1)}, u32[]{:S(2)}, u32[]{:S(2)}) async-start(bf16[32,8,512]{2,1,0:T(8,128)(2,1)} %bitcast.33), calls=%async_computation.3 | async-start | bytes 524288 | tf_op jit(solution)/shard_map/all_to_all | solution.py:94
  118.5 1.6 %copy-start.1 = (bf16[8,256,512]{2,1,0:T(8,128)(2,1)S(1)}, bf16[8,256,512]{2,1,0:T(8,128)(2,1)}, u32[]{:S(2)}) copy-start(bf16[8,256,512]{2,1,0:T(8,128)(2,1)} %copy-done) | copy-start | bytes 6291460

commit v12 on v11

--- a/solution.py
+++ b/solution.py
@@ -75,7 +75,7 @@
 def near_groups():
     groups = []
     for core in range(2):
-        pair = [[(k, 2 - k if odd else k) for k in range(2)] for odd in (core, 1 - core, core)]
+        pair = [[(k, 2 - k if odd else k) for k in range(2)] for odd in (core, core, 1 - core)]
         for y in range(4):
             for z in range(4):
                 for x in range(2):

time: 136 us -> 136 us (level)
    all_to_all x2, starting transfers between devices: 28.1 us -> 25.6 us  [exchange(): return lax.all_to_all(blocks, AXES, 0, 0, axis_index_groups=groups)]
    ppermute x3, starting transfers between devices: 7.85 us -> 9.4 us  [swap_cores(): return lax.ppermute(block, 'seq', [(i, i ^ 1) for i in range(count)])]
where the time goes in v12:
time: 136 us; the launch traced here: 135 us
  blocking collectives  43.9 us (32%)
  starting transfers between devices  39.4 us (29%)
  waiting for transfers between devices  25.2 us (19%)
  local copies, waits for them, and re-layouts  12.7 us (9%)
  matrix products  10.4 us (8%)
  other arithmetic  2.69 us (2%)
    all_to_all x2, blocking collectives, exchange(): return lax.all_to_all(blocks, AXES, 0, 0, axis_index_groups=groups)  43.9 us
    all_to_all x2, starting transfers between devices, exchange(): return lax.all_to_all(blocks, AXES, 0, 0, axis_index_groups=groups)  25.6 us
    all_to_all x2, waiting for transfers between devices, exchange(): return lax.all_to_all(blocks, AXES, 0, 0, axis_index_groups=groups)  17.4 us
    ppermute x3, starting transfers between devices, swap_cores(): return lax.ppermute(block, 'seq', [(i, i ^ 1) for i in range(count)])  9.4 us
    dot_general x5, matrix products, dot32(): return jnp.dot(a, b, preferred_element_type=jnp.float32)  5.93 us
    unnamed x12, local copies, waits for them, and re-layouts  5.25 us
    ppermute x2, waiting for transfers between devices, from_behind(): return lax.ppermute(block, axis, route)  4.43 us
    ppermute x2, starting transfers between devices, from_behind(): return lax.ppermute(block, axis, route)  4.37 us
  transfers between devices with their start and end apart: 7, of which 6 were waited for; matrix products, arithmetic and copies ran while one was open for 12% of the time, Pallas kernels for 0%

profile of v12, /device:TPU:1, one launch (start us, length us, event | category | flops | bytes accessed | tf_op | source)
XLA Modules:
  0.0 135.3 jit_solution(13388938153740651376)
XLA Ops:
  0.6 1.4 %broadcast_in_dim.36 = bf16[32,8,512]{2,1,0:T(8,128)(2,1)} broadcast(bf16[8,512]{1,0:T(8,128)(2,1)} %param.6), dimensions={1,2} | broadcast | bytes 270336 | tf_op jit(solution)/shard_map/broadcast_in_dim | solution.py:103
  2.0 19.0 %all-to-all-start = ((bf16[32,8,512]{2,1,0:T(8,128)(2,1)}), bf16[32,8,512]{2,1,0:T(8,128)(2,1)S(1)}, u32[]{:S(2)}, u32[]{:S(2)}) async-start(bf16[32,8,512]{2,1,0:T(8,128)(2,1)} %broadcast_in_dim.36), calls=%async_computation | async-start | bytes 524288 | tf_op jit(solution)/shard_map/all_to_all | solution.py:94
  21.0 4.1 %copy.42 = bf16[1,256,4096]{1,2,0:T(8,128)(2,1)} copy(bf16[1,256,4096]{2,1,0:T(8,128)(2,1)} %param.4) | data formatting | bytes 4194304 | tf_op args[0]
  25.1 1.9 %copy.43 = bf16[2,2,2,2,4,4,2,8,256]{8,7,6,5,4,3,2,1,0:T(8,128)(2,1)S(1)} copy(bf16[2,2,2,2,4,4,2,8,256]{8,7,3,6,0,2,5,1,4:T(8,128)(2,1)} %bitcast.93) | data formatting | bytes 4194304 | tf_op jit(solution)/shard_map/transpose | solution.py:116
  27.0 1.1 dynamic-slice_bitcast_fusion
  28.1 7.7 %all-to-all-done = bf16[32,8,512]{2,1,0:T(8,128)(2,1)S(1)} async-done(((bf16[32,8,512]{2,1,0:T(8,128)(2,1)}), bf16[32,8,512]{2,1,0:T(8,128)(2,1)S(1)}, u32[]{:S(2)}, u32[]{:S(2)}) %all-to-all-start) | async-done | bytes 262176 | tf_op jit(solution)/shard_map/all_to_all | solution.py:94
  36.0 20.3 %all_to_all.20 = bf16[8,256,512]{2,1,0:T(8,128)(2,1)S(1)} all-to-all(bf16[8,256,512]{2,1,0:T(8,128)(2,1)S(1)} %broadcast_in_dim.37), channel_id=1, replica_groups={{2,1,10,9,66,65,74,73},{0,3,8,11,64,67,72,75},{18,17,26,25,82,81,90,89}..., dimensions={0} | all-to-all | bytes 4194304 | tf_op jit(solution)/shard_map/all_to_all | solution.py:94
  56.4 5.4 %collective-permute-start = (bf16[2048,512]{1,0:T(8,128)(2,1)S(1)}, bf16[2048,512]{1,0:T(8,128)(2,1)}, u32[]{:S(2)}, u32[]{:S(2)}) collective-permute-start(bf16[2048,512]{1,0:T(8,128)(2,1)S(1)} %bitcast.90), channel_id=1, source_target_pairs={{0,4},{4,0},{8,12},{12,8},{16,20},{20,16},{24,28},{28,24},{32,36},... | collective-permute-start | bytes 6291464 | tf_op jit(solution)/shard_map/ppermute | solution.py:99
  62.2 1.9 %fusion.30 = f32[256,512]{1,0:T(8,128)S(1)} fusion(bf16[2048,256]{1,0:T(8,128)(2,1)} %get-tuple-element.8, bf16[2048,512]{1,0:T(8,128)(2,1)S(1)} %bitcast.91), kind=kOutput, calls=%fused_computation.60 | convolution fusion | flops 536870912 | bytes 3670016 | tf_op jit(solution)/shard_map/dot_general | solution.py:140
  64.1 1.6 %collective-permute-done = bf16[2048,512]{1,0:T(8,128)(2,1)} collective-permute-done((bf16[2048,512]{1,0:T(8,128)(2,1)S(1)}, bf16[2048,512]{1,0:T(8,128)(2,1)}, u32[]{:S(2)}, u32[]{:S(2)}) %collective-permute-start) | collective-permute-done | bytes 2097184 | tf_op jit(solution)/shard_map/ppermute | solution.py:99
  65.7 2.3 %fusion.6 = bf16[256,512]{1,0:T(8,128)(2,1)S(1)} fusion(f32[256,512]{1,0:T(8,128)S(1)} %fusion.30, bf16[2048,256]{1,0:T(8,128)(2,1)S(1)} %get-tuple-element.10, bf16[2048,512]{1,0:T(8,128)(2,1)} %collective-permute-done), kind=kOutput, calls=%fused_computation.16 | convolution fusion | flops 537133056 | bytes 3932160 | tf_op jit(solution)/shard_map/dot_general | solution.py:140
  68.1 2.4 %collective-permute-start.1 = (bf16[256,256]{1,0:T(8,128)(2,1)S(1)}, bf16[256,256]{1,0:T(8,128)(2,1)S(1)}, u32[]{:S(2)}, u32[]{:S(2)}) collective-permute-start(bf16[256,256]{1,0:T(8,128)(2,1)S(1)} %get-tuple-element.20), channel_id=1, source_target_pairs={{0,4},{4,8},{8,12},{12,16},{16,20},{20,24},{24,28},{28,32},{32,36}... | collective-permute-start | bytes 393224 | tf_op jit(solution)/shard_map/ppermute | solution.py:12
  70.6 1.9 %collective-permute-done.1 = bf16[256,256]{1,0:T(8,128)(2,1)S(1)} collective-permute-done((bf16[256,256]{1,0:T(8,128)(2,1)S(1)}, bf16[256,256]{1,0:T(8,128)(2,1)S(1)}, u32[]{:S(2)}, u32[]{:S(2)}) %collective-permute-start.1) | collective-permute-done | bytes 131104 | tf_op jit(solution)/shard_map/ppermute | solution.py:12
  73.3 0.3 fusion.10
  74.6 1.9 %collective-permute-start.2 = (bf16[256,256]{0,1:T(8,128)(2,1)S(1)}, bf16[256,256]{0,1:T(8,128)(2,1)S(1)}, u32[]{:S(2)}, u32[]{:S(2)}) collective-permute-start(bf16[256,256]{0,1:T(8,128)(2,1)S(1)} %pad_maximum_fusion.1), channel_id=1, source_target_pairs={{4,0},{8,4},{12,8},{16,12},{20,16},{24,20},{28,24},{32,28},{36,32}... | collective-permute-start | bytes 393224 | tf_op jit(solution)/shard_map/ppermute | solution.py:12
  76.5 0.5 convolution_convert_fusion.3
  77.0 2.1 %collective-permute-start.3 = (bf16[2048,256]{1,0:T(8,128)(2,1)S(1)}, bf16[2048,256]{1,0:T(8,128)(2,1)S(1)}, u32[]{:S(2)}, u32[]{:S(2)}) collective-permute-start(bf16[2048,256]{1,0:T(8,128)(2,1)S(1)} %convolution_convert_fusion.3), channel_id=1, source_target_pairs={{0,4},{4,0},{8,12},{12,8},{16,20},{20,16},{24,28},{28,24},{32,36},... | collective-permute-start | bytes 3145736 | tf_op jit(solution)/shard_map/ppermute | solution.py:99
  79.1 2.5 %collective-permute-done.2 = bf16[256,256]{0,1:T(8,128)(2,1)S(1)} collective-permute-done((bf16[256,256]{0,1:T(8,128)(2,1)S(1)}, bf16[256,256]{0,1:T(8,128)(2,1)S(1)}, u32[]{:S(2)}, u32[]{:S(2)}) %collective-permute-start.2) | collective-permute-done | bytes 131104 | tf_op jit(solution)/shard_map/ppermute | solution.py:12
  81.7 0.5 convolution_convert_fusion.2
  82.2 1.9 %collective-permute-start.4 = (bf16[2048,256]{1,0:T(8,128)(2,1)S(1)}, bf16[2048,256]{1,0:T(8,128)(2,1)S(1)}, u32[]{:S(2)}, u32[]{:S(2)}) collective-permute-start(bf16[2048,256]{1,0:T(8,128)(2,1)S(1)} %convolution_convert_fusion.2), channel_id=1, source_target_pairs={{0,4},{4,0},{8,12},{12,8},{16,20},{20,16},{24,28},{28,24},{32,36},... | collective-permute-start | bytes 3145736 | tf_op jit(solution)/shard_map/ppermute | solution.py:99
  84.1 0.7 convolution_convert_fusion.1
  84.9 1.9 %collective-permute-done.4 = bf16[2048,256]{1,0:T(8,128)(2,1)S(1)} collective-permute-done((bf16[2048,256]{1,0:T(8,128)(2,1)S(1)}, bf16[2048,256]{1,0:T(8,128)(2,1)S(1)}, u32[]{:S(2)}, u32[]{:S(2)}) %collective-permute-start.4) | collective-permute-done | bytes 1048608 | tf_op jit(solution)/shard_map/ppermute | solution.py:99
  86.7 0.5 add_convert_fusion
  87.3 23.6 %all_to_all.21 = bf16[8,256,512]{2,1,0:T(8,128)(2,1)S(1)} all-to-all(bf16[8,256,512]{2,1,0:T(8,128)(2,1)S(1)} %bitcast.88), channel_id=1, replica_groups={{2,1,10,9,66,65,74,73},{0,3,8,11,64,67,72,75},{18,17,26,25,82,81,90,89}..., dimensions={0} | all-to-all | bytes 4194304 | tf_op jit(solution)/shard_map/all_to_all | solution.py:94
  110.9 1.0 reduce_sum.41
  111.9 6.7 %all-to-all-start.3 = ((bf16[32,8,512]{2,1,0:T(8,128)(2,1)}), bf16[32,8,512]{2,1,0:T(8,128)(2,1)S(1)}, u32[]{:S(2)}, u32[]{:S(2)}) async-start(bf16[32,8,512]{2,1,0:T(8,128)(2,1)} %bitcast.33), calls=%async_computation.3 | async-start | bytes 524288 | tf_op jit(solution)/shard_map/all_to_all | solution.py:94
  118.6 0.5 broadcast_in_dim.40
  119.2 1.1 copy-done.1
  120.5 1.9 %copy_dynamic-update-slice_fusion = bf16[4,2,4,2,2,2,2,8,512]{8,7,6,5,4,3,2,1,0:T(8,128)(2,1)S(1)} fusion(bf16[4,2,4,2,2,2,2,8,512]{8,7,6,5,4,3,2,1,0:T(8,128)(2,1)S(1)} %copy_dynamic-update-slice_fusion.1, s32[]{:T(128)S(6)} %select_n.14, bf16[4,2,4,2,1,2,2,8,512]{8,7,5,2,0,6,3,1,4:T(8,128)(2,1)} %bitcast.30), kind=kLoop, calls=%fused_computation.6 | loop fusion | bytes 4194308 | tf_op jit(solution)/shard_map/dynamic_update_slice | solution.py:124
  122.4 2.6 %fusion = bf16[1,256,4096]{2,1,0:T(8,128)(2,1)} fusion(bf16[4096,512]{1,0:T(8,128)(2,1)S(1)} %bitcast.87, bf16[256,128]{0,1:T(8,128)(2,1)S(1)} %get-tuple-element.17, bf16[256,128]{0,1:T(8,128)(2,1)S(1)} %get-tuple-element.16, bf16[256,256]{0,1:T(8,128)(2,1)S(1)} %bitcast.99), kind=kOutput, calls=%fused_computation.1 | convolution fusion | flops 1075576832 | bytes 6553600 | tf_op jit(solution)/shard_map/dot_general | solution.py:195
  125.0 9.6 %all-to-all-done.3 = bf16[32,8,512]{2,1,0:T(8,128)(2,1)S(1)} async-done(((bf16[32,8,512]{2,1,0:T(8,128)(2,1)}), bf16[32,8,512]{2,1,0:T(8,128)(2,1)S(1)}, u32[]{:S(2)}, u32[]{:S(2)}) %all-to-all-start.3) | async-done | bytes 262176 | tf_op jit(solution)/shard_map/all_to_all | solution.py:94
  134.6 0.7 convert_reduce_fusion
  (32 shorter events, 2.7 us)
Async XLA Ops:
  2.0 33.8 %all-to-all-start = ((bf16[32,8,512]{2,1,0:T(8,128)(2,1)}), bf16[32,8,512]{2,1,0:T(8,128)(2,1)S(1)}, u32[]{:S(2)}, u32[]{:S(2)}) async-start(bf16[32,8,512]{2,1,0:T(8,128)(2,1)} %broadcast_in_dim.36), calls=%async_computation | async-start | bytes 524288 | tf_op jit(solution)/shard_map/all_to_all | solution.py:94
  36.0 25.8 %copy-start.3 = (bf16[1,256,256]{2,1,0:T(8,128)(2,1)S(1)}, bf16[1,256,256]{2,1,0:T(8,128)(2,1)}, u32[]{:S(2)}) copy-start(bf16[1,256,256]{2,1,0:T(8,128)(2,1)} %param.7) | copy-start | bytes 393220
  36.0 25.9 %copy-start.4 = (s32[1,256]{1,0:T(1,128)S(1)}, s32[1,256]{1,0:T(1,128)}, u32[]{:S(2)}) copy-start(s32[1,256]{1,0:T(1,128)} %param.5) | copy-start | bytes 3076
  56.4 7.8 %copy-start = (bf16[8,256,512]{2,1,0:T(8,128)(2,1)}, bf16[8,256,512]{2,1,0:T(8,128)(2,1)S(1)}, u32[]{:S(2)}) copy-start(bf16[8,256,512]{2,1,0:T(8,128)(2,1)S(1)} %all_to_all.20) | copy-start | bytes 6291460
  56.4 9.3 %collective-permute-start = (bf16[2048,512]{1,0:T(8,128)(2,1)S(1)}, bf16[2048,512]{1,0:T(8,128)(2,1)}, u32[]{:S(2)}, u32[]{:S(2)}) collective-permute-start(bf16[2048,512]{1,0:T(8,128)(2,1)S(1)} %bitcast.90), channel_id=1, source_target_pairs={{0,4},{4,0},{8,12},{12,8},{16,20},{20,16},{24,28},{28,24},{32,36},... | collective-permute-start | bytes 6291464 | tf_op jit(solution)/shard_map/ppermute | solution.py:99
  68.1 4.4 %collective-permute-start.1 = (bf16[256,256]{1,0:T(8,128)(2,1)S(1)}, bf16[256,256]{1,0:T(8,128)(2,1)S(1)}, u32[]{:S(2)}, u32[]{:S(2)}) collective-permute-start(bf16[256,256]{1,0:T(8,128)(2,1)S(1)} %get-tuple-element.20), channel_id=1, source_target_pairs={{0,4},{4,8},{8,12},{12,16},{16,20},{20,24},{24,28},{28,32},{32,36}... | collective-permute-start | bytes 393224 | tf_op jit(solution)/shard_map/ppermute | solution.py:12
  74.6 7.0 %collective-permute-start.2 = (bf16[256,256]{0,1:T(8,128)(2,1)S(1)}, bf16[256,256]{0,1:T(8,128)(2,1)S(1)}, u32[]{:S(2)}, u32[]{:S(2)}) collective-permute-start(bf16[256,256]{0,1:T(8,128)(2,1)S(1)} %pad_maximum_fusion.1), channel_id=1, source_target_pairs={{4,0},{8,4},{12,8},{16,12},{20,16},{24,20},{28,24},{32,28},{36,32}... | collective-permute-start | bytes 393224 | tf_op jit(solution)/shard_map/ppermute | solution.py:12
  77.0 7.1 %copy-start.2 = (bf16[2048,256]{1,0:T(8,128)(2,1)S(1)}, bf16[2048,256]{1,0:T(8,128)(2,1)}, u32[]{:S(2)}) copy-start(bf16[2048,256]{1,0:T(8,128)(2,1)} %get-tuple-element.8) | copy-start | bytes 3145732
  77.0 7.8 %collective-permute-start.3 = (bf16[2048,256]{1,0:T(8,128)(2,1)S(1)}, bf16[2048,256]{1,0:T(8,128)(2,1)S(1)}, u32[]{:S(2)}, u32[]{:S(2)}) collective-permute-start(bf16[2048,256]{1,0:T(8,128)(2,1)S(1)} %convolution_convert_fusion.3), channel_id=1, source_target_pairs={{0,4},{4,0},{8,12},{12,8},{16,20},{20,16},{24,28},{28,24},{32,36},... | collective-permute-start | bytes 3145736 | tf_op jit(solution)/shard_map/ppermute | solution.py:99
  82.2 4.6 %collective-permute-start.4 = (bf16[2048,256]{1,0:T(8,128)(2,1)S(1)}, bf16[2048,256]{1,0:T(8,128)(2,1)S(1)}, u32[]{:S(2)}, u32[]{:S(2)}) collective-permute-start(bf16[2048,256]{1,0:T(8,128)(2,1)S(1)} %convolution_convert_fusion.2), channel_id=1, source_target_pairs={{0,4},{4,0},{8,12},{12,8},{16,20},{20,16},{24,28},{28,24},{32,36},... | collective-permute-start | bytes 3145736 | tf_op jit(solution)/shard_map/ppermute | solution.py:99
  111.9 22.7 %all-to-all-start.3 = ((bf16[32,8,512]{2,1,0:T(8,128)(2,1)}), bf16[32,8,512]{2,1,0:T(8,128)(2,1)S(1)}, u32[]{:S(2)}, u32[]{:S(2)}) async-start(bf16[32,8,512]{2,1,0:T(8,128)(2,1)} %bitcast.33), calls=%async_computation.3 | async-start | bytes 524288 | tf_op jit(solution)/shard_map/all_to_all | solution.py:94
  118.6 1.6 %copy-start.1 = (bf16[8,256,512]{2,1,0:T(8,128)(2,1)S(1)}, bf16[8,256,512]{2,1,0:T(8,128)(2,1)}, u32[]{:S(2)}) copy-start(bf16[8,256,512]{2,1,0:T(8,128)(2,1)} %copy-done) | copy-start | bytes 6291460

commit v13 on v8

--- a/solution.py
+++ b/solution.py
@@ -158,11 +158,12 @@
     x_own, x_other = rows_own.T, rows_other.T
     w_own = gather_near(far)
     w_other = swap_cores(w_own)
-    projected = dot32(x_own, w_own) + dot32(x_other, w_other)
-    projected = projected.astype(jnp.bfloat16)
-    queries = projected[:, :q_width].reshape(tok_rows, heads, head_dim)
-    key_value = projected[:, q_width:]
+    partial = dot32(x_own, w_own)
+    key_value = partial[:, q_width:] + dot32(x_other, w_other[:, q_width:])
+    key_value = key_value.astype(jnp.bfloat16)
     prior = from_behind(key_value, "seq", 1)
+    queries = partial[:, :q_width] + dot32(x_other, w_other[:, :q_width])
+    queries = queries.astype(jnp.bfloat16).reshape(tok_rows, heads, head_dim)
     key_rows = jnp.concatenate([prior[:, :head_dim], key_value[:, :head_dim]], axis=0)
     value_rows = jnp.concatenate([prior[:, head_dim:], key_value[:, head_dim:]], axis=0)
     key_pos = jnp.concatenate([positions - tok_rows, positions])

time: 135 us -> 136 us (level)
    dot_general x5 -> x6, matrix products: 5.93 us -> 7.07 us  [dot32(): return jnp.dot(a, b, preferred_element_type=jnp.float32)]
    unnamed x12 -> x14, local copies, waits for them, and re-layouts: 5.25 us -> 5.26 us
where the time goes in v13:
time: 136 us; the launch traced here: 135 us
  blocking collectives  46.9 us (34%)
  starting transfers between devices  36.4 us (27%)
  waiting for transfers between devices  24.1 us (18%)
  local copies, waits for them, and re-layouts  12.6 us (9%)
  matrix products  11.5 us (8%)
  other arithmetic  2.68 us (2%)
    all_to_all x2, blocking collectives, exchange(): return lax.all_to_all(blocks, AXES, 0, 0, axis_index_groups=groups)  46.9 us
    all_to_all x2, starting transfers between devices, exchange(): return lax.all_to_all(blocks, AXES, 0, 0, axis_index_groups=groups)  26.1 us
    all_to_all x2, waiting for transfers between devices, exchange(): return lax.all_to_all(blocks, AXES, 0, 0, axis_index_groups=groups)  16.1 us
    dot_general x6, matrix products, dot32(): return jnp.dot(a, b, preferred_element_type=jnp.float32)  7.07 us
    ppermute x3, starting transfers between devices, swap_cores(): return lax.ppermute(block, 'seq', [(i, i ^ 1) for i in range(count)])  6.08 us
    unnamed x14, local copies, waits for them, and re-layouts  5.26 us
    ppermute x2, waiting for transfers between devices, from_behind(): return lax.ppermute(block, axis, route)  4.44 us
    ppermute x2, starting transfers between devices, from_behind(): return lax.ppermute(block, axis, route)  4.21 us
  transfers between devices with their start and end apart: 7, of which 6 were waited for; matrix products, arithmetic and copies ran while one was open for 12% of the time, Pallas kernels for 0%

profile of v13, /device:TPU:1, one launch (start us, length us, event | category | flops | bytes accessed | tf_op | source)
XLA Modules:
  0.0 135.3 jit_solution(5814831305573615540)
XLA Ops:
  0.6 1.4 %broadcast_in_dim.36 = bf16[32,8,512]{2,1,0:T(8,128)(2,1)} broadcast(bf16[8,512]{1,0:T(8,128)(2,1)} %param.6), dimensions={1,2} | broadcast | bytes 270336 | tf_op jit(solution)/shard_map/broadcast_in_dim | solution.py:103
  2.0 19.0 %all-to-all-start = ((bf16[32,8,512]{2,1,0:T(8,128)(2,1)}), bf16[32,8,512]{2,1,0:T(8,128)(2,1)S(1)}, u32[]{:S(2)}, u32[]{:S(2)}) async-start(bf16[32,8,512]{2,1,0:T(8,128)(2,1)} %broadcast_in_dim.36), calls=%async_computation | async-start | bytes 524288 | tf_op jit(solution)/shard_map/all_to_all | solution.py:94
  21.0 4.1 %copy.45 = bf16[1,256,4096]{1,2,0:T(8,128)(2,1)} copy(bf16[1,256,4096]{2,1,0:T(8,128)(2,1)} %param.4) | data formatting | bytes 4194304 | tf_op args[0]
  25.1 1.9 %copy.46 = bf16[2,2,2,2,4,4,2,8,256]{8,7,6,5,4,3,2,1,0:T(8,128)(2,1)S(1)} copy(bf16[2,2,2,2,4,4,2,8,256]{8,7,3,6,0,2,5,1,4:T(8,128)(2,1)} %bitcast.93) | data formatting | bytes 4194304 | tf_op jit(solution)/shard_map/transpose | solution.py:116
  27.0 1.1 dynamic-slice_bitcast_fusion
  28.1 7.7 %all-to-all-done = bf16[32,8,512]{2,1,0:T(8,128)(2,1)S(1)} async-done(((bf16[32,8,512]{2,1,0:T(8,128)(2,1)}), bf16[32,8,512]{2,1,0:T(8,128)(2,1)S(1)}, u32[]{:S(2)}, u32[]{:S(2)}) %all-to-all-start) | async-done | bytes 262176 | tf_op jit(solution)/shard_map/all_to_all | solution.py:94
  36.0 21.5 %all_to_all.20 = bf16[8,256,512]{2,1,0:T(8,128)(2,1)S(1)} all-to-all(bf16[8,256,512]{2,1,0:T(8,128)(2,1)S(1)} %broadcast_in_dim.37), channel_id=1, replica_groups={{0,1,8,9,64,65,72,73},{2,3,10,11,66,67,74,75},{16,17,24,25,80,81,88,89}..., dimensions={0} | all-to-all | bytes 4194304 | tf_op jit(solution)/shard_map/all_to_all | solution.py:94
  57.6 2.1 %collective-permute-start = (bf16[2048,512]{1,0:T(8,128)(2,1)S(1)}, bf16[2048,512]{1,0:T(8,128)(2,1)}, u32[]{:S(2)}, u32[]{:S(2)}) collective-permute-start(bf16[2048,512]{1,0:T(8,128)(2,1)S(1)} %bitcast.90), channel_id=1, source_target_pairs={{0,4},{4,0},{8,12},{12,8},{16,20},{20,16},{24,28},{28,24},{32,36},... | collective-permute-start | bytes 6291464 | tf_op jit(solution)/shard_map/ppermute | solution.py:99
  60.0 1.9 %fusion.32 = f32[256,512]{1,0:T(8,128)S(1)} fusion(bf16[2048,256]{1,0:T(8,128)(2,1)} %get-tuple-element.8, bf16[2048,512]{1,0:T(8,128)(2,1)S(1)} %bitcast.91), kind=kOutput, calls=%fused_computation.63 | convolution fusion | flops 536870912 | bytes 3670016 | tf_op jit(solution)/shard_map/dot_general | solution.py:140
  62.0 1.7 %collective-permute-done = bf16[2048,512]{1,0:T(8,128)(2,1)} collective-permute-done((bf16[2048,512]{1,0:T(8,128)(2,1)S(1)}, bf16[2048,512]{1,0:T(8,128)(2,1)}, u32[]{:S(2)}, u32[]{:S(2)}) %collective-permute-start) | collective-permute-done | bytes 2097184 | tf_op jit(solution)/shard_map/ppermute | solution.py:99
  63.7 1.7 %fusion.9 = bf16[256,256]{1,0:T(8,128)(2,1)S(1)} fusion(bf16[2048,256]{1,0:T(8,128)(2,1)S(1)} %get-tuple-element.10, bf16[2048,512]{1,0:T(8,128)(2,1)} %collective-permute-done, f32[256,512]{1,0:T(8,128)S(1)} %fusion.32), kind=kOutput, calls=%fused_computation.24 | convolution fusion | flops 268566528 | bytes 2490368 | tf_op jit(solution)/shard_map/dot_general | solution.py:140
  65.6 1.7 %fusion.8 = bf16[256,256]{1,0:T(8,128)(2,1)S(1)} fusion(bf16[2048,256]{1,0:T(8,128)(2,1)S(1)} %get-tuple-element.10, bf16[2048,512]{1,0:T(8,128)(2,1)} %collective-permute-done, f32[256,512]{1,0:T(8,128)} %copy-done.3), kind=kOutput, calls=%fused_computation.23 | convolution fusion | flops 268566528 | bytes 2490368 | tf_op jit(solution)/shard_map/dot_general | solution.py:140
  67.3 2.3 %collective-permute-start.1 = (bf16[256,256]{1,0:T(8,128)(2,1)S(1)}, bf16[256,256]{1,0:T(8,128)(2,1)S(1)}, u32[]{:S(2)}, u32[]{:S(2)}) collective-permute-start(bf16[256,256]{1,0:T(8,128)(2,1)S(1)} %fusion.8), channel_id=1, source_target_pairs={{0,4},{4,8},{8,12},{12,16},{16,20},{20,24},{24,28},{28,32},{32,36}... | collective-permute-start | bytes 393224 | tf_op jit(solution)/shard_map/ppermute | solution.py:12
  69.6 1.9 %collective-permute-done.1 = bf16[256,256]{1,0:T(8,128)(2,1)S(1)} collective-permute-done((bf16[256,256]{1,0:T(8,128)(2,1)S(1)}, bf16[256,256]{1,0:T(8,128)(2,1)S(1)}, u32[]{:S(2)}, u32[]{:S(2)}) %collective-permute-start.1) | collective-permute-done | bytes 131104 | tf_op jit(solution)/shard_map/ppermute | solution.py:12
  73.6 1.9 %collective-permute-start.2 = (bf16[256,256]{0,1:T(8,128)(2,1)S(1)}, bf16[256,256]{0,1:T(8,128)(2,1)S(1)}, u32[]{:S(2)}, u32[]{:S(2)}) collective-permute-start(bf16[256,256]{0,1:T(8,128)(2,1)S(1)} %pad_maximum_fusion.1), channel_id=1, source_target_pairs={{4,0},{8,4},{12,8},{16,12},{20,16},{24,20},{28,24},{32,28},{36,32}... | collective-permute-start | bytes 393224 | tf_op jit(solution)/shard_map/ppermute | solution.py:12
  75.6 0.5 convolution_convert_fusion.3
  76.0 2.1 %collective-permute-start.3 = (bf16[2048,256]{1,0:T(8,128)(2,1)S(1)}, bf16[2048,256]{1,0:T(8,128)(2,1)S(1)}, u32[]{:S(2)}, u32[]{:S(2)}) collective-permute-start(bf16[2048,256]{1,0:T(8,128)(2,1)S(1)} %convolution_convert_fusion.3), channel_id=1, source_target_pairs={{0,4},{4,0},{8,12},{12,8},{16,20},{20,16},{24,28},{28,24},{32,36},... | collective-permute-start | bytes 3145736 | tf_op jit(solution)/shard_map/ppermute | solution.py:99
  78.1 2.5 %collective-permute-done.2 = bf16[256,256]{0,1:T(8,128)(2,1)S(1)} collective-permute-done((bf16[256,256]{0,1:T(8,128)(2,1)S(1)}, bf16[256,256]{0,1:T(8,128)(2,1)S(1)}, u32[]{:S(2)}, u32[]{:S(2)}) %collective-permute-start.2) | collective-permute-done | bytes 131104 | tf_op jit(solution)/shard_map/ppermute | solution.py:12
  80.7 0.5 convolution_convert_fusion.2
  81.2 1.9 %collective-permute-start.4 = (bf16[2048,256]{1,0:T(8,128)(2,1)S(1)}, bf16[2048,256]{1,0:T(8,128)(2,1)S(1)}, u32[]{:S(2)}, u32[]{:S(2)}) collective-permute-start(bf16[2048,256]{1,0:T(8,128)(2,1)S(1)} %convolution_convert_fusion.2), channel_id=1, source_target_pairs={{0,4},{4,0},{8,12},{12,8},{16,20},{20,16},{24,28},{28,24},{32,36},... | collective-permute-start | bytes 3145736 | tf_op jit(solution)/shard_map/ppermute | solution.py:99
  83.1 0.7 convolution_convert_fusion.1
  83.9 1.9 %collective-permute-done.4 = bf16[2048,256]{1,0:T(8,128)(2,1)S(1)} collective-permute-done((bf16[2048,256]{1,0:T(8,128)(2,1)S(1)}, bf16[2048,256]{1,0:T(8,128)(2,1)S(1)}, u32[]{:S(2)}, u32[]{:S(2)}) %collective-permute-start.4) | collective-permute-done | bytes 1048608 | tf_op jit(solution)/shard_map/ppermute | solution.py:99
  85.7 0.5 add_convert_fusion
  86.3 25.4 %all_to_all.21 = bf16[8,256,512]{2,1,0:T(8,128)(2,1)S(1)} all-to-all(bf16[8,256,512]{2,1,0:T(8,128)(2,1)S(1)} %bitcast.88), channel_id=1, replica_groups={{0,1,8,9,64,65,72,73},{2,3,10,11,66,67,74,75},{16,17,24,25,80,81,88,89}..., dimensions={0} | all-to-all | bytes 4194304 | tf_op jit(solution)/shard_map/all_to_all | solution.py:94
  111.7 1.0 reduce_sum.41
  112.7 7.2 %all-to-all-start.3 = ((bf16[32,8,512]{2,1,0:T(8,128)(2,1)}), bf16[32,8,512]{2,1,0:T(8,128)(2,1)S(1)}, u32[]{:S(2)}, u32[]{:S(2)}) async-start(bf16[32,8,512]{2,1,0:T(8,128)(2,1)} %bitcast.33), calls=%async_computation.3 | async-start | bytes 524288 | tf_op jit(solution)/shard_map/all_to_all | solution.py:94
  119.9 0.5 broadcast_in_dim.40
  120.4 1.1 copy-done.1
  121.8 1.9 %copy_dynamic-update-slice_fusion = bf16[4,2,4,2,2,2,2,8,512]{8,7,6,5,4,3,2,1,0:T(8,128)(2,1)S(1)} fusion(bf16[4,2,4,2,2,2,2,8,512]{8,7,6,5,4,3,2,1,0:T(8,128)(2,1)S(1)} %copy_dynamic-update-slice_fusion.1, s32[]{:T(128)S(6)} %select_n.14, bf16[4,2,4,2,1,2,2,8,512]{8,7,5,2,0,6,3,1,4:T(8,128)(2,1)} %bitcast.30), kind=kLoop, calls=%fused_computation.6 | loop fusion | bytes 4194308 | tf_op jit(solution)/shard_map/dynamic_update_slice | solution.py:124
  123.6 2.6 %fusion = bf16[1,256,4096]{2,1,0:T(8,128)(2,1)} fusion(bf16[4096,512]{1,0:T(8,128)(2,1)S(1)} %bitcast.87, bf16[256,128]{0,1:T(8,128)(2,1)S(1)} %get-tuple-element.17, bf16[256,128]{0,1:T(8,128)(2,1)S(1)} %get-tuple-element.16, bf16[256,256]{0,1:T(8,128)(2,1)S(1)} %bitcast.99), kind=kOutput, calls=%fused_computation.1 | convolution fusion | flops 1075576832 | bytes 6553600 | tf_op jit(solution)/shard_map/dot_general | solution.py:196
  126.3 8.4 %all-to-all-done.3 = bf16[32,8,512]{2,1,0:T(8,128)(2,1)S(1)} async-done(((bf16[32,8,512]{2,1,0:T(8,128)(2,1)}), bf16[32,8,512]{2,1,0:T(8,128)(2,1)S(1)}, u32[]{:S(2)}, u32[]{:S(2)}) %all-to-all-start.3) | async-done | bytes 262176 | tf_op jit(solution)/shard_map/all_to_all | solution.py:94
  134.6 0.7 convert_reduce_fusion
  (34 shorter events, 3.0 us)
Async XLA Ops:
  2.0 33.8 %all-to-all-start = ((bf16[32,8,512]{2,1,0:T(8,128)(2,1)}), bf16[32,8,512]{2,1,0:T(8,128)(2,1)S(1)}, u32[]{:S(2)}, u32[]{:S(2)}) async-start(bf16[32,8,512]{2,1,0:T(8,128)(2,1)} %broadcast_in_dim.36), calls=%async_computation | async-start | bytes 524288 | tf_op jit(solution)/shard_map/all_to_all | solution.py:94
  36.0 23.7 %copy-start.4 = (bf16[1,256,256]{2,1,0:T(8,128)(2,1)S(1)}, bf16[1,256,256]{2,1,0:T(8,128)(2,1)}, u32[]{:S(2)}) copy-start(bf16[1,256,256]{2,1,0:T(8,128)(2,1)} %param.7) | copy-start | bytes 393220
  36.0 23.8 %copy-start.5 = (s32[1,256]{1,0:T(1,128)S(1)}, s32[1,256]{1,0:T(1,128)}, u32[]{:S(2)}) copy-start(s32[1,256]{1,0:T(1,128)} %param.5) | copy-start | bytes 3076
  57.6 4.4 %copy-start = (bf16[8,256,512]{2,1,0:T(8,128)(2,1)}, bf16[8,256,512]{2,1,0:T(8,128)(2,1)S(1)}, u32[]{:S(2)}) copy-start(bf16[8,256,512]{2,1,0:T(8,128)(2,1)S(1)} %all_to_all.20) | copy-start | bytes 6291460
  57.6 6.2 %collective-permute-start = (bf16[2048,512]{1,0:T(8,128)(2,1)S(1)}, bf16[2048,512]{1,0:T(8,128)(2,1)}, u32[]{:S(2)}, u32[]{:S(2)}) collective-permute-start(bf16[2048,512]{1,0:T(8,128)(2,1)S(1)} %bitcast.90), channel_id=1, source_target_pairs={{0,4},{4,0},{8,12},{12,8},{16,20},{20,16},{24,28},{28,24},{32,36},... | collective-permute-start | bytes 6291464 | tf_op jit(solution)/shard_map/ppermute | solution.py:99
  62.0 1.7 %copy-start.3 = (f32[256,512]{1,0:T(8,128)}, f32[256,512]{1,0:T(8,128)S(1)}, u32[]{:S(2)}) copy-start(f32[256,512]{1,0:T(8,128)S(1)} %fusion.32) | copy-start | bytes 1572868
  67.3 4.2 %collective-permute-start.1 = (bf16[256,256]{1,0:T(8,128)(2,1)S(1)}, bf16[256,256]{1,0:T(8,128)(2,1)S(1)}, u32[]{:S(2)}, u32[]{:S(2)}) collective-permute-start(bf16[256,256]{1,0:T(8,128)(2,1)S(1)} %fusion.8), channel_id=1, source_target_pairs={{0,4},{4,8},{8,12},{12,16},{16,20},{20,24},{24,28},{28,32},{32,36}... | collective-permute-start | bytes 393224 | tf_op jit(solution)/shard_map/ppermute | solution.py:12
  73.6 7.0 %collective-permute-start.2 = (bf16[256,256]{0,1:T(8,128)(2,1)S(1)}, bf16[256,256]{0,1:T(8,128)(2,1)S(1)}, u32[]{:S(2)}, u32[]{:S(2)}) collective-permute-start(bf16[256,256]{0,1:T(8,128)(2,1)S(1)} %pad_maximum_fusion.1), channel_id=1, source_target_pairs={{4,0},{8,4},{12,8},{16,12},{20,16},{24,20},{28,24},{32,28},{36,32}... | collective-permute-start | bytes 393224 | tf_op jit(solution)/shard_map/ppermute | solution.py:12
  76.0 7.1 %copy-start.2 = (bf16[2048,256]{1,0:T(8,128)(2,1)S(1)}, bf16[2048,256]{1,0:T(8,128)(2,1)}, u32[]{:S(2)}) copy-start(bf16[2048,256]{1,0:T(8,128)(2,1)} %get-tuple-element.8) | copy-start | bytes 3145732
  76.0 7.8 %collective-permute-start.3 = (bf16[2048,256]{1,0:T(8,128)(2,1)S(1)}, bf16[2048,256]{1,0:T(8,128)(2,1)S(1)}, u32[]{:S(2)}, u32[]{:S(2)}) collective-permute-start(bf16[2048,256]{1,0:T(8,128)(2,1)S(1)} %convolution_convert_fusion.3), channel_id=1, source_target_pairs={{0,4},{4,0},{8,12},{12,8},{16,20},{20,16},{24,28},{28,24},{32,36},... | collective-permute-start | bytes 3145736 | tf_op jit(solution)/shard_map/ppermute | solution.py:99
  81.2 4.6 %collective-permute-start.4 = (bf16[2048,256]{1,0:T(8,128)(2,1)S(1)}, bf16[2048,256]{1,0:T(8,128)(2,1)S(1)}, u32[]{:S(2)}, u32[]{:S(2)}) collective-permute-start(bf16[2048,256]{1,0:T(8,128)(2,1)S(1)} %convolution_convert_fusion.2), channel_id=1, source_target_pairs={{0,4},{4,0},{8,12},{12,8},{16,20},{20,16},{24,28},{28,24},{32,36},... | collective-permute-start | bytes 3145736 | tf_op jit(solution)/shard_map/ppermute | solution.py:99
  112.7 21.9 %all-to-all-start.3 = ((bf16[32,8,512]{2,1,0:T(8,128)(2,1)}), bf16[32,8,512]{2,1,0:T(8,128)(2,1)S(1)}, u32[]{:S(2)}, u32[]{:S(2)}) async-start(bf16[32,8,512]{2,1,0:T(8,128)(2,1)} %bitcast.33), calls=%async_computation.3 | async-start | bytes 524288 | tf_op jit(solution)/shard_map/all_to_all | solution.py:94
  119.9 1.6 %copy-start.1 = (bf16[8,256,512]{2,1,0:T(8,128)(2,1)S(1)}, bf16[8,256,512]{2,1,0:T(8,128)(2,1)}, u32[]{:S(2)}) copy-start(bf16[8,256,512]{2,1,0:T(8,128)(2,1)} %copy-done) | copy-start | bytes 6291460
